TPU v7x, 256 devices: a whole 4x4x8 slice. The times are simulated.
256 devices in a mesh: row: 64 (over y, z, core), col: 4 (over x).
Axes of the slice: x: 4, y: 4, z: 8, core: 2. Of those that a mesh axis runs over, the one named last changes fastest.
Arguments:
- green: bfloat16 [8192, 5, 8192], P('col', None, 'row'), as said below
- arrival: int32 [1200, 5, 64], P(None, None, 'row'), may hold values from 512 to 3071
- row_gauge: int32 [8192], P('col'), may hold values from 0 to 1199
- row_time: int32 [8192], P('col'), may hold values from 0 to 4095, as said below
- damping: float32 [512], replicated, may hold values from 0.5 to 2
- trail: float32 [5, 8192, 8, 512], P(None, 'row', None, 'col'), may hold values from -0.4 to 0.4
Outputs:
- chol_panel: float32 [5, 8192, 512], P(None, 'row', 'col')
- trail_out: float32 [5, 8192, 8, 512], P(None, 'row', None, 'col')
Inputs may be any that keep to these rules, and one draw needn't show every extreme that they name: `row_time`: nondecreasing along the rows; the first row has time 0 and the last row time 4096 - 1. `green`: real-valued entries of order 2048 ** -0.5.
All inputs are finite; a program needn't handle non-finite values.
Results may differ from a plain program's by a relative error of at most 0.0003.
Values may be sent and summed in bfloat16 or wider, within the bound.
A program may use at most 64 MiB of HBM per device.

v0:
```python
import jax
import jax.numpy as jnp
from jax import lax
from jax.sharding import PartitionSpec as P

NB = 128
PANEL = 512


def spread(shard, axis, root):
    mine = lax.axis_index(axis) == root
    return lax.psum(jnp.where(mine, shard, jnp.zeros_like(shard)), axis)


def local(green, arrival, row_gauge, row_time, damping, trail):
    row_count = lax.axis_size("row")
    col_count = lax.axis_size("col")
    row_pos = lax.axis_index("row")
    col_pos = lax.axis_index("col")
    kq_rows, tile_rows, tile_width = green.shape
    panel_tiles = PANEL // NB
    arrive = arrival[row_gauge][:, :, 0]
    is_live = row_time[:, None] >= arrive
    masked = jnp.where(is_live[:, :, None], green, jnp.zeros_like(green))
    flat_green = masked.reshape(kq_rows, tile_rows * tile_width)
    pieces = []
    for tile_no in range(panel_tiles):
        pieces.append(spread(masked[:, tile_no // row_count, :], "row", tile_no % row_count))
    panel_cols = jnp.concatenate(pieces, axis=1)
    contract_rows = (((0,), (0,)), ((), ()))
    partial_value = lax.dot_general(
        flat_green, panel_cols, contract_rows, preferred_element_type=jnp.float32
    )
    normal_rows = lax.psum(partial_value, "col")
    block_list = []
    for tile_no in range(panel_tiles):
        local_no = tile_no // row_count
        block_list.append(
            spread(
                normal_rows[local_no * tile_width : (local_no + 1) * tile_width],
                "row",
                tile_no % row_count,
            )
        )
    diag_block = jnp.concatenate(block_list, axis=0)
    factor = jnp.linalg.cholesky(diag_block + jnp.diag(damping))
    solved = lax.linalg.triangular_solve(
        factor, normal_rows, left_side=False, lower=True, transpose_a=True
    )
    solved = solved.reshape(tile_rows, tile_width, PANEL)
    tiles_list = []
    for local_no in range(tile_rows):
        tile_id = local_no * row_count + row_pos
        diag_rows = lax.dynamic_slice_in_dim(
            factor, jnp.minimum(tile_id, panel_tiles - 1) * tile_width, tile_width, 0
        )
        tiles_list.append(jnp.where(tile_id < panel_tiles, diag_rows, solved[local_no]))
    lower_rows = jnp.stack(tiles_list)
    col_share = PANEL // col_count
    chol_out = lax.dynamic_slice_in_dim(lower_rows, col_pos * col_share, col_share, 2)
    far_list = []
    for slot_no in range(trail.shape[2]):
        tile_id = panel_tiles + slot_no * col_count + col_pos
        picked = lax.dynamic_index_in_dim(lower_rows, tile_id // row_count, 0, keepdims=False)
        far_list.append(spread(picked, "row", tile_id % row_count))
    far_rows = jnp.stack(far_list).reshape(trail.shape[2] * tile_width, PANEL)
    update = lax.dot_general(
        lower_rows.reshape(tile_rows * tile_width, PANEL),
        far_rows,
        (((1,), (1,)), ((), ())),
        precision=lax.Precision.HIGHEST,
        preferred_element_type=jnp.float32,
    )
    update = update.reshape(tile_rows, tile_width, trail.shape[2], tile_width)
    tile_ids = jnp.arange(tile_rows, dtype=jnp.int32) * row_count + row_pos
    below_panel = (tile_ids >= panel_tiles)[:, None, None, None]
    return (chol_out, trail - jnp.where(below_panel, update, jnp.zeros_like(update)))


def solution(mesh):
    return jax.shard_map(
        local,
        mesh=mesh,
        in_specs=(
            P("col", None, "row"),
            P(None, None, "row"),
            P("col"),
            P("col"),
            P(),
            P(None, "row", None, "col"),
        ),
        out_specs=(P(None, "row", "col"), P(None, "row", None, "col")),
        check_vma=False,
    )
```

profile of v0, /device:TPU:1, one launch (start us, length us, event | category | flops | bytes accessed | tf_op | source)
XLA Modules:
  0.0 817.9 jit_solution(13425590704047043025)
XLA Ops:
  7.2 3.0 copy.45
  10.3 0.2 copy.43
  10.6 7.6 gather_fusion
  18.2 1.5 copy.44
  19.8 0.2 broadcast_select_fusion
  20.0 1.5 copy-done
  21.5 1.4 select_bitcast_fusion.3
  22.9 192.3 %all-reduce.15.cloned.1.call-done = (bf16[2048,128]{0,1:T(8,128)(2,1)}, bf16[2048,128]{0,1:T(8,128)(2,1)}, bf16[2048,128]{0,1:T(8,128)(2,1)}, bf16[2048,128]{0,1:T(8,128)(2,1)}) async-done(((bf16[2048,128]{0,1:T(8,128)(2,1)}, bf16[2048,128]{0,1:T(8,128)(2,1)}, bf16[2048,128]{0,1:T(8,128)(2,1)}, bf16[2048,128]{0,1:T(8,128)(2,1)}), (bf16[2048,128]{0,1:T(8,128)(2,1)}, bf16[2048,128]{0,1:T(8,128)(2,1)}, ...) | async-done | bytes 2097168 | tf_op jit(solution)/shard_map/psum | solution.py:12
  215.3 5.2 fusion
  220.6 52.0 %all-reduce.9.cloned.1.call-done = f32[640,512]{0,1:T(8,128)} async-done(((f32[640,512]{0,1:T(8,128)}), f32[640,512]{0,1:T(8,128)}) %all-reduce.9.cloned.1.call-update) | async-done | bytes 1310736 | tf_op jit(solution)/shard_map/psum | solution.py:34
  272.5 2.0 slice_select_fusion.8
  274.5 0.5 all-reduce.11.cloned.1.call-start
  275.2 188.2 %all-reduce.13.cloned.1.call-done = (f32[128,512]{0,1:T(8,128)}, f32[128,512]{0,1:T(8,128)}, f32[128,512]{0,1:T(8,128)}, f32[128,512]{0,1:T(8,128)}) async-done(((f32[128,512]{0,1:T(8,128)}, f32[128,512]{0,1:T(8,128)}, f32[128,512]{0,1:T(8,128)}, f32[128,512]{0,1:T(8,128)}), (f32[128,512]{0,1:T(8,128)}, f32[128,512]{0,1:T(8,128)}, f32[128,512]{0,1:T(8,128)}, ...) | async-done | bytes 1048592 | tf_op jit(solution)/shard_map/psum | solution.py:12
  463.4 1.3 maximum_add_fusion
  464.7 0.3 copy.47
  465.0 0.2 fusion.13
  465.3 11.7 %cholesky.103 = f32[128,128]{1,0:T(8,128)S(1)} custom-call(f32[128,128]{1,0:T(8,128)S(1)} %cholesky.263), custom_call_target="Cholesky" | custom-call | tf_op jit(solution)/shard_map/jit(cholesky)/cholesky | solution.py:46
  477.0 9.8 %custom-call.30 = f32[1,128,128]{1,2,0:T(8,128)S(1)} custom-call(f32[1,128,128]{2,1,0:T(8,128)S(1)} %get-tuple-element.77), custom_call_target="InvertDiagBlocksLowerTriangular" | custom-call | tf_op jit(solution)/shard_map/jit(cholesky)/cholesky | solution.py:46
  486.9 0.3 fusion.38
  487.2 0.3 convolution_subtract_fusion.3
  487.5 11.7 %cholesky.215 = f32[128,128]{1,0:T(8,128)S(1)} custom-call(f32[128,128]{1,0:T(8,128)S(1)} %cholesky.267), custom_call_target="Cholesky" | custom-call | tf_op jit(solution)/shard_map/jit(cholesky)/cholesky | solution.py:46
  499.4 0.1 copy.49
  499.6 10.0 %custom-call.31 = f32[1,128,128]{1,2,0:T(8,128)S(1)} custom-call(f32[1,128,128]{2,1,0:T(8,128)S(1)} %get-tuple-element.75), custom_call_target="InvertDiagBlocksLowerTriangular" | custom-call | tf_op jit(solution)/shard_map/jit(cholesky)/cholesky | solution.py:46
  509.7 0.3 convolution_dynamic-update-slice_fusion
  510.1 0.6 convolution_subtract_fusion.4
  510.7 11.7 %cholesky.236 = f32[128,128]{1,0:T(8,128)S(1)} custom-call(f32[128,128]{1,0:T(8,128)S(1)} %cholesky.272), custom_call_target="Cholesky" | custom-call | tf_op jit(solution)/shard_map/jit(cholesky)/cholesky | solution.py:46
  522.5 9.8 %custom-call.32 = f32[1,128,128]{1,2,0:T(8,128)S(1)} custom-call(f32[1,128,128]{2,1,0:T(8,128)S(1)} %get-tuple-element.73), custom_call_target="InvertDiagBlocksLowerTriangular" | custom-call | tf_op jit(solution)/shard_map/jit(cholesky)/cholesky | solution.py:46
  532.3 0.3 convolution_dynamic-update-slice_fusion.1
  532.6 0.5 convolution_subtract_fusion.5
  533.1 11.9 %cholesky.253 = f32[128,128]{1,0:T(8,128)S(1)} custom-call(f32[128,128]{1,0:T(8,128)S(1)} %convolution_subtract_fusion.5), custom_call_target="Cholesky" | custom-call | tf_op jit(solution)/shard_map/jit(cholesky)/cholesky | solution.py:46
  545.2 0.7 compare_reduce_fusion.1
  545.9 0.6 compare_reduce_fusion
  546.5 0.6 compare_reduce_fusion.2
  549.6 0.3 fusion.14
  549.9 10.9 %while.1 = (s32[]{:T(128)}, f32[512,512]{0,1:T(8,128)S(1)}, s32[4,2]{0,1:T(2,128)S(1)}, f32[4,128,128]{2,1,0:T(8,128)}, s32[]{:T(128)}) while((s32[]{:T(128)}, f32[512,512]{0,1:T(8,128)S(1)}, s32[4,2]{0,1:T(2,128)S(1)}, f32[4,128,128]{2,1,0:T(8,128)}, s32[]{:T(128)}) %tuple.47), condition=%wide.while_cond, body=%wide.while_body.sunk | while | flops 2 | bytes 393829 | solution.py:47
  550.0 0.5 fusion.64
  550.5 1.4 dynamic-slice.7
  552.0 0.6 bitcast_dynamic-update-slice_fusion.2
  552.7 0.5 fusion.64
  553.2 1.4 dynamic-slice.7
  554.7 0.6 bitcast_dynamic-update-slice_fusion.2
  555.4 0.5 fusion.64
  555.9 1.4 dynamic-slice.7
  557.4 0.6 bitcast_dynamic-update-slice_fusion.2
  558.1 0.5 fusion.64
  558.6 1.4 dynamic-slice.7
  560.1 0.6 bitcast_dynamic-update-slice_fusion.2
  560.8 40.1 %custom-call.33 = f32[4,128,128]{1,2,0:T(8,128)S(1)} custom-call(f32[4,128,128]{2,1,0:T(8,128)} %get-tuple-element.9), custom_call_target="InvertDiagBlocksLowerTriangular" | custom-call | tf_op jit(solution)/shard_map/triangular_solve | solution.py:47
  600.9 1.4 fusion.23
  602.3 1.4 convolution_subtract_fusion.1
  603.8 0.5 fusion.45
  604.3 1.6 convolution_subtract_fusion
  605.8 0.5 fusion.44
  606.3 1.9 convolution_subtract_fusion.2
  608.2 0.5 fusion.43
  609.1 1.3 dynamic-slice_select_fusion
  610.5 0.9 copy.62
  611.4 187.6 %all-reduce.11.cloned.1.call-done = (f32[1,128,512]{1,2,0:T(8,128)}, f32[1,128,512]{1,2,0:T(8,128)}, f32[1,128,512]{1,2,0:T(8,128)}, f32[1,128,512]{1,2,0:T(8,12...) async-done(((f32[1,128,512]{1,2,0:T(8,128)}, f32[1,128,512]{1,2,0:T(8,128)}, f32[1,128,512]{1,2,0:T(8,128)}, ...) | async-done | bytes 2097168 | tf_op jit(solution)/shard_map/psum | solution.py:12
  799.0 1.1 constant_dynamic-update-slice_fusion.7
  800.1 1.0 constant_dynamic-update-slice_fusion.6
  801.1 1.0 constant_dynamic-update-slice_fusion.5
  802.1 1.0 constant_dynamic-update-slice_fusion.4
  803.2 5.0 copy_subtract_fusion
  808.2 3.0 copy.63
  (67 shorter events, 2.1 us)
Async XLA Ops:
  7.2 208.1 %all-reduce.15.cloned.1.call-start = ((), (), s32[]{:S(2)}) async-start(), calls=%async_computation.3 | async-start | bytes 4194304 | tf_op jit(solution)/shard_map/psum | solution.py:12
  7.2 3.0 copy-start.6
  7.2 3.3 copy-start.7
  10.5 9.2 %copy-start.8 = (s32[2048]{0:T(1024)S(1)}, s32[2048]{0:T(1024)}, u32[]{:S(2)}) copy-start(s32[2048]{0:T(1024)} %param.9) | copy-start | bytes 24580
  20.0 1.5 copy-start
  22.9 249.6 %all-reduce.9.cloned.1.call-start = ((), (), s32[]{:S(2)}) async-start(), calls=%async_computation | async-start | bytes 2621440 | tf_op jit(solution)/shard_map/psum | solution.py:34
  220.5 242.9 %copy-start.9 = (f32[512]{0:T(512)S(1)}, f32[512]{0:T(512)}, u32[]{:S(2)}) copy-start(f32[512]{0:T(512)} %param.10) | copy-start | bytes 6148
  220.5 242.9 %all-reduce.13.cloned.1.call-start = ((), (), s32[]{:S(2)}) async-start(), calls=%async_computation.2 | async-start | bytes 2097152 | tf_op jit(solution)/shard_map/psum | solution.py:12
  274.5 524.5 %all-reduce.11.cloned.1.call-start = ((), (), s32[]{:S(2)}) async-start(), calls=%async_computation.1 | async-start | bytes 4194304 | tf_op jit(solution)/shard_map/psum | solution.py:12
  799.0 4.1 copy-start.5
  799.0 4.1 copy-start.4
  799.0 4.2 copy-start.3
  799.0 4.2 copy-start.2
  799.0 4.2 copy-start.1
Sparse Core Ops, SparseCore 0:
  23.0 192.2 all-reduce.14
  220.6 51.8 all-reduce.8
  276.9 186.4 all-reduce.12
  610.5 188.3 all-reduce.10
where the time goes:
time: 822 us; the launch traced here: 818 us
  waiting for transfers between devices  620 us (75%)
  other arithmetic  126 us (15%)
  local copies, waits for them, and re-layouts  33.8 us (4%)
  matrix products  20.3 us (2%)
  between operations  17.2 us (2%)
    psum x3, waiting for transfers between devices, spread(): return lax.psum(jnp.where(mine, shard, jnp.zeros_like(shard)), axis)  568 us
    another operation x14, other arithmetic, local(): factor = jnp.linalg.cholesky(diag_block + jnp.diag(damping))  78.7 us
    psum x1, waiting for transfers between devices, local(): normal_rows = lax.psum(partial_value, 'col')  52 us
    another operation x4, other arithmetic, local(): lax.linalg.triangular_solve(factor, normal_rows, left_side=False, lower=T...  40.5 us
  transfers between devices with their start and end apart: 4, of which 4 were waited for; matrix products, arithmetic and copies ran while one was open for 0% of the time, Pallas kernels for 0%

commit v1 on v0

v1 whole, which is shorter than its diff:
```python
import numpy as np
import jax
import jax.numpy as jnp
from jax import lax
from jax.sharding import PartitionSpec as P

NB = 128
PANEL = 512


def tree_share(piece, holds, spread_masks, gather_masks, row_count, col_count):
    row_pos = lax.axis_index("row")
    col_pos = lax.axis_index("col")
    flat_pos = row_pos * col_count + col_pos
    have = np.array(holds, dtype=bool)
    for mask in spread_masks:
        pairs = []
        gets = np.zeros_like(have)
        for r in range(row_count):
            for c in range(col_count):
                if have[r, c] and not have[r ^ mask, c]:
                    pairs.append((r * col_count + c, (r ^ mask) * col_count + c))
                    gets[r ^ mask, c] = True
        moved = lax.ppermute(piece, ("row", "col"), pairs)
        took = jnp.asarray(gets.reshape(-1))[flat_pos]
        piece = jnp.where(took, moved, piece)
        have = have | gets
    assert have.all()
    for mask in gather_masks:
        pairs = [
            (r * col_count + c, (r ^ mask) * col_count + c)
            for r in range(row_count)
            for c in range(col_count)
        ]
        other = lax.ppermute(piece, ("row", "col"), pairs)
        upper = (row_pos & mask) != 0
        low = jnp.where(upper, other, piece)
        high = jnp.where(upper, piece, other)
        piece = jnp.stack([low, high])
    return piece


def local(green, arrival, row_gauge, row_time, damping, trail):
    row_count = lax.axis_size("row")
    col_count = lax.axis_size("col")
    row_pos = lax.axis_index("row")
    col_pos = lax.axis_index("col")
    kq_rows, tile_rows, tile_width = green.shape
    panel_tiles = PANEL // NB
    far_slots = trail.shape[2]
    arrive = arrival[row_gauge][:, :, 0]
    is_live = row_time[:, None] >= arrive
    masked = jnp.where(is_live[:, :, None], green, jnp.zeros_like(green))
    flat_green = masked.reshape(kq_rows, tile_rows * tile_width)

    panel_holds = np.zeros((row_count, col_count), dtype=bool)
    panel_holds[:panel_tiles, :] = True
    shared = tree_share(
        masked[:, 0, :], panel_holds, (8, 32, 4, 16), (2, 1), row_count, col_count
    )
    panel_stack = jnp.transpose(shared, (1, 0, 2, 3)).reshape(panel_tiles, kq_rows, tile_width)
    panel_cols = jnp.transpose(panel_stack, (1, 0, 2)).reshape(kq_rows, PANEL)

    contract_rows = (((0,), (0,)), ((), ()))
    diag_part = lax.dot_general(
        panel_cols, panel_cols, contract_rows, preferred_element_type=jnp.float32
    )
    partial_value = lax.dot_general(
        flat_green, panel_cols, contract_rows, preferred_element_type=jnp.float32
    )
    diag_block = lax.psum(diag_part, "col")
    normal_rows = lax.psum(partial_value, "col")
    factor = jnp.linalg.cholesky(diag_block + jnp.diag(damping))
    solved = lax.linalg.triangular_solve(
        factor, normal_rows, left_side=False, lower=True, transpose_a=True
    )
    solved = solved.reshape(tile_rows, tile_width, PANEL)
    tiles_list = []
    for local_no in range(tile_rows):
        tile_id = local_no * row_count + row_pos
        diag_rows = lax.dynamic_slice_in_dim(
            factor, jnp.minimum(tile_id, panel_tiles - 1) * tile_width, tile_width, 0
        )
        tiles_list.append(jnp.where(tile_id < panel_tiles, diag_rows, solved[local_no]))
    lower_rows = jnp.stack(tiles_list)
    col_share = PANEL // col_count
    chol_out = lax.dynamic_slice_in_dim(lower_rows, col_pos * col_share, col_share, 2)

    far_holds = np.zeros((row_count, col_count), dtype=bool)
    for slot_no in range(far_slots):
        for c in range(col_count):
            far_holds[panel_tiles + slot_no * col_count + c, c] = True
    far_shared = tree_share(
        lower_rows[0], far_holds, (32, 2, 1), (8, 4, 16), row_count, col_count
    )
    by_value = jnp.transpose(far_shared, (0, 2, 1, 3, 4)).reshape(far_slots, tile_width, PANEL)
    far_rows = jnp.roll(by_value, -1, axis=0).reshape(far_slots * tile_width, PANEL)
    update = lax.dot_general(
        lower_rows.reshape(tile_rows * tile_width, PANEL),
        far_rows,
        (((1,), (1,)), ((), ())),
        precision=lax.Precision.HIGHEST,
        preferred_element_type=jnp.float32,
    )
    update = update.reshape(tile_rows, tile_width, far_slots, tile_width)
    tile_ids = jnp.arange(tile_rows, dtype=jnp.int32) * row_count + row_pos
    below_panel = (tile_ids >= panel_tiles)[:, None, None, None]
    return (chol_out, trail - jnp.where(below_panel, update, jnp.zeros_like(update)))


def solution(mesh):
    return jax.shard_map(
        local,
        mesh=mesh,
        in_specs=(
            P("col", None, "row"),
            P(None, None, "row"),
            P("col"),
            P("col"),
            P(),
            P(None, "row", None, "col"),
        ),
        out_specs=(P(None, "row", "col"), P(None, "row", None, "col")),
        check_vma=False,
    )
```

time: 822 us -> 463 us (0.56)
  waiting for transfers between devices: 620 us -> 185 us
  starting transfers between devices: 0.63 us -> 45.7 us
  other arithmetic: 126 us -> 142 us
    psum x3 -> x0, waiting for transfers between devices: 568 us -> none  [spread(): return lax.psum(jnp.where(mine, shard, jnp.zeros_like(shard)), axis)]
    ppermute x0 -> x12, waiting for transfers between devices: none -> 111 us  [the longest x5 61.7 us: tree_share(): other = lax.ppermute(piece, ('row', 'col'), pairs)]
    ppermute x0 -> x12, starting transfers between devices: none -> 45.6 us  [the longest x5 29.2 us: tree_share(): other = lax.ppermute(piece, ('row', 'col'), pairs)]
    psum x1, waiting for transfers between devices: 52 us -> 73.2 us  [local(): normal_rows = lax.psum(partial_value, 'col')]
  transfers between devices with their start and end apart: 4 -> 13, of which waited for: 4 -> 11; matrix products, arithmetic and copies ran while one was open for 0% -> 2% of each run, Pallas kernels for 0% -> 0%
where the time goes in v1:
time: 463 us; the launch traced here: 455 us
  waiting for transfers between devices  185 us (40%)
  other arithmetic  142 us (31%)
  starting transfers between devices  45.7 us (10%)
  local copies, waits for them, and re-layouts  39.1 us (8%)
  matrix products  26.8 us (6%)
  between operations  17.5 us (4%)
    another operation x14, other arithmetic, local(): factor = jnp.linalg.cholesky(diag_block + jnp.diag(damping))  78.9 us
    psum x1, waiting for transfers between devices, local(): normal_rows = lax.psum(partial_value, 'col')  73.2 us
    ppermute x5, waiting for transfers between devices, tree_share(): other = lax.ppermute(piece, ('row', 'col'), pairs)  61.7 us
    ppermute x7, waiting for transfers between devices, tree_share(): moved = lax.ppermute(piece, ('row', 'col'), pairs)  49.8 us
    another operation x4, other arithmetic, local(): lax.linalg.triangular_solve(factor, normal_rows, left_side=False, lower=T...  41.1 us
    ppermute x5, starting transfers between devices, tree_share(): other = lax.ppermute(piece, ('row', 'col'), pairs)  29.2 us
    ppermute x7, starting transfers between devices, tree_share(): moved = lax.ppermute(piece, ('row', 'col'), pairs)  16.4 us
    another operation x20, local copies, waits for them, and re-layouts  10.4 us
  transfers between devices with their start and end apart: 13, of which 11 were waited for; matrix products, arithmetic and copies ran while one was open for 2% of the time, Pallas kernels for 0%

profile of v1, /device:TPU:1, one launch (start us, length us, event | category | flops | bytes accessed | tf_op | source)
XLA Modules:
  0.0 455.4 jit_solution(2575601470714939250)
XLA Ops:
  7.2 1.0 copy.51
  8.2 0.7 fusion.41
  8.9 5.5 %gather_fusion = s32[2048,5]{1,0:T(8,128)S(1)} fusion(s32[1200,5]{1,0:T(8,128)S(1)} %bitcast.122, s32[2048]{0:T(1024)S(1)} %fusion.41), kind=kCustom, calls=%fused_computation | custom fusion | bytes 90112 | tf_op jit(solution)/shard_map/gather | solution.py:51
  14.7 4.2 broadcast_select_fusion
  19.0 0.8 slice_bitcast_fusion
  19.8 9.8 %collective-permute-start = (bf16[2048,128]{1,0:T(8,128)(2,1)}, bf16[2048,128]{1,0:T(8,128)(2,1)S(1)}, u32[]{:S(2)}, u32[]{:S(2)}) collective-permute-start(bf16[2048,128]{1,0:T(8,128)(2,1)} %slice_bitcast_fusion), channel_id=1, source_target_pairs={{0,32},{1,33},{2,34},{3,35},{4,36},{5,37},{6,38},{7,39},{8,40},{9,... | collective-permute-start | bytes 1572872 | tf_op jit(solution)/shard_map/ppermute | solution.py:24
  30.2 10.2 %collective-permute-done = bf16[2048,128]{1,0:T(8,128)(2,1)S(1)} collective-permute-done((bf16[2048,128]{1,0:T(8,128)(2,1)}, bf16[2048,128]{1,0:T(8,128)(2,1)S(1)}, u32[]{:S(2)}, u32[]{:S(2)}) %collective-permute-start) | collective-permute-done | bytes 524320 | tf_op jit(solution)/shard_map/ppermute | solution.py:24
  40.5 0.7 broadcast_select_fusion.1
  41.2 1.3 collective-permute-start.1
  43.1 9.3 %collective-permute-done.1 = bf16[2048,128]{1,0:T(8,128)(2,1)S(1)} collective-permute-done((bf16[2048,128]{1,0:T(8,128)(2,1)S(1)}, bf16[2048,128]{1,0:T(8,128)(2,1)S(1)}, u32[]{:S(2)}, u32[]{:S(2)}) %collective-permute-start.1) | collective-permute-done | bytes 524320 | tf_op jit(solution)/shard_map/ppermute | solution.py:24
  53.1 1.3 collective-permute-start.2
  55.0 8.7 %collective-permute-done.2 = bf16[2048,128]{1,0:T(8,128)(2,1)S(1)} collective-permute-done((bf16[2048,128]{1,0:T(8,128)(2,1)S(1)}, bf16[2048,128]{1,0:T(8,128)(2,1)S(1)}, u32[]{:S(2)}, u32[]{:S(2)}) %collective-permute-start.2) | collective-permute-done | bytes 524320 | tf_op jit(solution)/shard_map/ppermute | solution.py:24
  64.5 1.3 collective-permute-start.3
  66.4 8.1 %collective-permute-done.3 = bf16[2048,128]{1,0:T(8,128)(2,1)S(1)} collective-permute-done((bf16[2048,128]{1,0:T(8,128)(2,1)S(1)}, bf16[2048,128]{1,0:T(8,128)(2,1)S(1)}, u32[]{:S(2)}, u32[]{:S(2)}) %collective-permute-start.3) | collective-permute-done | bytes 524320 | tf_op jit(solution)/shard_map/ppermute | solution.py:24
  75.2 15.6 %collective-permute-start.4 = (bf16[2048,128]{1,0:T(8,128)(2,1)S(1)}, bf16[2048,128]{1,0:T(8,128)(2,1)}, u32[]{:S(2)}, u32[]{:S(2)}) collective-permute-start(bf16[2048,128]{1,0:T(8,128)(2,1)S(1)} %broadcast_select_fusion.4), channel_id=1, source_target_pairs={{0,8},{1,9},{2,10},{3,11},{4,12},{5,13},{6,14},{7,15},{8,0},{9,1},... | collective-permute-start | bytes 1572872 | tf_op jit(solution)/shard_map/ppermute | solution.py:35
  90.8 10.7 %collective-permute-done.4 = bf16[2048,128]{1,0:T(8,128)(2,1)} collective-permute-done((bf16[2048,128]{1,0:T(8,128)(2,1)S(1)}, bf16[2048,128]{1,0:T(8,128)(2,1)}, u32[]{:S(2)}, u32[]{:S(2)}) %collective-permute-start.4) | collective-permute-done | bytes 524320 | tf_op jit(solution)/shard_map/ppermute | solution.py:35
  101.6 1.3 select_bitcast_fusion.7
  102.9 0.8 copy-done
  103.6 1.1 pad_maximum_fusion.2
  104.7 2.2 collective-permute-start.5
  106.9 2.6 copy.64
  109.6 1.5 select_bitcast_fusion.3
  111.3 2.9 copy.54
  114.2 4.6 %fusion.46 = f32[512,512]{0,1:T(8,128)} fusion(bf16[2048,512]{0,1:T(8,128)(2,1)} %bitcast.127), kind=kOutput, calls=%fused_computation.121 | convolution fusion | flops 1073741824 | bytes 3145728 | tf_op jit(solution)/shard_map/dot_general | solution.py:65
  118.8 2.6 fusion.47
  121.5 73.2 %all-reduce.4.cloned.1.call-done = (f32[640,512]{1,0:T(8,128)}, f32[512,512]{0,1:T(8,128)}) async-done(((f32[640,512]{1,0:T(8,128)}, f32[512,512]{0,1:T(8,128)}), (f32[640,512]{1,0:T(8,128)}, f32[512,512]{0,1:T(8,128)})) %all-reduce.4.cloned.1.call-update) | async-done | bytes 2359312 | tf_op jit(solution)/shard_map/psum | solution.py:72
  194.7 1.4 select_add_fusion
  196.7 11.7 %cholesky.103 = f32[128,128]{1,0:T(8,128)S(1)} custom-call(f32[128,128]{1,0:T(8,128)S(1)} %cholesky.263), custom_call_target="Cholesky" | custom-call | tf_op jit(solution)/shard_map/jit(cholesky)/cholesky | solution.py:73
  208.6 9.8 %custom-call.30 = f32[1,128,128]{1,2,0:T(8,128)S(1)} custom-call(f32[1,128,128]{2,1,0:T(8,128)S(1)} %get-tuple-element.59), custom_call_target="InvertDiagBlocksLowerTriangular" | custom-call | tf_op jit(solution)/shard_map/jit(cholesky)/cholesky | solution.py:73
  219.2 12.1 %cholesky.215 = f32[128,128]{1,0:T(8,128)S(1)} custom-call(f32[128,128]{1,0:T(8,128)S(1)} %cholesky.267), custom_call_target="Cholesky" | custom-call | tf_op jit(solution)/shard_map/jit(cholesky)/cholesky | solution.py:73
  231.4 9.8 %custom-call.31 = f32[1,128,128]{1,2,0:T(8,128)S(1)} custom-call(f32[1,128,128]{2,1,0:T(8,128)S(1)} %get-tuple-element.57), custom_call_target="InvertDiagBlocksLowerTriangular" | custom-call | tf_op jit(solution)/shard_map/jit(cholesky)/cholesky | solution.py:73
  242.3 11.7 %cholesky.236 = f32[128,128]{1,0:T(8,128)S(1)} custom-call(f32[128,128]{1,0:T(8,128)S(1)} %cholesky.272), custom_call_target="Cholesky" | custom-call | tf_op jit(solution)/shard_map/jit(cholesky)/cholesky | solution.py:73
  254.2 9.8 %custom-call.32 = f32[1,128,128]{1,2,0:T(8,128)S(1)} custom-call(f32[1,128,128]{2,1,0:T(8,128)S(1)} %get-tuple-element.55), custom_call_target="InvertDiagBlocksLowerTriangular" | custom-call | tf_op jit(solution)/shard_map/jit(cholesky)/cholesky | solution.py:73
  264.8 11.9 %cholesky.253 = f32[128,128]{1,0:T(8,128)S(1)} custom-call(f32[128,128]{1,0:T(8,128)S(1)} %convolution_subtract_fusion.5), custom_call_target="Cholesky" | custom-call | tf_op jit(solution)/shard_map/jit(cholesky)/cholesky | solution.py:73
  281.5 10.5 %while.1 = (s32[]{:T(128)}, f32[512,512]{0,1:T(8,128)S(1)}, s32[4,2]{0,1:T(2,128)S(1)}, f32[4,128,128]{2,1,0:T(8,128)}, s32[]{:T(128)}) while((s32[]{:T(128)}, f32[512,512]{0,1:T(8,128)S(1)}, s32[4,2]{0,1:T(2,128)S(1)}, f32[4,128,128]{2,1,0:T(8,128)}, s32[]{:T(128)}) %tuple.40), condition=%wide.while_cond, body=%wide.while_body.sunk | while | flops 2 | bytes 393329 | solution.py:74
  282.1 1.3 dynamic-slice.7
  284.7 1.3 dynamic-slice.7
  287.3 1.3 dynamic-slice.7
  290.0 1.3 dynamic-slice.7
  292.0 40.8 %custom-call.33 = f32[4,128,128]{1,2,0:T(8,128)} custom-call(f32[4,128,128]{2,1,0:T(8,128)} %get-tuple-element.9), custom_call_target="InvertDiagBlocksLowerTriangular" | custom-call | tf_op jit(solution)/shard_map/triangular_solve | solution.py:74
  332.7 1.5 fusion.14
  334.3 1.7 convolution_subtract_fusion.1
  335.9 1.3 fusion.34
  337.3 1.2 convolution_subtract_fusion
  339.0 1.8 convolution_subtract_fusion.2
  341.4 0.8 bitcast_dynamic-update-slice_fusion.1
  346.1 1.3 collective-permute-start.8
  348.0 13.4 %collective-permute-done.8 = f32[128,512]{0,1:T(8,128)S(1)} collective-permute-done((f32[128,512]{0,1:T(8,128)S(1)}, f32[128,512]{0,1:T(8,128)S(1)}, u32[]{:S(2)}, u32[]{:S(2)}) %collective-permute-start.8) | collective-permute-done | bytes 262176 | tf_op jit(solution)/shard_map/ppermute | solution.py:24
  362.2 4.8 %collective-permute-start.9 = (f32[128,512]{0,1:T(8,128)S(1)}, f32[128,512]{0,1:T(8,128)S(1)}, u32[]{:S(2)}, u32[]{:S(2)}) collective-permute-start(f32[128,512]{0,1:T(8,128)S(1)} %broadcast_select_fusion.7), channel_id=1, source_target_pairs={{0,32},{1,33},{2,34},{3,35},{4,36},{5,37},{6,38},{7,39},{8,40},{9,... | collective-permute-start | bytes 786440 | tf_op jit(solution)/shard_map/ppermute | solution.py:35
  366.9 9.6 %collective-permute-done.9 = f32[128,512]{0,1:T(8,128)S(1)} collective-permute-done((f32[128,512]{0,1:T(8,128)S(1)}, f32[128,512]{0,1:T(8,128)S(1)}, u32[]{:S(2)}, u32[]{:S(2)}) %collective-permute-start.9) | collective-permute-done | bytes 262176 | tf_op jit(solution)/shard_map/ppermute | solution.py:35
  377.4 4.3 collective-permute-start.10
  381.8 21.7 %collective-permute-done.10 = f32[2,128,512]{1,2,0:T(8,128)} collective-permute-done((f32[2,128,512]{1,2,0:T(8,128)S(1)}, f32[2,128,512]{1,2,0:T(8,128)}, u32[]{:S(2)}, u32[]{:S(2)}) %collective-permute-start.10) | collective-permute-done | bytes 524320 | tf_op jit(solution)/shard_map/ppermute | solution.py:35
  403.5 1.3 select_bitcast_fusion.5
  404.7 1.0 pad_maximum_fusion.3
  405.8 2.2 collective-permute-start.11
  408.2 1.1 copy-done.3
  409.3 0.9 copy.69
  410.2 19.5 %collective-permute-done.11 = f32[2,2,128,512]{2,3,1,0:T(8,128)} collective-permute-done((f32[2,2,128,512]{2,3,1,0:T(8,128)}, f32[2,2,128,512]{2,3,1,0:T(8,128)}, u32[]{:S(2)}, u32[]{:S(2)}) %collective-permute-start.11) | collective-permute-done | bytes 1048608 | tf_op jit(solution)/shard_map/ppermute | solution.py:35
  429.8 1.4 select_bitcast_fusion.1
  431.1 1.5 maximum_bitcast_fusion
  432.6 1.9 copy.66
  434.7 1.5 copy-done.5
  436.6 8.7 %copy_subtract_fusion = f32[5,128,8,128]{3,1,2,0:T(8,128)S(1)} fusion(f32[5,128,8,128]{3,2,1,0:T(8,128)S(1)} %copy-done.5, f32[1,128,512]{2,1,0:T(8,128)S(1)} %slice.162, f32[7,128,512]{2,1,0:T(8,128)S(1)} %slice.161, f32[5,128,512]{1,2,0:T(8,128)S(1)} %copy-done.4, pred[5]{0:T(512)(128)(4,1)S(1)} %add_compare_fusion), kind=kOutput, calls=%fused_computation.3 | convolution fusion | flops 4028366848 | bytes 8650757 | tf_op jit(solution)/shard_map/dot_general | solution.py:98
  445.3 3.0 copy.70
  (125 shorter events, 24.2 us)
Async XLA Ops:
  7.2 187.5 %all-reduce.4.cloned.1.call-start = ((), (), s32[]{:S(2)}) async-start(), calls=%async_computation | async-start | bytes 4718592 | tf_op jit(solution)/shard_map/psum | solution.py:72
  8.9 5.8 %copy-start.13 = (s32[2048]{0:T(1024)S(1)}, s32[2048]{0:T(1024)}, u32[]{:S(2)}) copy-start(s32[2048]{0:T(1024)} %param.16) | copy-start | bytes 24580
  14.7 14.9 %copy-start.21 = (pred[256]{0:T(512)(128)(4,1)S(1)}, pred[256]{0:T(512)(128)(4,1)}, u32[]{:S(2)}) copy-start(pred[256]{0:T(512)(128)(4,1)} %constant.197.clone) | copy-start | bytes 772
  18.9 23.6 %copy-start.20 = (pred[256]{0:T(512)(128)(4,1)S(1)}, pred[256]{0:T(512)(128)(4,1)}, u32[]{:S(2)}) copy-start(pred[256]{0:T(512)(128)(4,1)} %constant.198.clone) | copy-start | bytes 772
  19.8 34.7 %copy-start.19 = (pred[256]{0:T(512)(128)(4,1)S(1)}, pred[256]{0:T(512)(128)(4,1)}, u32[]{:S(2)}) copy-start(pred[256]{0:T(512)(128)(4,1)} %constant.199.clone) | copy-start | bytes 772
  19.8 20.7 %collective-permute-start = (bf16[2048,128]{1,0:T(8,128)(2,1)}, bf16[2048,128]{1,0:T(8,128)(2,1)S(1)}, u32[]{:S(2)}, u32[]{:S(2)}) collective-permute-start(bf16[2048,128]{1,0:T(8,128)(2,1)} %slice_bitcast_fusion), channel_id=1, source_target_pairs={{0,32},{1,33},{2,34},{3,35},{4,36},{5,37},{6,38},{7,39},{8,40},{9,... | collective-permute-start | bytes 1572872 | tf_op jit(solution)/shard_map/ppermute | solution.py:24
  41.2 24.7 %copy-start.18 = (pred[256]{0:T(512)(128)(4,1)S(1)}, pred[256]{0:T(512)(128)(4,1)}, u32[]{:S(2)}) copy-start(pred[256]{0:T(512)(128)(4,1)} %constant.200.clone) | copy-start | bytes 772
  41.2 11.2 %collective-permute-start.1 = (bf16[2048,128]{1,0:T(8,128)(2,1)S(1)}, bf16[2048,128]{1,0:T(8,128)(2,1)S(1)}, u32[]{:S(2)}, u32[]{:S(2)}) collective-permute-start(bf16[2048,128]{1,0:T(8,128)(2,1)S(1)} %broadcast_select_fusion.1), channel_id=1, source_target_pairs={{0,128},{1,129},{2,130},{3,131},{4,132},{5,133},{6,134},{7,135},{8... | collective-permute-start | bytes 1572872 | tf_op jit(solution)/shard_map/ppermute | solution.py:24
  53.1 10.7 %collective-permute-start.2 = (bf16[2048,128]{1,0:T(8,128)(2,1)S(1)}, bf16[2048,128]{1,0:T(8,128)(2,1)S(1)}, u32[]{:S(2)}, u32[]{:S(2)}) collective-permute-start(bf16[2048,128]{1,0:T(8,128)(2,1)S(1)} %broadcast_select_fusion.2), channel_id=1, source_target_pairs={{0,16},{1,17},{2,18},{3,19},{4,20},{5,21},{6,22},{7,23},{8,24},{9,... | collective-permute-start | bytes 1572872 | tf_op jit(solution)/shard_map/ppermute | solution.py:24
  64.5 10.0 %collective-permute-start.3 = (bf16[2048,128]{1,0:T(8,128)(2,1)S(1)}, bf16[2048,128]{1,0:T(8,128)(2,1)S(1)}, u32[]{:S(2)}, u32[]{:S(2)}) collective-permute-start(bf16[2048,128]{1,0:T(8,128)(2,1)S(1)} %broadcast_select_fusion.3), channel_id=1, source_target_pairs={{0,64},{1,65},{2,66},{3,67},{4,68},{5,69},{6,70},{7,71},{8,72},{9,... | collective-permute-start | bytes 1572872 | tf_op jit(solution)/shard_map/ppermute | solution.py:24
  75.2 15.6 %copy-start.9 = (bf16[2048,128]{1,0:T(8,128)(2,1)}, bf16[2048,128]{1,0:T(8,128)(2,1)S(1)}, u32[]{:S(2)}) copy-start(bf16[2048,128]{1,0:T(8,128)(2,1)S(1)} %broadcast_select_fusion.4) | copy-start | bytes 1572868
  75.2 26.4 %collective-permute-start.4 = (bf16[2048,128]{1,0:T(8,128)(2,1)S(1)}, bf16[2048,128]{1,0:T(8,128)(2,1)}, u32[]{:S(2)}, u32[]{:S(2)}) collective-permute-start(bf16[2048,128]{1,0:T(8,128)(2,1)S(1)} %broadcast_select_fusion.4), channel_id=1, source_target_pairs={{0,8},{1,9},{2,10},{3,11},{4,12},{5,13},{6,14},{7,15},{8,0},{9,1},... | collective-permute-start | bytes 1572872 | tf_op jit(solution)/shard_map/ppermute | solution.py:35
  102.8 0.8 copy-start
  104.7 4.9 %collective-permute-start.5 = (bf16[2,2048,128]{2,1,0:T(8,128)(2,1)}, bf16[2,2048,128]{2,1,0:T(8,128)(2,1)}, u32[]{:S(2)}, u32[]{:S(2)}) collective-permute-start(bf16[2,2048,128]{2,1,0:T(8,128)(2,1)} %pad_maximum_fusion.2), channel_id=1, source_target_pairs={{0,4},{1,5},{2,6},{3,7},{4,0},{5,1},{6,2},{7,3},{8,12},{9,13},{10,... | collective-permute-start | bytes 3145736 | tf_op jit(solution)/shard_map/ppermute | solution.py:35
  114.1 4.7 %copy-start.6 = (bf16[2048,5,128]{0,2,1:T(8,128)(2,1)S(1)}, bf16[2048,5,128]{0,2,1:T(8,128)(2,1)}, u32[]{:S(2)}) copy-start(bf16[2048,5,128]{0,2,1:T(8,128)(2,1)} %copy.64) | copy-start | bytes 7864324
  114.2 4.7 %copy-start.10 = (bf16[2048,4,128]{0,2,1:T(8,128)(2,1)S(1)}, bf16[2048,4,128]{0,2,1:T(8,128)(2,1)}, u32[]{:S(2)}) copy-start(bf16[2048,4,128]{0,2,1:T(8,128)(2,1)} %copy.54) | copy-start | bytes 6291460
  121.4 73.3 %copy-start.14 = (f32[512]{0:T(512)S(1)}, f32[512]{0:T(512)}, u32[]{:S(2)}) copy-start(f32[512]{0:T(512)} %param.17) | copy-start | bytes 6148
  194.7 1.8 copy-start.1
  281.5 55.8 %copy-start.11 = (f32[640,512]{1,0:T(8,128)S(1)}, f32[640,512]{1,0:T(8,128)}, u32[]{:S(2)}) copy-start(f32[640,512]{1,0:T(8,128)} %get-tuple-element.36) | copy-start | bytes 3932164
  332.7 5.7 %copy-start.12 = (f32[4,128,128]{1,2,0:T(8,128)S(1)}, f32[4,128,128]{1,2,0:T(8,128)}, u32[]{:S(2)}) copy-start(f32[4,128,128]{1,2,0:T(8,128)} %custom-call.33) | copy-start | bytes 786436
  341.3 1.6 copy-start.17
  341.3 3.5 copy-start.16
  341.4 6.0 %copy-start.15 = (pred[256]{0:T(512)(128)(4,1)S(1)}, pred[256]{0:T(512)(128)(4,1)}, u32[]{:S(2)}) copy-start(pred[256]{0:T(512)(128)(4,1)} %constant.203.clone) | copy-start | bytes 772
  342.2 1.3 collective-permute-start.6
  344.2 1.3 collective-permute-start.7
  346.1 15.3 %collective-permute-start.8 = (f32[128,512]{0,1:T(8,128)S(1)}, f32[128,512]{0,1:T(8,128)S(1)}, u32[]{:S(2)}, u32[]{:S(2)}) collective-permute-start(f32[128,512]{0,1:T(8,128)S(1)} %broadcast_select_fusion.6), channel_id=1, source_target_pairs={{0,4},{2,6},{5,1},{7,3},{8,12},{10,14},{13,9},{15,11},{16,20},{18,... | collective-permute-start | bytes 786440 | tf_op jit(solution)/shard_map/ppermute | solution.py:24
  362.2 14.4 %collective-permute-start.9 = (f32[128,512]{0,1:T(8,128)S(1)}, f32[128,512]{0,1:T(8,128)S(1)}, u32[]{:S(2)}, u32[]{:S(2)}) collective-permute-start(f32[128,512]{0,1:T(8,128)S(1)} %broadcast_select_fusion.7), channel_id=1, source_target_pairs={{0,32},{1,33},{2,34},{3,35},{4,36},{5,37},{6,38},{7,39},{8,40},{9,... | collective-permute-start | bytes 786440 | tf_op jit(solution)/shard_map/ppermute | solution.py:35
  376.6 0.7 copy-start.7
  376.6 0.8 copy-start.8
  377.4 26.1 %collective-permute-start.10 = (f32[2,128,512]{1,2,0:T(8,128)S(1)}, f32[2,128,512]{1,2,0:T(8,128)}, u32[]{:S(2)}, u32[]{:S(2)}) collective-permute-start(f32[2,128,512]{1,2,0:T(8,128)S(1)} %pad_maximum_fusion.4), channel_id=1, source_target_pairs={{0,16},{1,17},{2,18},{3,19},{4,20},{5,21},{6,22},{7,23},{8,24},{9,... | collective-permute-start | bytes 1572872 | tf_op jit(solution)/shard_map/ppermute | solution.py:35
  381.8 26.2 %copy-start.2 = (f32[5,128,512]{1,2,0:T(8,128)S(1)}, f32[5,128,512]{1,2,0:T(8,128)}, u32[]{:S(2)}) copy-start(f32[5,128,512]{1,2,0:T(8,128)} %get-tuple-element.38) | copy-start | bytes 3932164
  405.8 24.0 %collective-permute-start.11 = (f32[2,2,128,512]{2,3,1,0:T(8,128)}, f32[2,2,128,512]{2,3,1,0:T(8,128)}, u32[]{:S(2)}, u32[]{:S(2)}) collective-permute-start(f32[2,2,128,512]{2,3,1,0:T(8,128)} %pad_maximum_fusion.3), channel_id=1, source_target_pairs={{0,64},{1,65},{2,66},{3,67},{4,68},{5,69},{6,70},{7,71},{8,72},{9,... | collective-permute-start | bytes 3145736 | tf_op jit(solution)/shard_map/ppermute | solution.py:35
  408.2 1.1 copy-start.3
  434.5 1.7 copy-start.5
  434.5 2.1 copy-start.4
Sparse Core Ops, SparseCore 0:
  121.6 73.0 all-reduce.3

commit v2 on v1

v2 whole, which is shorter than its diff:
```python
import numpy as np
import jax
import jax.numpy as jnp
from jax import lax
from jax.sharding import PartitionSpec as P

NB = 128
PANEL = 512


def span_of(masks):
    values = [0]
    for mask in masks:
        values = values + [v ^ mask for v in values]
    return values


def tree_share(piece, holds, spread_rounds, gather_masks, row_count, col_count):
    row_pos = lax.axis_index("row")
    col_pos = lax.axis_index("col")
    flat_pos = row_pos * col_count + col_pos
    have = np.array(holds, dtype=bool)
    for round_masks in spread_rounds:
        gets_all = np.zeros_like(have)
        moved_list = []
        for mask in span_of(round_masks)[1:]:
            pairs = []
            gets = np.zeros_like(have)
            for r in range(row_count):
                for c in range(col_count):
                    if have[r, c] and not have[r ^ mask, c]:
                        pairs.append((r * col_count + c, (r ^ mask) * col_count + c))
                        gets[r ^ mask, c] = True
            assert not (gets & gets_all).any()
            gets_all = gets_all | gets
            moved_list.append((lax.ppermute(piece, ("row", "col"), pairs), gets))
        for moved, gets in moved_list:
            took = jnp.asarray(gets.reshape(-1))[flat_pos]
            piece = jnp.where(took, moved, piece)
        have = have | gets_all
    assert have.all()
    offsets = span_of(gather_masks)
    recv = [piece]
    for mask in offsets[1:]:
        pairs = [
            (r * col_count + c, (r ^ mask) * col_count + c)
            for r in range(row_count)
            for c in range(col_count)
        ]
        recv.append(lax.ppermute(piece, ("row", "col"), pairs))
    stacked = jnp.stack(recv)
    own_value = sum(
        jnp.where((row_pos & mask) != 0, 1 << bit, 0) for bit, mask in enumerate(gather_masks)
    )
    return jnp.stack(
        [lax.dynamic_index_in_dim(stacked, u ^ own_value, 0, keepdims=False) for u in range(len(offsets))]
    )


def local(green, arrival, row_gauge, row_time, damping, trail):
    row_count = lax.axis_size("row")
    col_count = lax.axis_size("col")
    row_pos = lax.axis_index("row")
    col_pos = lax.axis_index("col")
    kq_rows, tile_rows, tile_width = green.shape
    panel_tiles = PANEL // NB
    far_slots = trail.shape[2]
    arrive = arrival[row_gauge][:, :, 0]
    is_live = row_time[:, None] >= arrive
    masked = jnp.where(is_live[:, :, None], green, jnp.zeros_like(green))
    flat_green = masked.reshape(kq_rows, tile_rows * tile_width)

    panel_holds = np.zeros((row_count, col_count), dtype=bool)
    panel_holds[:panel_tiles, :] = True
    panel_stack = tree_share(
        masked[:, 0, :], panel_holds, ((4, 8), (16, 32)), (1, 2), row_count, col_count
    )
    panel_cols = jnp.transpose(panel_stack, (1, 0, 2)).reshape(kq_rows, PANEL)

    contract_rows = (((0,), (0,)), ((), ()))
    diag_part = lax.dot_general(
        panel_cols, panel_cols, contract_rows, preferred_element_type=jnp.float32
    )
    partial_value = lax.dot_general(
        flat_green, panel_cols, contract_rows, preferred_element_type=jnp.float32
    )
    diag_block = lax.psum(diag_part, "col")
    diag_block, partial_value = lax.optimization_barrier((diag_block, partial_value))
    normal_rows = lax.psum(partial_value, "col")

    far_holds = np.zeros((row_count, col_count), dtype=bool)
    for slot_no in range(far_slots):
        for c in range(col_count):
            far_holds[panel_tiles + slot_no * col_count + c, c] = True
    far_shared = tree_share(
        normal_rows[:tile_width], far_holds, ((32,), (1, 2)), (4, 8, 16), row_count, col_count
    )
    far_normal = jnp.roll(far_shared, -1, axis=0).reshape(far_slots * tile_width, PANEL)

    factor = jnp.linalg.cholesky(diag_block + jnp.diag(damping))
    factor_inv = lax.linalg.triangular_solve(
        factor, jnp.eye(PANEL, dtype=jnp.float32), left_side=True, lower=True
    )
    by_inverse = (((1,), (1,)), ((), ()))
    solved = lax.dot_general(
        normal_rows, factor_inv, by_inverse,
        precision=lax.Precision.HIGHEST, preferred_element_type=jnp.float32,
    )
    far_rows = lax.dot_general(
        far_normal, factor_inv, by_inverse,
        precision=lax.Precision.HIGHEST, preferred_element_type=jnp.float32,
    )
    solved = solved.reshape(tile_rows, tile_width, PANEL)
    tiles_list = []
    for local_no in range(tile_rows):
        tile_id = local_no * row_count + row_pos
        diag_rows = lax.dynamic_slice_in_dim(
            factor, jnp.minimum(tile_id, panel_tiles - 1) * tile_width, tile_width, 0
        )
        tiles_list.append(jnp.where(tile_id < panel_tiles, diag_rows, solved[local_no]))
    lower_rows = jnp.stack(tiles_list)
    col_share = PANEL // col_count
    chol_out = lax.dynamic_slice_in_dim(lower_rows, col_pos * col_share, col_share, 2)

    update = lax.dot_general(
        lower_rows.reshape(tile_rows * tile_width, PANEL),
        far_rows,
        (((1,), (1,)), ((), ())),
        precision=lax.Precision.HIGHEST,
        preferred_element_type=jnp.float32,
    )
    update = update.reshape(tile_rows, tile_width, far_slots, tile_width)
    tile_ids = jnp.arange(tile_rows, dtype=jnp.int32) * row_count + row_pos
    below_panel = (tile_ids >= panel_tiles)[:, None, None, None]
    return (chol_out, trail - jnp.where(below_panel, update, jnp.zeros_like(update)))


def solution(mesh):
    return jax.shard_map(
        local,
        mesh=mesh,
        in_specs=(
            P("col", None, "row"),
            P(None, None, "row"),
            P("col"),
            P("col"),
            P(),
            P(None, "row", None, "col"),
        ),
        out_specs=(P(None, "row", "col"), P(None, "row", None, "col")),
        check_vma=False,
    )
```

time: 463 us -> 442 us (0.955)
  the two profiles are of different devices: /device:TPU:1 before, /device:TPU:52 now
where the time goes in v2:
time: 442 us; the launch traced here: 436 us
  waiting for transfers between devices  162 us (37%)
  other arithmetic  134 us (30%)
  local copies, waits for them, and re-layouts  52.7 us (12%)
  starting transfers between devices  35.3 us (8%)
  matrix products  35 us (8%)
  between operations  17.7 us (4%)
    another operation x14, other arithmetic, local(): factor = jnp.linalg.cholesky(diag_block + jnp.diag(damping))  79 us
    ppermute x10, waiting for transfers between devices, tree_share(): moved_list.append((lax.ppermute(piece, ('row', 'col'), pairs), gets))  54 us
    ppermute x10, waiting for transfers between devices, tree_share(): recv.append(lax.ppermute(piece, ('row', 'col'), pairs))  53.8 us
    psum x1, waiting for transfers between devices, local(): diag_block = lax.psum(diag_part, 'col')  53.6 us
    another operation x3, other arithmetic, local(): lax.linalg.triangular_solve(factor, jnp.eye(PANEL, dtype=jnp.float32), le...  41.4 us
    ppermute x10, starting transfers between devices, tree_share(): recv.append(lax.ppermute(piece, ('row', 'col'), pairs))  23.9 us
    unnamed x63, local copies, waits for them, and re-layouts  19.4 us
    another operation x20, local copies, waits for them, and re-layouts  14.8 us
  transfers between devices with their start and end apart: 22, of which 9 were waited for; matrix products, arithmetic and copies ran while one was open for 20% of the time, Pallas kernels for 0%

profile of v2, /device:TPU:52, one launch (start us, length us, event | category | flops | bytes accessed | tf_op | source)
XLA Modules:
  0.0 436.1 jit_solution(12076559655328019647)
XLA Ops:
  7.2 3.0 copy.63
  10.5 7.6 %gather_fusion = s32[2048,5]{1,0:T(8,128)} fusion(s32[1200,5]{1,0:T(8,128)S(1)} %bitcast.124, s32[2048]{0:T(1024)S(1)} %fusion.48), kind=kCustom, calls=%fused_computation | custom fusion | bytes 90112 | tf_op jit(solution)/shard_map/gather | solution.py:68
  18.2 1.5 copy.62
  20.0 1.5 copy-done
  25.6 3.1 select_select_fusion.2
  29.4 1.3 collective-permute-start.4
  33.2 50.1 %collective-permute-done.4 = bf16[2048,128]{0,1:T(8,128)(2,1)S(1)} collective-permute-done((bf16[2048,128]{0,1:T(8,128)(2,1)S(1)}, bf16[2048,128]{0,1:T(8,128)(2,1)S(1)}, u32[]{:S(2)}, u32[]{:S(2)}) %collective-permute-start.4) | collective-permute-done | bytes 524320 | tf_op jit(solution)/shard_map/ppermute | solution.py:36
  83.3 2.1 select_select_fusion.1
  85.7 1.9 collective-permute-start.6
  87.6 12.7 %collective-permute-done.7 = bf16[2048,128]{0,1:T(8,128)(2,1)S(1)} collective-permute-done((bf16[2048,128]{0,1:T(8,128)(2,1)S(1)}, bf16[2048,128]{0,1:T(8,128)(2,1)S(1)}, u32[]{:S(2)}, u32[]{:S(2)}) %collective-permute-start.7) | collective-permute-done | bytes 524320 | tf_op jit(solution)/shard_map/ppermute | solution.py:50
  100.3 6.9 %collective-permute-done.8 = bf16[2048,128]{0,1:T(8,128)(2,1)S(1)} collective-permute-done((bf16[2048,128]{0,1:T(8,128)(2,1)S(1)}, bf16[2048,128]{0,1:T(8,128)(2,1)S(1)}, u32[]{:S(2)}, u32[]{:S(2)}) %collective-permute-start.8) | collective-permute-done | bytes 524320 | tf_op jit(solution)/shard_map/ppermute | solution.py:50
  108.0 1.3 copy-done.7
  109.4 2.3 fusion.54
  114.7 1.1 fusion.15
  115.8 4.2 fusion.55
  120.0 53.6 %all-reduce.4.cloned.1.call-done = f32[512,512]{0,1:T(8,128)} async-done(((f32[512,512]{0,1:T(8,128)}), f32[512,512]{0,1:T(8,128)}) %all-reduce.4.cloned.1.call-update) | async-done | bytes 1048592 | tf_op jit(solution)/shard_map/psum | solution.py:87
  173.7 1.4 select_add_fusion
  175.7 11.7 %cholesky.103 = f32[128,128]{1,0:T(8,128)S(1)} custom-call(f32[128,128]{1,0:T(8,128)S(1)} %cholesky.263), custom_call_target="Cholesky" | custom-call | tf_op jit(solution)/shard_map/jit(cholesky)/cholesky | solution.py:100
  187.4 9.8 %custom-call.30 = f32[1,128,128]{1,2,0:T(8,128)S(1)} custom-call(f32[1,128,128]{2,1,0:T(8,128)S(1)} %get-tuple-element.55), custom_call_target="InvertDiagBlocksLowerTriangular" | custom-call | tf_op jit(solution)/shard_map/jit(cholesky)/cholesky | solution.py:100
  197.9 12.1 %cholesky.215 = f32[128,128]{1,0:T(8,128)S(1)} custom-call(f32[128,128]{1,0:T(8,128)S(1)} %cholesky.267), custom_call_target="Cholesky" | custom-call | tf_op jit(solution)/shard_map/jit(cholesky)/cholesky | solution.py:100
  210.5 9.8 %custom-call.31 = f32[1,128,128]{1,2,0:T(8,128)S(1)} custom-call(f32[1,128,128]{2,1,0:T(8,128)S(1)} %get-tuple-element.53), custom_call_target="InvertDiagBlocksLowerTriangular" | custom-call | tf_op jit(solution)/shard_map/jit(cholesky)/cholesky | solution.py:100
  220.8 1.5 convolution_subtract_fusion.4
  222.3 11.7 %cholesky.236 = f32[128,128]{1,0:T(8,128)S(1)} custom-call(f32[128,128]{1,0:T(8,128)S(1)} %cholesky.272), custom_call_target="Cholesky" | custom-call | tf_op jit(solution)/shard_map/jit(cholesky)/cholesky | solution.py:100
  234.1 9.8 %custom-call.32 = f32[1,128,128]{1,2,0:T(8,128)S(1)} custom-call(f32[1,128,128]{2,1,0:T(8,128)S(1)} %get-tuple-element.51), custom_call_target="InvertDiagBlocksLowerTriangular" | custom-call | tf_op jit(solution)/shard_map/jit(cholesky)/cholesky | solution.py:100
  244.3 1.3 convolution_subtract_fusion.5
  245.6 11.9 %cholesky.253 = f32[128,128]{1,0:T(8,128)S(1)} custom-call(f32[128,128]{1,0:T(8,128)S(1)} %convolution_subtract_fusion.5), custom_call_target="Cholesky" | custom-call | tf_op jit(solution)/shard_map/jit(cholesky)/cholesky | solution.py:100
  262.1 1.2 fusion.8
  263.3 14.8 %while.1 = (s32[]{:T(128)}, f32[512,512]{0,1:T(8,128)}, s32[4,2]{0,1:T(2,128)S(1)}, f32[4,128,128]{2,1,0:T(8,128)}, s32[]{:T(128)}) while((s32[]{:T(128)}, f32[512,512]{0,1:T(8,128)}, s32[4,2]{0,1:T(2,128)S(1)}, f32[4,128,128]{2,1,0:T(8,128)}, s32[]{:T(128)}) %tuple.40), condition=%wide.while_cond, body=%wide.while_body.sunk | while | flops 2 | bytes 393829 | solution.py:101
  264.0 2.3 dynamic-slice.7
  267.7 2.3 dynamic-slice.7
  271.5 2.3 dynamic-slice.7
  275.2 2.2 dynamic-slice.7
  278.2 40.1 %custom-call.33 = f32[4,128,128]{1,2,0:T(8,128)S(1)} custom-call(f32[4,128,128]{2,1,0:T(8,128)} %get-tuple-element.13), custom_call_target="InvertDiagBlocksLowerTriangular" | custom-call | tf_op jit(solution)/shard_map/triangular_solve | solution.py:101
  318.6 1.6 convolution_subtract_fusion.1
  320.7 1.9 convolution_subtract_fusion
  323.0 2.4 convolution_subtract_fusion.2
  325.4 1.3 fusion.39
  326.7 1.0 slice.160
  327.7 2.4 collective-permute-start.9
  330.1 4.0 fusion.14
  334.3 1.7 broadcast_select_fusion.1
  336.0 1.3 collective-permute-start.10
  337.3 1.3 collective-permute-start.11
  338.6 1.3 collective-permute-start.12
  340.0 1.1 collective-permute-done.10
  341.1 2.8 collective-permute-done.11
  343.9 2.8 bitcast_dynamic-update-slice_fusion.8
  346.7 5.7 %collective-permute-start.13 = (f32[128,512]{1,0:T(8,128)}, f32[128,512]{1,0:T(8,128)}, u32[]{:S(2)}, u32[]{:S(2)}) collective-permute-start(f32[128,512]{1,0:T(8,128)} %get-tuple-element.41), channel_id=1, source_target_pairs={{0,16},{1,17},{2,18},{3,19},{4,20},{5,21},{6,22},{7,23},{8,24},{9,... | collective-permute-start | bytes 786440 | tf_op jit(solution)/shard_map/ppermute | solution.py:50
  352.5 3.1 collective-permute-start.14
  357.0 1.6 collective-permute-start.16
  358.6 2.8 collective-permute-start.17
  361.4 16.3 %collective-permute-done.13 = f32[128,512]{1,0:T(8,128)} collective-permute-done((f32[128,512]{1,0:T(8,128)}, f32[128,512]{1,0:T(8,128)}, u32[]{:S(2)}, u32[]{:S(2)}) %collective-permute-start.13) | collective-permute-done | bytes 262176 | tf_op jit(solution)/shard_map/ppermute | solution.py:50
  377.8 5.5 %collective-permute-start.18 = (f32[128,512]{1,0:T(8,128)}, f32[128,512]{1,0:T(8,128)S(1)}, u32[]{:S(2)}, u32[]{:S(2)}) collective-permute-start(f32[128,512]{1,0:T(8,128)} %get-tuple-element.41), channel_id=1, source_target_pairs={{0,96},{1,97},{2,98},{3,99},{4,100},{5,101},{6,102},{7,103},{8,104... | collective-permute-start | bytes 786440 | tf_op jit(solution)/shard_map/ppermute | solution.py:50
  383.2 1.7 bitcast_dynamic-update-slice_fusion.7
  384.9 2.4 collective-permute-start.19
  390.2 10.1 %collective-permute-done.18 = f32[128,512]{1,0:T(8,128)S(1)} collective-permute-done((f32[128,512]{1,0:T(8,128)}, f32[128,512]{1,0:T(8,128)S(1)}, u32[]{:S(2)}, u32[]{:S(2)}) %collective-permute-start.18) | collective-permute-done | bytes 262176 | tf_op jit(solution)/shard_map/ppermute | solution.py:50
  401.0 7.8 %collective-permute-done.19 = f32[128,512]{1,0:T(8,128)S(1)} collective-permute-done((f32[128,512]{1,0:T(8,128)}, f32[128,512]{1,0:T(8,128)S(1)}, u32[]{:S(2)}, u32[]{:S(2)}) %collective-permute-start.19) | collective-permute-done | bytes 262176 | tf_op jit(solution)/shard_map/ppermute | solution.py:50
  409.6 1.1 dynamic-slice_dynamic-update-slice_fusion.7
  410.7 1.0 dynamic-slice_dynamic-update-slice_fusion.6
  411.7 1.0 dynamic-slice_dynamic-update-slice_fusion.5
  412.6 1.0 dynamic-slice_dynamic-update-slice_fusion.4
  413.8 3.5 fusion.5
  417.3 8.6 %copy_subtract_fusion = f32[5,128,8,128]{3,1,2,0:T(8,128)S(1)} fusion(f32[5,128,8,128]{3,2,1,0:T(8,128)S(1)} %copy-done.6, f32[8,128,512]{2,1,0:T(8,128)S(1)} %fusion.5, f32[5,128,512]{1,2,0:T(8,128)S(1)} %fusion.20, pred[5]{0:T(512)(128)(4,1)S(1)} %add_compare_fusion), kind=kOutput, calls=%fused_computation.3 | convolution fusion | flops 4027842560 | bytes 8650757 | tf_op jit(solution)/shard_map/dot_general | solution.py:125
  425.9 3.0 copy.85
  (154 shorter events, 29.4 us)
Async XLA Ops:
  7.2 3.1 copy-start.9
  7.2 3.3 copy-start.10
  7.2 166.5 %all-reduce.4.cloned.1.call-start = ((), (), s32[]{:S(2)}) async-start(), calls=%async_computation | async-start | bytes 2097152 | tf_op jit(solution)/shard_map/psum | solution.py:87
  10.5 9.2 %copy-start.11 = (s32[2048]{0:T(1024)S(1)}, s32[2048]{0:T(1024)}, u32[]{:S(2)}) copy-start(s32[2048]{0:T(1024)} %param.19) | copy-start | bytes 24580
  19.8 3.9 copy-start.22
  19.8 4.5 %copy-start.21 = (pred[256]{0:T(512)(128)(4,1)S(1)}, pred[256]{0:T(512)(128)(4,1)}, u32[]{:S(2)}) copy-start(pred[256]{0:T(512)(128)(4,1)} %constant.238.clone) | copy-start | bytes 772
  19.8 5.2 %copy-start.20 = (pred[256]{0:T(512)(128)(4,1)S(1)}, pred[256]{0:T(512)(128)(4,1)}, u32[]{:S(2)}) copy-start(pred[256]{0:T(512)(128)(4,1)} %constant.237.clone) | copy-start | bytes 772
  20.0 1.5 copy-start
  21.5 9.9 %copy-start.19 = (pred[256]{0:T(512)(128)(4,1)S(1)}, pred[256]{0:T(512)(128)(4,1)}, u32[]{:S(2)}) copy-start(pred[256]{0:T(512)(128)(4,1)} %constant.242.clone) | copy-start | bytes 772
  21.5 10.5 %copy-start.18 = (pred[256]{0:T(512)(128)(4,1)S(1)}, pred[256]{0:T(512)(128)(4,1)}, u32[]{:S(2)}) copy-start(pred[256]{0:T(512)(128)(4,1)} %constant.241.clone) | copy-start | bytes 772
  21.5 11.2 %copy-start.17 = (pred[256]{0:T(512)(128)(4,1)S(1)}, pred[256]{0:T(512)(128)(4,1)}, u32[]{:S(2)}) copy-start(pred[256]{0:T(512)(128)(4,1)} %constant.240.clone) | copy-start | bytes 772
  21.6 4.0 collective-permute-start
  22.3 3.3 collective-permute-start.1
  23.0 2.6 collective-permute-start.2
  28.7 4.6 %collective-permute-start.3 = (bf16[2048,128]{0,1:T(8,128)(2,1)S(1)}, bf16[2048,128]{0,1:T(8,128)(2,1)S(1)}, u32[]{:S(2)}, u32[]{:S(2)}) collective-permute-start(bf16[2048,128]{0,1:T(8,128)(2,1)S(1)} %select_select_fusion.2), channel_id=1, source_target_pairs={{0,192},{1,193},{2,194},{3,195},{4,196},{5,197},{6,198},{7,199},{8... | collective-permute-start | bytes 1572872 | tf_op jit(solution)/shard_map/ppermute | solution.py:36
  29.4 53.9 %collective-permute-start.4 = (bf16[2048,128]{0,1:T(8,128)(2,1)S(1)}, bf16[2048,128]{0,1:T(8,128)(2,1)S(1)}, u32[]{:S(2)}, u32[]{:S(2)}) collective-permute-start(bf16[2048,128]{0,1:T(8,128)(2,1)S(1)} %select_select_fusion.2), channel_id=1, source_target_pairs={{0,128},{1,129},{2,130},{3,131},{4,132},{5,133},{6,134},{7,135},{8... | collective-permute-start | bytes 1572872 | tf_op jit(solution)/shard_map/ppermute | solution.py:36
  30.7 52.6 %collective-permute-start.5 = (bf16[2048,128]{0,1:T(8,128)(2,1)S(1)}, bf16[2048,128]{0,1:T(8,128)(2,1)S(1)}, u32[]{:S(2)}, u32[]{:S(2)}) collective-permute-start(bf16[2048,128]{0,1:T(8,128)(2,1)S(1)} %select_select_fusion.2), channel_id=1, source_target_pairs={{0,64},{1,65},{2,66},{3,67},{4,68},{5,69},{6,70},{7,71},{8,72},{9,... | collective-permute-start | bytes 1572872 | tf_op jit(solution)/shard_map/ppermute | solution.py:36
  85.4 14.9 %collective-permute-start.7 = (bf16[2048,128]{0,1:T(8,128)(2,1)S(1)}, bf16[2048,128]{0,1:T(8,128)(2,1)S(1)}, u32[]{:S(2)}, u32[]{:S(2)}) collective-permute-start(bf16[2048,128]{0,1:T(8,128)(2,1)S(1)} %select_select_fusion.1), channel_id=1, source_target_pairs={{0,8},{1,9},{2,10},{3,11},{4,12},{5,13},{6,14},{7,15},{8,0},{9,1},... | collective-permute-start | bytes 1572872 | tf_op jit(solution)/shard_map/ppermute | solution.py:50
  85.5 21.8 %collective-permute-start.8 = (bf16[2048,128]{0,1:T(8,128)(2,1)S(1)}, bf16[2048,128]{0,1:T(8,128)(2,1)S(1)}, u32[]{:S(2)}, u32[]{:S(2)}) collective-permute-start(bf16[2048,128]{0,1:T(8,128)(2,1)S(1)} %select_select_fusion.1), channel_id=1, source_target_pairs={{0,12},{1,13},{2,14},{3,15},{4,8},{5,9},{6,10},{7,11},{8,4},{9,5},... | collective-permute-start | bytes 1572872 | tf_op jit(solution)/shard_map/ppermute | solution.py:50
  85.7 21.5 %collective-permute-start.6 = (bf16[2048,128]{0,1:T(8,128)(2,1)S(1)}, bf16[2048,128]{0,1:T(8,128)(2,1)S(1)}, u32[]{:S(2)}, u32[]{:S(2)}) collective-permute-start(bf16[2048,128]{0,1:T(8,128)(2,1)S(1)} %select_select_fusion.1), channel_id=1, source_target_pairs={{0,4},{1,5},{2,6},{3,7},{4,0},{5,1},{6,2},{7,3},{8,12},{9,13},{10,... | collective-permute-start | bytes 1572872 | tf_op jit(solution)/shard_map/ppermute | solution.py:50
  108.0 1.3 copy-start.7
  109.4 2.7 copy-start.16
  109.4 3.4 copy-start.15
  109.4 4.0 copy-start.14
  109.4 4.6 %copy-start.13 = (pred[256]{0:T(512)(128)(4,1)S(1)}, pred[256]{0:T(512)(128)(4,1)}, u32[]{:S(2)}) copy-start(pred[256]{0:T(512)(128)(4,1)} %constant.244.clone) | copy-start | bytes 772
  109.4 6.4 %copy-start.1 = (bf16[2048,5,128]{0,2,1:T(8,128)(2,1)S(1)}, bf16[2048,5,128]{0,2,1:T(8,128)(2,1)}, u32[]{:S(2)}) copy-start(bf16[2048,5,128]{0,2,1:T(8,128)(2,1)} %copy-done) | copy-start | bytes 7864324
  111.7 215.0 %all-reduce.6.cloned.1.call-start = ((), (), s32[]{:S(2)}) async-start(), calls=%async_computation.1 | async-start | bytes 2621440 | tf_op jit(solution)/shard_map/psum | solution.py:89
  115.8 57.8 %copy-start.12 = (f32[512]{0:T(512)S(1)}, f32[512]{0:T(512)}, u32[]{:S(2)}) copy-start(f32[512]{0:T(512)} %param.20) | copy-start | bytes 6148
  173.7 1.8 copy-start.2
  175.7 34.8 %copy-start.4 = (f32[512,512]{1,0:T(8,128)}, f32[512,512]{1,0:T(8,128)S(1)}, u32[]{:S(2)}) copy-start(f32[512,512]{1,0:T(8,128)S(1)} %fusion.7) | copy-start | bytes 3145732
  263.3 57.3 %copy-start.3 = (f32[512,512]{0,1:T(8,128)S(1)}, f32[512,512]{0,1:T(8,128)}, u32[]{:S(2)}) copy-start(f32[512,512]{0,1:T(8,128)} %fusion.15) | copy-start | bytes 3145732
  318.3 4.3 copy-start.8
  327.7 6.6 %collective-permute-start.9 = (f32[128,512]{1,0:T(8,128)S(1)}, f32[128,512]{1,0:T(8,128)S(1)}, u32[]{:S(2)}, u32[]{:S(2)}) collective-permute-start(f32[128,512]{1,0:T(8,128)S(1)} %slice.160), channel_id=1, source_target_pairs={{16,144},{21,149},{26,154},{31,159},{32,160},{37,165},{42,170},{47... | collective-permute-start | bytes 786440 | tf_op jit(solution)/shard_map/ppermute | solution.py:36
  336.0 5.2 %collective-permute-start.10 = (f32[128,512]{1,0:T(8,128)S(1)}, f32[128,512]{1,0:T(8,128)S(1)}, u32[]{:S(2)}, u32[]{:S(2)}) collective-permute-start(f32[128,512]{1,0:T(8,128)S(1)} %broadcast_select_fusion.1), channel_id=1, source_target_pairs={{0,12},{5,9},{10,6},{15,3},{16,28},{21,25},{26,22},{31,19},{32,44}... | collective-permute-start | bytes 786440 | tf_op jit(solution)/shard_map/ppermute | solution.py:36
  337.3 6.7 %collective-permute-start.11 = (f32[128,512]{1,0:T(8,128)S(1)}, f32[128,512]{1,0:T(8,128)S(1)}, u32[]{:S(2)}, u32[]{:S(2)}) collective-permute-start(f32[128,512]{1,0:T(8,128)S(1)} %broadcast_select_fusion.1), channel_id=1, source_target_pairs={{0,8},{5,13},{10,2},{15,7},{16,24},{21,29},{26,18},{31,23},{32,40}... | collective-permute-start | bytes 786440 | tf_op jit(solution)/shard_map/ppermute | solution.py:36
  338.6 5.4 %collective-permute-start.12 = (f32[128,512]{1,0:T(8,128)S(1)}, f32[128,512]{1,0:T(8,128)S(1)}, u32[]{:S(2)}, u32[]{:S(2)}) collective-permute-start(f32[128,512]{1,0:T(8,128)S(1)} %broadcast_select_fusion.1), channel_id=1, source_target_pairs={{0,4},{5,1},{10,14},{15,11},{16,20},{21,17},{26,30},{31,27},{32,36... | collective-permute-start | bytes 786440 | tf_op jit(solution)/shard_map/ppermute | solution.py:36
  346.7 31.1 %collective-permute-start.13 = (f32[128,512]{1,0:T(8,128)}, f32[128,512]{1,0:T(8,128)}, u32[]{:S(2)}, u32[]{:S(2)}) collective-permute-start(f32[128,512]{1,0:T(8,128)} %get-tuple-element.41), channel_id=1, source_target_pairs={{0,16},{1,17},{2,18},{3,19},{4,20},{5,21},{6,22},{7,23},{8,24},{9,... | collective-permute-start | bytes 786440 | tf_op jit(solution)/shard_map/ppermute | solution.py:50
  352.5 32.4 %collective-permute-start.14 = (f32[128,512]{1,0:T(8,128)}, f32[128,512]{1,0:T(8,128)S(1)}, u32[]{:S(2)}, u32[]{:S(2)}) collective-permute-start(f32[128,512]{1,0:T(8,128)} %get-tuple-element.41), channel_id=1, source_target_pairs={{0,32},{1,33},{2,34},{3,35},{4,36},{5,37},{6,38},{7,39},{8,40},{9,... | collective-permute-start | bytes 786440 | tf_op jit(solution)/shard_map/ppermute | solution.py:50
  356.5 31.6 %collective-permute-start.15 = (f32[128,512]{1,0:T(8,128)}, f32[128,512]{1,0:T(8,128)S(1)}, u32[]{:S(2)}, u32[]{:S(2)}) collective-permute-start(f32[128,512]{1,0:T(8,128)} %get-tuple-element.41), channel_id=1, source_target_pairs={{0,48},{1,49},{2,50},{3,51},{4,52},{5,53},{6,54},{7,55},{8,56},{9,... | collective-permute-start | bytes 786440 | tf_op jit(solution)/shard_map/ppermute | solution.py:50
  357.0 31.8 %collective-permute-start.16 = (f32[128,512]{1,0:T(8,128)}, f32[128,512]{1,0:T(8,128)S(1)}, u32[]{:S(2)}, u32[]{:S(2)}) collective-permute-start(f32[128,512]{1,0:T(8,128)} %get-tuple-element.41), channel_id=1, source_target_pairs={{0,64},{1,65},{2,66},{3,67},{4,68},{5,69},{6,70},{7,71},{8,72},{9,... | collective-permute-start | bytes 786440 | tf_op jit(solution)/shard_map/ppermute | solution.py:50
  358.6 30.9 %collective-permute-start.17 = (f32[128,512]{1,0:T(8,128)}, f32[128,512]{1,0:T(8,128)S(1)}, u32[]{:S(2)}, u32[]{:S(2)}) collective-permute-start(f32[128,512]{1,0:T(8,128)} %get-tuple-element.41), channel_id=1, source_target_pairs={{0,80},{1,81},{2,82},{3,83},{4,84},{5,85},{6,86},{7,87},{8,88},{9,... | collective-permute-start | bytes 786440 | tf_op jit(solution)/shard_map/ppermute | solution.py:50
  377.8 22.6 %collective-permute-start.18 = (f32[128,512]{1,0:T(8,128)}, f32[128,512]{1,0:T(8,128)S(1)}, u32[]{:S(2)}, u32[]{:S(2)}) collective-permute-start(f32[128,512]{1,0:T(8,128)} %get-tuple-element.41), channel_id=1, source_target_pairs={{0,96},{1,97},{2,98},{3,99},{4,100},{5,101},{6,102},{7,103},{8,104... | collective-permute-start | bytes 786440 | tf_op jit(solution)/shard_map/ppermute | solution.py:50
  384.9 23.9 %collective-permute-start.19 = (f32[128,512]{1,0:T(8,128)}, f32[128,512]{1,0:T(8,128)S(1)}, u32[]{:S(2)}, u32[]{:S(2)}) collective-permute-start(f32[128,512]{1,0:T(8,128)} %get-tuple-element.41), channel_id=1, source_target_pairs={{0,112},{1,113},{2,114},{3,115},{4,116},{5,117},{6,118},{7,119},{8... | collective-permute-start | bytes 786440 | tf_op jit(solution)/shard_map/ppermute | solution.py:50
  409.6 4.1 copy-start.5
  413.8 3.5 copy-start.6
Sparse Core Ops, SparseCore 0:
  111.8 61.7 all-reduce.3
  257.7 53.8 all-reduce.5

commit v3 on v2

--- a/solution.py
+++ b/solution.py
@@ -15,7 +15,7 @@
     return values
 
 
-def tree_share(piece, holds, spread_rounds, gather_masks, row_count, col_count):
+def spread_share(piece, holds, spread_rounds, row_count, col_count):
     row_pos = lax.axis_index("row")
     col_pos = lax.axis_index("col")
     flat_pos = row_pos * col_count + col_pos
@@ -39,6 +39,11 @@
             piece = jnp.where(took, moved, piece)
         have = have | gets_all
     assert have.all()
+    return piece
+
+
+def gather_share(piece, gather_masks, row_count, col_count):
+    row_pos = lax.axis_index("row")
     offsets = span_of(gather_masks)
     recv = [piece]
     for mask in offsets[1:]:
@@ -72,9 +77,10 @@
 
     panel_holds = np.zeros((row_count, col_count), dtype=bool)
     panel_holds[:panel_tiles, :] = True
-    panel_stack = tree_share(
-        masked[:, 0, :], panel_holds, ((4, 8), (16, 32)), (1, 2), row_count, col_count
+    panel_piece = spread_share(
+        masked[:, 0, :], panel_holds, ((8,), (32,), (4,), (16,)), row_count, col_count
     )
+    panel_stack = gather_share(panel_piece, (1, 2), row_count, col_count)
     panel_cols = jnp.transpose(panel_stack, (1, 0, 2)).reshape(kq_rows, PANEL)
 
     contract_rows = (((0,), (0,)), ((), ()))
@@ -92,15 +98,17 @@
     for slot_no in range(far_slots):
         for c in range(col_count):
             far_holds[panel_tiles + slot_no * col_count + c, c] = True
-    far_shared = tree_share(
-        normal_rows[:tile_width], far_holds, ((32,), (1, 2)), (4, 8, 16), row_count, col_count
+    far_piece = spread_share(
+        normal_rows[:tile_width], far_holds, ((32,), (1, 2)), row_count, col_count
     )
-    far_normal = jnp.roll(far_shared, -1, axis=0).reshape(far_slots * tile_width, PANEL)
-
     factor = jnp.linalg.cholesky(diag_block + jnp.diag(damping))
+    factor, far_piece = lax.optimization_barrier((factor, far_piece))
+    far_shared = gather_share(far_piece, (4, 8, 16), row_count, col_count)
     factor_inv = lax.linalg.triangular_solve(
         factor, jnp.eye(PANEL, dtype=jnp.float32), left_side=True, lower=True
     )
+    factor_inv, far_shared = lax.optimization_barrier((factor_inv, far_shared))
+    far_normal = jnp.roll(far_shared, -1, axis=0).reshape(far_slots * tile_width, PANEL)
     by_inverse = (((1,), (1,)), ((), ()))
     solved = lax.dot_general(
         normal_rows, factor_inv, by_inverse,

time: 442 us -> 420 us (0.950)
  waiting for transfers between devices: 162 us -> 150 us
  local copies, waits for them, and re-layouts: 52.7 us -> 44 us
    ppermute x20 -> x18, waiting for transfers between devices: 108 us -> 97.7 us  [the longest x8 65 us: spread_share(): moved_list.append((lax.ppermute(piece, ('row', 'col'), pairs), gets))]
    psum x1, waiting for transfers between devices: 53.6 us -> 45.8 us  [local(): diag_block = lax.psum(diag_part, 'col')]
    psum x1, waiting for transfers between devices: 0.02 us -> 6.07 us  [local(): normal_rows = lax.psum(partial_value, 'col')]
    another operation x21 -> x22, local copies, waits for them, and re-layouts: 15.5 us -> 11 us
    ppermute x20 -> x18, starting transfers between devices: 35 us -> 38.7 us  [the longest x10 27.6 us: gather_share(): recv.append(lax.ppermute(piece, ('row', 'col'), pairs))]
    unnamed x63 -> x60, local copies, waits for them, and re-layouts: 19.4 us -> 16.5 us
    another operation x3 -> x4, other arithmetic: 41.4 us -> 40.9 us  [local(): lax.linalg.triangular_solve(factor, jnp.eye(PANEL, dtype=jnp.float32), le...]
  transfers between devices with their start and end apart: 22 -> 20, of which waited for: 9 -> 11; matrix products, arithmetic and copies ran while one was open for 20% -> 30% of each run, Pallas kernels for 0% -> 0%
where the time goes in v3:
time: 420 us; the launch traced here: 415 us
  waiting for transfers between devices  150 us (36%)
  other arithmetic  132 us (31%)
  local copies, waits for them, and re-layouts  44 us (10%)
  starting transfers between devices  39 us (9%)
  matrix products  32.1 us (8%)
  between operations  18 us (4%)
    another operation x14, other arithmetic, local(): factor = jnp.linalg.cholesky(diag_block + jnp.diag(damping))  79 us
    ppermute x8, waiting for transfers between devices, spread_share(): moved_list.append((lax.ppermute(piece, ('row', 'col'), pairs), gets))  65 us
    psum x1, waiting for transfers between devices, local(): diag_block = lax.psum(diag_part, 'col')  45.8 us
    another operation x4, other arithmetic, local(): lax.linalg.triangular_solve(factor, jnp.eye(PANEL, dtype=jnp.float32), le...  40.9 us
    ppermute x10, waiting for transfers between devices, gather_share(): recv.append(lax.ppermute(piece, ('row', 'col'), pairs))  32.7 us
    ppermute x10, starting transfers between devices, gather_share(): recv.append(lax.ppermute(piece, ('row', 'col'), pairs))  27.6 us
    unnamed x60, local copies, waits for them, and re-layouts  16.5 us
    ppermute x8, starting transfers between devices, spread_share(): moved_list.append((lax.ppermute(piece, ('row', 'col'), pairs), gets))  11.1 us
  transfers between devices with their start and end apart: 20, of which 11 were waited for; matrix products, arithmetic and copies ran while one was open for 30% of the time, Pallas kernels for 0%

profile of v3, /device:TPU:52, one launch (start us, length us, event | category | flops | bytes accessed | tf_op | source)
XLA Modules:
  0.0 414.9 jit_solution(14036349153720519803)
XLA Ops:
  7.2 3.0 copy.61
  10.5 7.6 %gather_fusion = s32[2048,5]{1,0:T(8,128)} fusion(s32[1200,5]{1,0:T(8,128)S(1)} %bitcast.122, s32[2048]{0:T(1024)S(1)} %fusion.50), kind=kCustom, calls=%fused_computation | custom fusion | bytes 90112 | tf_op jit(solution)/shard_map/gather | solution.py:73
  18.2 1.5 copy.60
  20.0 1.5 copy-done
  22.8 1.8 broadcast_select_fusion.1
  24.6 1.3 collective-permute-start.1
  26.5 28.8 %collective-permute-done.1 = bf16[2048,128]{0,1:T(8,128)(2,1)S(1)} collective-permute-done((bf16[2048,128]{0,1:T(8,128)(2,1)S(1)}, bf16[2048,128]{0,1:T(8,128)(2,1)S(1)}, u32[]{:S(2)}, u32[]{:S(2)}) %collective-permute-start.1) | collective-permute-done | bytes 524320 | tf_op jit(solution)/shard_map/ppermute | solution.py:36
  56.0 1.3 collective-permute-start.2
  58.0 20.5 %collective-permute-done.2 = bf16[2048,128]{0,1:T(8,128)(2,1)S(1)} collective-permute-done((bf16[2048,128]{0,1:T(8,128)(2,1)S(1)}, bf16[2048,128]{0,1:T(8,128)(2,1)S(1)}, u32[]{:S(2)}, u32[]{:S(2)}) %collective-permute-start.2) | collective-permute-done | bytes 524320 | tf_op jit(solution)/shard_map/ppermute | solution.py:36
  79.2 1.3 collective-permute-start.3
  81.1 10.5 %collective-permute-done.3 = bf16[2048,128]{0,1:T(8,128)(2,1)S(1)} collective-permute-done((bf16[2048,128]{0,1:T(8,128)(2,1)S(1)}, bf16[2048,128]{0,1:T(8,128)(2,1)S(1)}, u32[]{:S(2)}, u32[]{:S(2)}) %collective-permute-start.3) | collective-permute-done | bytes 524320 | tf_op jit(solution)/shard_map/ppermute | solution.py:36
  92.5 1.8 collective-permute-start.6
  94.3 12.9 %collective-permute-done.5 = bf16[2048,128]{0,1:T(8,128)(2,1)S(1)} collective-permute-done((bf16[2048,128]{0,1:T(8,128)(2,1)S(1)}, bf16[2048,128]{0,1:T(8,128)(2,1)S(1)}, u32[]{:S(2)}, u32[]{:S(2)}) %collective-permute-start.5) | collective-permute-done | bytes 524320 | tf_op jit(solution)/shard_map/ppermute | solution.py:55
  107.2 10.3 %collective-permute-done.6 = bf16[2048,128]{0,1:T(8,128)(2,1)S(1)} collective-permute-done((bf16[2048,128]{0,1:T(8,128)(2,1)S(1)}, bf16[2048,128]{0,1:T(8,128)(2,1)S(1)}, u32[]{:S(2)}, u32[]{:S(2)}) %collective-permute-start.6) | collective-permute-done | bytes 524320 | tf_op jit(solution)/shard_map/ppermute | solution.py:55
  118.3 1.3 copy-done.7
  119.7 2.3 fusion.55
  125.6 1.1 fusion.17
  126.7 4.2 %fusion.56 = f32[640,512]{1,0:T(8,128)} fusion(bf16[2048,640]{0,1:T(8,128)(2,1)S(1)} %bitcast.123, bf16[2048,512]{0,1:T(8,128)(2,1)} %bitcast.125), kind=kOutput, calls=%fused_computation.133 | convolution fusion | flops 1342177280 | bytes 6029312 | tf_op jit(solution)/shard_map/dot_general | solution.py:90
  130.9 45.8 %all-reduce.4.cloned.1.call-done = f32[512,512]{0,1:T(8,128)} async-done(((f32[512,512]{0,1:T(8,128)}), f32[512,512]{0,1:T(8,128)}) %all-reduce.4.cloned.1.call-update) | async-done | bytes 1048592 | tf_op jit(solution)/shard_map/psum | solution.py:93
  176.7 1.4 select_add_fusion
  178.8 11.7 %cholesky.103 = f32[128,128]{1,0:T(8,128)S(1)} custom-call(f32[128,128]{1,0:T(8,128)S(1)} %cholesky.263), custom_call_target="Cholesky" | custom-call | tf_op jit(solution)/shard_map/jit(cholesky)/cholesky | solution.py:104
  190.5 9.8 %custom-call.30 = f32[1,128,128]{1,2,0:T(8,128)S(1)} custom-call(f32[1,128,128]{2,1,0:T(8,128)S(1)} %get-tuple-element.59), custom_call_target="InvertDiagBlocksLowerTriangular" | custom-call | tf_op jit(solution)/shard_map/jit(cholesky)/cholesky | solution.py:104
  201.0 12.2 %cholesky.215 = f32[128,128]{1,0:T(8,128)S(1)} custom-call(f32[128,128]{1,0:T(8,128)S(1)} %cholesky.267), custom_call_target="Cholesky" | custom-call | tf_op jit(solution)/shard_map/jit(cholesky)/cholesky | solution.py:104
  213.6 9.8 %custom-call.31 = f32[1,128,128]{1,2,0:T(8,128)S(1)} custom-call(f32[1,128,128]{2,1,0:T(8,128)S(1)} %get-tuple-element.57), custom_call_target="InvertDiagBlocksLowerTriangular" | custom-call | tf_op jit(solution)/shard_map/jit(cholesky)/cholesky | solution.py:104
  223.9 1.5 convolution_subtract_fusion.4
  225.4 11.7 %cholesky.236 = f32[128,128]{1,0:T(8,128)S(1)} custom-call(f32[128,128]{1,0:T(8,128)S(1)} %cholesky.272), custom_call_target="Cholesky" | custom-call | tf_op jit(solution)/shard_map/jit(cholesky)/cholesky | solution.py:104
  237.3 9.8 %custom-call.32 = f32[1,128,128]{1,2,0:T(8,128)S(1)} custom-call(f32[1,128,128]{2,1,0:T(8,128)S(1)} %get-tuple-element.55), custom_call_target="InvertDiagBlocksLowerTriangular" | custom-call | tf_op jit(solution)/shard_map/jit(cholesky)/cholesky | solution.py:104
  247.4 1.3 convolution_subtract_fusion.5
  248.7 11.9 %cholesky.253 = f32[128,128]{1,0:T(8,128)S(1)} custom-call(f32[128,128]{1,0:T(8,128)S(1)} %convolution_subtract_fusion.5), custom_call_target="Cholesky" | custom-call | tf_op jit(solution)/shard_map/jit(cholesky)/cholesky | solution.py:104
  261.3 6.1 %all-reduce.6.cloned.1.call-done = f32[640,512]{1,0:T(8,128)} async-done(((f32[640,512]{1,0:T(8,128)}), f32[640,512]{1,0:T(8,128)}) %all-reduce.6.cloned.1.call-update) | async-done | bytes 1310736 | tf_op jit(solution)/shard_map/psum | solution.py:95
  268.4 2.5 collective-permute-start.7
  274.8 1.7 broadcast_select_fusion.5
  276.5 1.3 collective-permute-start.10
  277.8 1.3 collective-permute-start.8
  279.1 1.3 collective-permute-start.9
  280.6 2.4 collective-permute-done.8
  283.0 2.8 collective-permute-done.9
  285.8 1.9 select_select_fusion.1
  287.7 12.8 %collective-permute-start.11 = (f32[128,512]{1,0:T(8,128)S(1)}, f32[128,512]{1,0:T(8,128)}, u32[]{:S(2)}, u32[]{:S(2)}) collective-permute-start(f32[128,512]{1,0:T(8,128)S(1)} %select_select_fusion.1), channel_id=1, source_target_pairs={{0,16},{1,17},{2,18},{3,19},{4,20},{5,21},{6,22},{7,23},{8,24},{9,... | collective-permute-start | bytes 786440 | tf_op jit(solution)/shard_map/ppermute | solution.py:55
  300.5 1.0 collective-permute-start.12
  301.5 2.6 collective-permute-start.13
  304.1 1.1 collective-permute-start.14
  305.2 3.2 collective-permute-start.15
  308.6 11.0 %while.1 = (s32[]{:T(128)}, f32[512,512]{0,1:T(8,128)S(1)}, s32[4,2]{0,1:T(2,128)S(1)}, f32[4,128,128]{2,1,0:T(8,128)}, s32[]{:T(128)}) while((s32[]{:T(128)}, f32[512,512]{0,1:T(8,128)S(1)}, s32[4,2]{0,1:T(2,128)S(1)}, f32[4,128,128]{2,1,0:T(8,128)}, s32[]{:T(128)}) %tuple.42), condition=%wide.while_cond, body=%wide.while_body.sunk | while | flops 2 | bytes 393829 | solution.py:107
  309.2 1.4 dynamic-slice.7
  312.0 1.4 dynamic-slice.7
  314.7 1.4 dynamic-slice.7
  317.4 1.4 dynamic-slice.7
  319.5 40.8 %custom-call.33 = f32[4,128,128]{1,2,0:T(8,128)} custom-call(f32[4,128,128]{2,1,0:T(8,128)} %get-tuple-element.21), custom_call_target="InvertDiagBlocksLowerTriangular" | custom-call | tf_op jit(solution)/shard_map/triangular_solve | solution.py:107
  360.3 1.2 fusion.32
  362.1 1.3 fusion.44
  363.4 1.0 convolution_subtract_fusion
  364.8 1.5 convolution_subtract_fusion.2
  366.9 1.7 collective-permute-start.16
  369.6 3.2 collective-permute-start.17
  373.8 1.0 bitcast_dynamic-update-slice_fusion.5
  374.8 1.0 bitcast_dynamic-update-slice_fusion.4
  376.7 3.9 collective-permute-done.16
  380.6 5.6 %collective-permute-done.17 = f32[128,512]{1,0:T(8,128)S(1)} collective-permute-done((f32[128,512]{1,0:T(8,128)S(1)}, f32[128,512]{1,0:T(8,128)S(1)}, u32[]{:S(2)}, u32[]{:S(2)}) %collective-permute-start.17) | collective-permute-done | bytes 262176 | tf_op jit(solution)/shard_map/ppermute | solution.py:55
  386.8 3.5 fusion
  390.3 2.7 fusion.57
  393.3 1.4 copy-done.5
  394.7 9.0 %copy_subtract_fusion = f32[5,128,8,128]{3,1,2,0:T(8,128)S(1)} fusion(f32[5,128,8,128]{3,2,1,0:T(8,128)S(1)} %copy-done.5, f32[8,128,512]{2,1,0:T(8,128)S(1)} %fusion, f32[5,128,512]{1,2,0:T(8,128)S(1)} %fusion.22, pred[5]{0:T(512)(128)(4,1)S(1)} %add_compare_fusion), kind=kOutput, calls=%fused_computation.3 | convolution fusion | flops 4027842560 | bytes 8650757 | tf_op jit(solution)/shard_map/dot_general | solution.py:133
  403.7 3.0 copy.83
  (151 shorter events, 27.7 us)
Async XLA Ops:
  7.2 3.1 copy-start.9
  7.2 3.3 copy-start.10
  7.2 169.5 %all-reduce.4.cloned.1.call-start = ((), (), s32[]{:S(2)}) async-start(), calls=%async_computation | async-start | bytes 2097152 | tf_op jit(solution)/shard_map/psum | solution.py:93
  10.5 9.2 %copy-start.11 = (s32[2048]{0:T(1024)S(1)}, s32[2048]{0:T(1024)}, u32[]{:S(2)}) copy-start(s32[2048]{0:T(1024)} %param.17) | copy-start | bytes 24580
  19.8 2.5 copy-start.20
  20.0 1.5 copy-start
  21.5 4.4 %copy-start.19 = (pred[256]{0:T(512)(128)(4,1)S(1)}, pred[256]{0:T(512)(128)(4,1)}, u32[]{:S(2)}) copy-start(pred[256]{0:T(512)(128)(4,1)} %constant.234.clone) | copy-start | bytes 772
  21.5 35.9 %copy-start.18 = (pred[256]{0:T(512)(128)(4,1)S(1)}, pred[256]{0:T(512)(128)(4,1)}, u32[]{:S(2)}) copy-start(pred[256]{0:T(512)(128)(4,1)} %constant.235.clone) | copy-start | bytes 772
  21.5 1.3 collective-permute-start
  22.8 57.7 %copy-start.17 = (pred[256]{0:T(512)(128)(4,1)S(1)}, pred[256]{0:T(512)(128)(4,1)}, u32[]{:S(2)}) copy-start(pred[256]{0:T(512)(128)(4,1)} %constant.236.clone) | copy-start | bytes 772
  24.6 30.7 %collective-permute-start.1 = (bf16[2048,128]{0,1:T(8,128)(2,1)S(1)}, bf16[2048,128]{0,1:T(8,128)(2,1)S(1)}, u32[]{:S(2)}, u32[]{:S(2)}) collective-permute-start(bf16[2048,128]{0,1:T(8,128)(2,1)S(1)} %broadcast_select_fusion.1), channel_id=1, source_target_pairs={{0,128},{1,129},{2,130},{3,131},{4,132},{5,133},{6,134},{7,135},{8... | collective-permute-start | bytes 1572872 | tf_op jit(solution)/shard_map/ppermute | solution.py:36
  56.0 22.5 %collective-permute-start.2 = (bf16[2048,128]{0,1:T(8,128)(2,1)S(1)}, bf16[2048,128]{0,1:T(8,128)(2,1)S(1)}, u32[]{:S(2)}, u32[]{:S(2)}) collective-permute-start(bf16[2048,128]{0,1:T(8,128)(2,1)S(1)} %broadcast_select_fusion.2), channel_id=1, source_target_pairs={{0,16},{1,17},{2,18},{3,19},{4,20},{5,21},{6,22},{7,23},{8,24},{9,... | collective-permute-start | bytes 1572872 | tf_op jit(solution)/shard_map/ppermute | solution.py:36
  79.2 12.4 %collective-permute-start.3 = (bf16[2048,128]{0,1:T(8,128)(2,1)S(1)}, bf16[2048,128]{0,1:T(8,128)(2,1)S(1)}, u32[]{:S(2)}, u32[]{:S(2)}) collective-permute-start(bf16[2048,128]{0,1:T(8,128)(2,1)S(1)} %broadcast_select_fusion.3), channel_id=1, source_target_pairs={{0,64},{1,65},{2,66},{3,67},{4,68},{5,69},{6,70},{7,71},{8,72},{9,... | collective-permute-start | bytes 1572872 | tf_op jit(solution)/shard_map/ppermute | solution.py:36
  92.3 2.0 collective-permute-start.4
  92.4 14.8 %collective-permute-start.5 = (bf16[2048,128]{0,1:T(8,128)(2,1)S(1)}, bf16[2048,128]{0,1:T(8,128)(2,1)S(1)}, u32[]{:S(2)}, u32[]{:S(2)}) collective-permute-start(bf16[2048,128]{0,1:T(8,128)(2,1)S(1)} %broadcast_select_fusion.4), channel_id=1, source_target_pairs={{0,8},{1,9},{2,10},{3,11},{4,12},{5,13},{6,14},{7,15},{8,0},{9,1},... | collective-permute-start | bytes 1572872 | tf_op jit(solution)/shard_map/ppermute | solution.py:55
  92.5 25.0 %collective-permute-start.6 = (bf16[2048,128]{0,1:T(8,128)(2,1)S(1)}, bf16[2048,128]{0,1:T(8,128)(2,1)S(1)}, u32[]{:S(2)}, u32[]{:S(2)}) collective-permute-start(bf16[2048,128]{0,1:T(8,128)(2,1)S(1)} %broadcast_select_fusion.4), channel_id=1, source_target_pairs={{0,12},{1,13},{2,14},{3,15},{4,8},{5,9},{6,10},{7,11},{8,4},{9,5},... | collective-permute-start | bytes 1572872 | tf_op jit(solution)/shard_map/ppermute | solution.py:55
  118.3 1.3 copy-start.7
  119.7 2.7 copy-start.16
  119.7 3.3 copy-start.15
  119.7 3.9 copy-start.14
  119.7 4.5 %copy-start.13 = (pred[256]{0:T(512)(128)(4,1)S(1)}, pred[256]{0:T(512)(128)(4,1)}, u32[]{:S(2)}) copy-start(pred[256]{0:T(512)(128)(4,1)} %constant.238.clone) | copy-start | bytes 772
  119.7 7.0 %copy-start.1 = (bf16[2048,5,128]{0,2,1:T(8,128)(2,1)S(1)}, bf16[2048,5,128]{0,2,1:T(8,128)(2,1)}, u32[]{:S(2)}) copy-start(bf16[2048,5,128]{0,2,1:T(8,128)(2,1)} %copy-done) | copy-start | bytes 7864324
  122.0 145.4 %all-reduce.6.cloned.1.call-start = ((), (), s32[]{:S(2)}) async-start(), calls=%async_computation.1 | async-start | bytes 2621440 | tf_op jit(solution)/shard_map/psum | solution.py:95
  126.7 50.0 %copy-start.12 = (f32[512]{0:T(512)S(1)}, f32[512]{0:T(512)}, u32[]{:S(2)}) copy-start(f32[512]{0:T(512)} %param.18) | copy-start | bytes 6148
  176.7 1.8 copy-start.2
  178.7 34.8 %copy-start.4 = (f32[512,512]{1,0:T(8,128)}, f32[512,512]{1,0:T(8,128)S(1)}, u32[]{:S(2)}) copy-start(f32[512,512]{1,0:T(8,128)S(1)} %fusion.10) | copy-start | bytes 3145732
  268.4 6.5 %collective-permute-start.7 = (f32[128,512]{1,0:T(8,128)S(1)}, f32[128,512]{1,0:T(8,128)S(1)}, u32[]{:S(2)}, u32[]{:S(2)}) collective-permute-start(f32[128,512]{1,0:T(8,128)S(1)} %slice.160), channel_id=1, source_target_pairs={{16,144},{21,149},{26,154},{31,159},{32,160},{37,165},{42,170},{47... | collective-permute-start | bytes 786440 | tf_op jit(solution)/shard_map/ppermute | solution.py:36
  276.5 4.1 collective-permute-start.10
  277.8 5.2 %collective-permute-start.8 = (f32[128,512]{1,0:T(8,128)S(1)}, f32[128,512]{1,0:T(8,128)S(1)}, u32[]{:S(2)}, u32[]{:S(2)}) collective-permute-start(f32[128,512]{1,0:T(8,128)S(1)} %broadcast_select_fusion.5), channel_id=1, source_target_pairs={{0,12},{5,9},{10,6},{15,3},{16,28},{21,25},{26,22},{31,19},{32,44}... | collective-permute-start | bytes 786440 | tf_op jit(solution)/shard_map/ppermute | solution.py:36
  279.1 6.7 %collective-permute-start.9 = (f32[128,512]{1,0:T(8,128)S(1)}, f32[128,512]{1,0:T(8,128)S(1)}, u32[]{:S(2)}, u32[]{:S(2)}) collective-permute-start(f32[128,512]{1,0:T(8,128)S(1)} %broadcast_select_fusion.5), channel_id=1, source_target_pairs={{0,8},{5,13},{10,2},{15,7},{16,24},{21,29},{26,18},{31,23},{32,40}... | collective-permute-start | bytes 786440 | tf_op jit(solution)/shard_map/ppermute | solution.py:36
  287.7 73.8 %copy-start.3 = (f32[512,512]{0,1:T(8,128)S(1)}, f32[512,512]{0,1:T(8,128)}, u32[]{:S(2)}) copy-start(f32[512,512]{0,1:T(8,128)} %fusion.17) | copy-start | bytes 3145732
  287.7 79.2 %collective-permute-start.11 = (f32[128,512]{1,0:T(8,128)S(1)}, f32[128,512]{1,0:T(8,128)}, u32[]{:S(2)}, u32[]{:S(2)}) collective-permute-start(f32[128,512]{1,0:T(8,128)S(1)} %select_select_fusion.1), channel_id=1, source_target_pairs={{0,16},{1,17},{2,18},{3,19},{4,20},{5,21},{6,22},{7,23},{8,24},{9,... | collective-permute-start | bytes 786440 | tf_op jit(solution)/shard_map/ppermute | solution.py:55
  300.5 69.1 %collective-permute-start.12 = (f32[128,512]{1,0:T(8,128)S(1)}, f32[128,512]{1,0:T(8,128)}, u32[]{:S(2)}, u32[]{:S(2)}) collective-permute-start(f32[128,512]{1,0:T(8,128)S(1)} %select_select_fusion.1), channel_id=1, source_target_pairs={{0,32},{1,33},{2,34},{3,35},{4,36},{5,37},{6,38},{7,39},{8,40},{9,... | collective-permute-start | bytes 786440 | tf_op jit(solution)/shard_map/ppermute | solution.py:55
  301.5 72.3 %collective-permute-start.13 = (f32[128,512]{1,0:T(8,128)S(1)}, f32[128,512]{1,0:T(8,128)}, u32[]{:S(2)}, u32[]{:S(2)}) collective-permute-start(f32[128,512]{1,0:T(8,128)S(1)} %select_select_fusion.1), channel_id=1, source_target_pairs={{0,48},{1,49},{2,50},{3,51},{4,52},{5,53},{6,54},{7,55},{8,56},{9,... | collective-permute-start | bytes 786440 | tf_op jit(solution)/shard_map/ppermute | solution.py:55
  304.1 70.6 %collective-permute-start.14 = (f32[128,512]{1,0:T(8,128)S(1)}, f32[128,512]{1,0:T(8,128)}, u32[]{:S(2)}, u32[]{:S(2)}) collective-permute-start(f32[128,512]{1,0:T(8,128)S(1)} %select_select_fusion.1), channel_id=1, source_target_pairs={{0,64},{1,65},{2,66},{3,67},{4,68},{5,69},{6,70},{7,71},{8,72},{9,... | collective-permute-start | bytes 786440 | tf_op jit(solution)/shard_map/ppermute | solution.py:55
  305.2 70.5 %collective-permute-start.15 = (f32[128,512]{1,0:T(8,128)S(1)}, f32[128,512]{1,0:T(8,128)}, u32[]{:S(2)}, u32[]{:S(2)}) collective-permute-start(f32[128,512]{1,0:T(8,128)S(1)} %select_select_fusion.1), channel_id=1, source_target_pairs={{0,80},{1,81},{2,82},{3,83},{4,84},{5,85},{6,86},{7,87},{8,88},{9,... | collective-permute-start | bytes 786440 | tf_op jit(solution)/shard_map/ppermute | solution.py:55
  360.3 4.1 copy-start.8
  366.9 13.7 %collective-permute-start.16 = (f32[128,512]{1,0:T(8,128)S(1)}, f32[128,512]{1,0:T(8,128)S(1)}, u32[]{:S(2)}, u32[]{:S(2)}) collective-permute-start(f32[128,512]{1,0:T(8,128)S(1)} %select_select_fusion.1), channel_id=1, source_target_pairs={{0,96},{1,97},{2,98},{3,99},{4,100},{5,101},{6,102},{7,103},{8,104... | collective-permute-start | bytes 786440 | tf_op jit(solution)/shard_map/ppermute | solution.py:55
  369.6 16.6 %collective-permute-start.17 = (f32[128,512]{1,0:T(8,128)S(1)}, f32[128,512]{1,0:T(8,128)S(1)}, u32[]{:S(2)}, u32[]{:S(2)}) collective-permute-start(f32[128,512]{1,0:T(8,128)S(1)} %select_select_fusion.1), channel_id=1, source_target_pairs={{0,112},{1,113},{2,114},{3,115},{4,116},{5,117},{6,118},{7,119},{8... | collective-permute-start | bytes 786440 | tf_op jit(solution)/shard_map/ppermute | solution.py:55
  386.8 3.5 copy-start.6
  393.0 1.7 copy-start.5
Sparse Core Ops, SparseCore 0:
  122.1 54.5 all-reduce.3
  213.7 53.6 all-reduce.5

commit v4 on v3

--- a/solution.py
+++ b/solution.py
@@ -23,10 +23,15 @@
     for round_masks in spread_rounds:
         gets_all = np.zeros_like(have)
         moved_list = []
-        for mask in span_of(round_masks)[1:]:
+        if isinstance(round_masks, list):
+            mask_sets = [round_masks]
+        else:
+            mask_sets = [[mask, mask] for mask in span_of(round_masks)[1:]]
+        for parity_masks in mask_sets:
             pairs = []
             gets = np.zeros_like(have)
             for r in range(row_count):
+                mask = parity_masks[r % 2]
                 for c in range(col_count):
                     if have[r, c] and not have[r ^ mask, c]:
                         pairs.append((r * col_count + c, (r ^ mask) * col_count + c))
@@ -78,19 +83,34 @@
     panel_holds = np.zeros((row_count, col_count), dtype=bool)
     panel_holds[:panel_tiles, :] = True
     panel_piece = spread_share(
-        masked[:, 0, :], panel_holds, ((8,), (32,), (4,), (16,)), row_count, col_count
+        masked[:, 0, :], panel_holds, [[8, 32], [32, 8], [4, 16], [16, 4]], row_count, col_count
     )
-    panel_stack = gather_share(panel_piece, (1, 2), row_count, col_count)
-    panel_cols = jnp.transpose(panel_stack, (1, 0, 2)).reshape(kq_rows, PANEL)
+    panel_pair = gather_share(panel_piece, (2,), row_count, col_count)
+    panel_stack = gather_share(panel_pair, (1,), row_count, col_count)
+    panel_cols = jnp.transpose(panel_stack, (2, 1, 0, 3)).reshape(kq_rows, PANEL)
 
     contract_rows = (((0,), (0,)), ((), ()))
+    half = PANEL // 2
+    core_bit = row_pos % 2
     diag_part = lax.dot_general(
-        panel_cols, panel_cols, contract_rows, preferred_element_type=jnp.float32
+        lax.dynamic_slice_in_dim(panel_cols, core_bit * half, half, 1),
+        panel_cols, contract_rows, preferred_element_type=jnp.float32,
     )
     partial_value = lax.dot_general(
         flat_green, panel_cols, contract_rows, preferred_element_type=jnp.float32
     )
-    diag_block = lax.psum(diag_part, "col")
+    diag_half = lax.psum(diag_part, "col")
+    swap_pairs = [
+        (r * col_count + c, (r ^ 1) * col_count + c)
+        for r in range(row_count)
+        for c in range(col_count)
+    ]
+    other_half = lax.ppermute(diag_half, ("row", "col"), swap_pairs)
+    diag_block = jnp.where(
+        core_bit == 0,
+        jnp.concatenate([diag_half, other_half]),
+        jnp.concatenate([other_half, diag_half]),
+    )
     diag_block, partial_value = lax.optimization_barrier((diag_block, partial_value))
     normal_rows = lax.psum(partial_value, "col")
 
@@ -99,7 +119,7 @@
         for c in range(col_count):
             far_holds[panel_tiles + slot_no * col_count + c, c] = True
     far_piece = spread_share(
-        normal_rows[:tile_width], far_holds, ((32,), (1, 2)), row_count, col_count
+        normal_rows[:tile_width], far_holds, ((32,), (2,), (1,)), row_count, col_count
     )
     factor = jnp.linalg.cholesky(diag_block + jnp.diag(damping))
     factor, far_piece = lax.optimization_barrier((factor, far_piece))

time: 420 us -> 391 us (0.931)
  the two profiles are of different devices: /device:TPU:52 before, /device:TPU:1 now
where the time goes in v4:
time: 391 us; the launch traced here: 385 us
  other arithmetic  132 us (34%)
  waiting for transfers between devices  111 us (28%)
  starting transfers between devices  49.6 us (13%)
  local copies, waits for them, and re-layouts  43.2 us (11%)
  matrix products  31.4 us (8%)
  between operations  17.8 us (5%)
    another operation x14, other arithmetic, local(): factor = jnp.linalg.cholesky(diag_block + jnp.diag(damping))  78.6 us
    psum x1, waiting for transfers between devices, local(): diag_half = lax.psum(diag_part, 'col')  49.1 us
    another operation x4, other arithmetic, local(): lax.linalg.triangular_solve(factor, jnp.eye(PANEL, dtype=jnp.float32), le...  40.9 us
    ppermute x9, starting transfers between devices, gather_share(): recv.append(lax.ppermute(piece, ('row', 'col'), pairs))  34.2 us
    ppermute x7, waiting for transfers between devices, spread_share(): moved_list.append((lax.ppermute(piece, ('row', 'col'), pairs), gets))  34 us
    ppermute x9, waiting for transfers between devices, gather_share(): recv.append(lax.ppermute(piece, ('row', 'col'), pairs))  27.4 us
    unnamed x58, local copies, waits for them, and re-layouts  16.5 us
    ppermute x7, starting transfers between devices, spread_share(): moved_list.append((lax.ppermute(piece, ('row', 'col'), pairs), gets))  12.7 us
  transfers between devices with their start and end apart: 19, of which 10 were waited for; matrix products, arithmetic and copies ran while one was open for 41% of the time, Pallas kernels for 0%

profile of v4, /device:TPU:1, one launch (start us, length us, event | category | flops | bytes accessed | tf_op | source)
XLA Modules:
  0.0 384.8 jit_solution(14477227560024338241)
XLA Ops:
  7.2 3.0 copy.61
  10.5 7.6 %gather_fusion = s32[2048,5]{1,0:T(8,128)} fusion(s32[1200,5]{1,0:T(8,128)S(1)} %bitcast.123, s32[2048]{0:T(1024)S(1)} %fusion.56), kind=kCustom, calls=%fused_computation | custom fusion | bytes 90112 | tf_op jit(solution)/shard_map/gather | solution.py:78
  18.2 1.5 copy.60
  20.0 1.5 copy-done
  21.5 5.7 %collective-permute-start = (bf16[2048,128]{0,1:T(8,128)(2,1)S(1)}, bf16[2048,128]{0,1:T(8,128)(2,1)S(1)}, u32[]{:S(2)}, u32[]{:S(2)}) collective-permute-start(bf16[2048,128]{0,1:T(8,128)(2,1)S(1)} %slice_bitcast_fusion), channel_id=1, source_target_pairs={{0,32},{1,33},{2,34},{3,35},{4,132},{5,133},{6,134},{7,135},{8,40}... | collective-permute-start | bytes 1572872 | tf_op jit(solution)/shard_map/ppermute | solution.py:41
  27.8 5.5 %collective-permute-done = bf16[2048,128]{0,1:T(8,128)(2,1)S(1)} collective-permute-done((bf16[2048,128]{0,1:T(8,128)(2,1)S(1)}, bf16[2048,128]{0,1:T(8,128)(2,1)S(1)}, u32[]{:S(2)}, u32[]{:S(2)}) %collective-permute-start) | collective-permute-done | bytes 524320 | tf_op jit(solution)/shard_map/ppermute | solution.py:41
  33.3 1.8 broadcast_select_fusion.1
  35.1 1.3 collective-permute-start.1
  37.0 7.1 %collective-permute-done.1 = bf16[2048,128]{0,1:T(8,128)(2,1)S(1)} collective-permute-done((bf16[2048,128]{0,1:T(8,128)(2,1)S(1)}, bf16[2048,128]{0,1:T(8,128)(2,1)S(1)}, u32[]{:S(2)}, u32[]{:S(2)}) %collective-permute-start.1) | collective-permute-done | bytes 524320 | tf_op jit(solution)/shard_map/ppermute | solution.py:41
  44.7 1.3 collective-permute-start.2
  46.7 8.6 %collective-permute-done.2 = bf16[2048,128]{0,1:T(8,128)(2,1)S(1)} collective-permute-done((bf16[2048,128]{0,1:T(8,128)(2,1)S(1)}, bf16[2048,128]{0,1:T(8,128)(2,1)S(1)}, u32[]{:S(2)}, u32[]{:S(2)}) %collective-permute-start.2) | collective-permute-done | bytes 524320 | tf_op jit(solution)/shard_map/ppermute | solution.py:41
  56.0 1.3 collective-permute-start.3
  57.9 9.2 %collective-permute-done.3 = bf16[2048,128]{0,1:T(8,128)(2,1)S(1)} collective-permute-done((bf16[2048,128]{0,1:T(8,128)(2,1)S(1)}, bf16[2048,128]{0,1:T(8,128)(2,1)S(1)}, u32[]{:S(2)}, u32[]{:S(2)}) %collective-permute-start.3) | collective-permute-done | bytes 524320 | tf_op jit(solution)/shard_map/ppermute | solution.py:41
  67.8 10.2 %collective-permute-start.4 = (bf16[2048,128]{0,1:T(8,128)(2,1)S(1)}, bf16[2048,128]{0,1:T(8,128)(2,1)S(1)}, u32[]{:S(2)}, u32[]{:S(2)}) collective-permute-start(bf16[2048,128]{0,1:T(8,128)(2,1)S(1)} %broadcast_select_fusion.4), channel_id=1, source_target_pairs={{0,8},{1,9},{2,10},{3,11},{4,12},{5,13},{6,14},{7,15},{8,0},{9,1},... | collective-permute-start | bytes 1572872 | tf_op jit(solution)/shard_map/ppermute | solution.py:60
  78.0 6.6 %collective-permute-done.4 = bf16[2048,128]{0,1:T(8,128)(2,1)S(1)} collective-permute-done((bf16[2048,128]{0,1:T(8,128)(2,1)S(1)}, bf16[2048,128]{0,1:T(8,128)(2,1)S(1)}, u32[]{:S(2)}, u32[]{:S(2)}) %collective-permute-start.4) | collective-permute-done | bytes 524320 | tf_op jit(solution)/shard_map/ppermute | solution.py:60
  85.1 7.6 %collective-permute-start.5 = (bf16[2,2048,128]{1,2,0:T(8,128)(2,1)S(1)}, bf16[2,2048,128]{1,2,0:T(8,128)(2,1)S(1)}, u32[]{:S(2)}, u32[]{:S(2)}) collective-permute-start(bf16[2,2048,128]{1,2,0:T(8,128)(2,1)S(1)} %get-tuple-element.52), channel_id=1, source_target_pairs={{0,4},{1,5},{2,6},{3,7},{4,0},{5,1},{6,2},{7,3},{8,12},{9,13},{10,... | collective-permute-start | bytes 3145736 | tf_op jit(solution)/shard_map/ppermute | solution.py:60
  92.8 2.3 collective-permute-done.5
  96.0 1.3 copy-done.6
  97.3 1.5 fusion.13
  101.7 1.1 fusion.21
  102.8 49.1 %all-reduce.4.cloned.1.call-done = f32[256,512]{0,1:T(8,128)} async-done(((f32[256,512]{0,1:T(8,128)}), f32[256,512]{0,1:T(8,128)}) %all-reduce.4.cloned.1.call-update) | async-done | bytes 524304 | tf_op jit(solution)/shard_map/psum | solution.py:102
  151.9 2.6 collective-permute-start.6
  154.5 4.3 %fusion.63 = f32[640,512]{1,0:T(8,128)} fusion(bf16[2048,640]{0,1:T(8,128)(2,1)S(1)} %bitcast.124, bf16[2048,512]{0,1:T(8,128)(2,1)} %bitcast.126), kind=kOutput, calls=%fused_computation.146 | convolution fusion | flops 1342177280 | bytes 6029312 | tf_op jit(solution)/shard_map/dot_general | solution.py:99
  158.8 1.4 maximum_select_fusion
  161.0 11.7 %cholesky.103 = f32[128,128]{1,0:T(8,128)S(1)} custom-call(f32[128,128]{1,0:T(8,128)S(1)} %cholesky.263), custom_call_target="Cholesky" | custom-call | tf_op jit(solution)/shard_map/jit(cholesky)/cholesky | solution.py:124
  172.7 9.8 %custom-call.30 = f32[1,128,128]{1,2,0:T(8,128)S(1)} custom-call(f32[1,128,128]{2,1,0:T(8,128)S(1)} %get-tuple-element.61), custom_call_target="InvertDiagBlocksLowerTriangular" | custom-call | tf_op jit(solution)/shard_map/jit(cholesky)/cholesky | solution.py:124
  183.4 11.9 %cholesky.215 = f32[128,128]{1,0:T(8,128)S(1)} custom-call(f32[128,128]{1,0:T(8,128)S(1)} %cholesky.267), custom_call_target="Cholesky" | custom-call | tf_op jit(solution)/shard_map/jit(cholesky)/cholesky | solution.py:124
  195.5 9.8 %custom-call.31 = f32[1,128,128]{1,2,0:T(8,128)S(1)} custom-call(f32[1,128,128]{2,1,0:T(8,128)S(1)} %get-tuple-element.59), custom_call_target="InvertDiagBlocksLowerTriangular" | custom-call | tf_op jit(solution)/shard_map/jit(cholesky)/cholesky | solution.py:124
  205.8 1.5 convolution_subtract_fusion.4
  207.3 11.7 %cholesky.236 = f32[128,128]{1,0:T(8,128)S(1)} custom-call(f32[128,128]{1,0:T(8,128)S(1)} %cholesky.272), custom_call_target="Cholesky" | custom-call | tf_op jit(solution)/shard_map/jit(cholesky)/cholesky | solution.py:124
  219.2 9.8 %custom-call.32 = f32[1,128,128]{1,2,0:T(8,128)S(1)} custom-call(f32[1,128,128]{2,1,0:T(8,128)S(1)} %get-tuple-element.57), custom_call_target="InvertDiagBlocksLowerTriangular" | custom-call | tf_op jit(solution)/shard_map/jit(cholesky)/cholesky | solution.py:124
  229.3 1.0 slice.160
  230.3 1.1 collective-permute-start.7
  231.4 1.3 convolution_subtract_fusion.5
  232.7 11.7 %cholesky.253 = f32[128,128]{1,0:T(8,128)S(1)} custom-call(f32[128,128]{1,0:T(8,128)S(1)} %convolution_subtract_fusion.5), custom_call_target="Cholesky" | custom-call | tf_op jit(solution)/shard_map/jit(cholesky)/cholesky | solution.py:124
  245.2 1.5 broadcast_select_fusion.5
  252.1 1.3 collective-permute-start.9
  253.5 3.7 collective-permute-done.9
  258.0 4.4 %collective-permute-start.10 = (f32[128,512]{1,0:T(8,128)S(1)}, f32[128,512]{1,0:T(8,128)}, u32[]{:S(2)}, u32[]{:S(2)}) collective-permute-start(f32[128,512]{1,0:T(8,128)S(1)} %broadcast_select_fusion.7), channel_id=1, source_target_pairs={{0,16},{1,17},{2,18},{3,19},{4,20},{5,21},{6,22},{7,23},{8,24},{9,... | collective-permute-start | bytes 786440 | tf_op jit(solution)/shard_map/ppermute | solution.py:60
  262.4 3.7 collective-permute-start.11
  266.4 3.0 collective-permute-start.14
  269.5 11.0 %while.1 = (s32[]{:T(128)}, f32[512,512]{0,1:T(8,128)S(1)}, s32[4,2]{0,1:T(2,128)S(1)}, f32[4,128,128]{2,1,0:T(8,128)}, s32[]{:T(128)}) while((s32[]{:T(128)}, f32[512,512]{0,1:T(8,128)S(1)}, s32[4,2]{0,1:T(2,128)S(1)}, f32[4,128,128]{2,1,0:T(8,128)}, s32[]{:T(128)}) %tuple.42), condition=%wide.while_cond, body=%wide.while_body.sunk | while | flops 2 | bytes 393829 | solution.py:127
  270.2 1.4 dynamic-slice.7
  272.9 1.4 dynamic-slice.7
  275.7 1.4 dynamic-slice.7
  278.4 1.4 dynamic-slice.7
  280.5 40.8 %custom-call.33 = f32[4,128,128]{1,2,0:T(8,128)} custom-call(f32[4,128,128]{2,1,0:T(8,128)} %get-tuple-element.21), custom_call_target="InvertDiagBlocksLowerTriangular" | custom-call | tf_op jit(solution)/shard_map/triangular_solve | solution.py:127
  321.3 1.2 fusion.38
  323.1 1.3 fusion.50
  324.4 1.0 convolution_subtract_fusion
  325.8 1.5 convolution_subtract_fusion.2
  327.9 3.8 collective-permute-start.15
  331.6 1.0 bitcast_dynamic-update-slice_fusion.7
  332.6 1.2 collective-permute-start.16
  334.8 1.0 bitcast_dynamic-update-slice_fusion.5
  335.7 1.0 bitcast_dynamic-update-slice_fusion.4
  336.7 1.0 bitcast_dynamic-update-slice_fusion.3
  337.7 3.2 collective-permute-done.15
  340.9 15.4 %collective-permute-done.16 = f32[128,512]{1,0:T(8,128)S(1)} collective-permute-done((f32[128,512]{1,0:T(8,128)S(1)}, f32[128,512]{1,0:T(8,128)S(1)}, u32[]{:S(2)}, u32[]{:S(2)}) %collective-permute-start.16) | collective-permute-done | bytes 262176 | tf_op jit(solution)/shard_map/ppermute | solution.py:60
  356.8 3.5 fusion
  360.3 2.7 fusion.64
  363.3 1.4 copy-done.4
  364.8 9.0 %copy_subtract_fusion = f32[5,128,8,128]{3,1,2,0:T(8,128)S(1)} fusion(f32[5,128,8,128]{3,2,1,0:T(8,128)S(1)} %copy-done.4, f32[8,128,512]{2,1,0:T(8,128)S(1)} %fusion, f32[5,128,512]{1,2,0:T(8,128)S(1)} %fusion.28, pred[5]{0:T(512)(128)(4,1)S(1)} %add_compare_fusion), kind=kOutput, calls=%fused_computation.3 | convolution fusion | flops 4027842560 | bytes 8650757 | tf_op jit(solution)/shard_map/dot_general | solution.py:153
  373.7 3.0 copy.84
  (149 shorter events, 26.4 us)
Async XLA Ops:
  7.2 3.1 copy-start.9
  7.2 3.3 copy-start.10
  7.2 144.7 %all-reduce.4.cloned.1.call-start = ((), (), s32[]{:S(2)}) async-start(), calls=%async_computation | async-start | bytes 1048576 | tf_op jit(solution)/shard_map/psum | solution.py:102
  10.5 9.2 %copy-start.11 = (s32[2048]{0:T(1024)S(1)}, s32[2048]{0:T(1024)}, u32[]{:S(2)}) copy-start(s32[2048]{0:T(1024)} %param.16) | copy-start | bytes 24580
  19.8 7.5 %copy-start.19 = (pred[256]{0:T(512)(128)(4,1)S(1)}, pred[256]{0:T(512)(128)(4,1)}, u32[]{:S(2)}) copy-start(pred[256]{0:T(512)(128)(4,1)} %constant.244.clone) | copy-start | bytes 772
  20.0 1.5 copy-start
  21.5 14.9 %copy-start.18 = (pred[256]{0:T(512)(128)(4,1)S(1)}, pred[256]{0:T(512)(128)(4,1)}, u32[]{:S(2)}) copy-start(pred[256]{0:T(512)(128)(4,1)} %constant.245.clone) | copy-start | bytes 772
  21.5 24.6 %copy-start.17 = (pred[256]{0:T(512)(128)(4,1)S(1)}, pred[256]{0:T(512)(128)(4,1)}, u32[]{:S(2)}) copy-start(pred[256]{0:T(512)(128)(4,1)} %constant.246.clone) | copy-start | bytes 772
  21.5 11.8 %collective-permute-start = (bf16[2048,128]{0,1:T(8,128)(2,1)S(1)}, bf16[2048,128]{0,1:T(8,128)(2,1)S(1)}, u32[]{:S(2)}, u32[]{:S(2)}) collective-permute-start(bf16[2048,128]{0,1:T(8,128)(2,1)S(1)} %slice_bitcast_fusion), channel_id=1, source_target_pairs={{0,32},{1,33},{2,34},{3,35},{4,132},{5,133},{6,134},{7,135},{8,40}... | collective-permute-start | bytes 1572872 | tf_op jit(solution)/shard_map/ppermute | solution.py:41
  33.3 24.0 %copy-start.16 = (pred[256]{0:T(512)(128)(4,1)S(1)}, pred[256]{0:T(512)(128)(4,1)}, u32[]{:S(2)}) copy-start(pred[256]{0:T(512)(128)(4,1)} %constant.247.clone) | copy-start | bytes 772
  35.1 9.0 %collective-permute-start.1 = (bf16[2048,128]{0,1:T(8,128)(2,1)S(1)}, bf16[2048,128]{0,1:T(8,128)(2,1)S(1)}, u32[]{:S(2)}, u32[]{:S(2)}) collective-permute-start(bf16[2048,128]{0,1:T(8,128)(2,1)S(1)} %broadcast_select_fusion.1), channel_id=1, source_target_pairs={{0,128},{1,129},{2,130},{3,131},{4,36},{5,37},{6,38},{7,39},{8,136... | collective-permute-start | bytes 1572872 | tf_op jit(solution)/shard_map/ppermute | solution.py:41
  44.7 10.5 %collective-permute-start.2 = (bf16[2048,128]{0,1:T(8,128)(2,1)S(1)}, bf16[2048,128]{0,1:T(8,128)(2,1)S(1)}, u32[]{:S(2)}, u32[]{:S(2)}) collective-permute-start(bf16[2048,128]{0,1:T(8,128)(2,1)S(1)} %broadcast_select_fusion.2), channel_id=1, source_target_pairs={{0,16},{1,17},{2,18},{3,19},{4,68},{5,69},{6,70},{7,71},{8,24},{9,... | collective-permute-start | bytes 1572872 | tf_op jit(solution)/shard_map/ppermute | solution.py:41
  56.0 11.1 %collective-permute-start.3 = (bf16[2048,128]{0,1:T(8,128)(2,1)S(1)}, bf16[2048,128]{0,1:T(8,128)(2,1)S(1)}, u32[]{:S(2)}, u32[]{:S(2)}) collective-permute-start(bf16[2048,128]{0,1:T(8,128)(2,1)S(1)} %broadcast_select_fusion.3), channel_id=1, source_target_pairs={{0,64},{1,65},{2,66},{3,67},{4,20},{5,21},{6,22},{7,23},{8,72},{9,... | collective-permute-start | bytes 1572872 | tf_op jit(solution)/shard_map/ppermute | solution.py:41
  67.8 16.8 %collective-permute-start.4 = (bf16[2048,128]{0,1:T(8,128)(2,1)S(1)}, bf16[2048,128]{0,1:T(8,128)(2,1)S(1)}, u32[]{:S(2)}, u32[]{:S(2)}) collective-permute-start(bf16[2048,128]{0,1:T(8,128)(2,1)S(1)} %broadcast_select_fusion.4), channel_id=1, source_target_pairs={{0,8},{1,9},{2,10},{3,11},{4,12},{5,13},{6,14},{7,15},{8,0},{9,1},... | collective-permute-start | bytes 1572872 | tf_op jit(solution)/shard_map/ppermute | solution.py:60
  85.1 9.9 %collective-permute-start.5 = (bf16[2,2048,128]{1,2,0:T(8,128)(2,1)S(1)}, bf16[2,2048,128]{1,2,0:T(8,128)(2,1)S(1)}, u32[]{:S(2)}, u32[]{:S(2)}) collective-permute-start(bf16[2,2048,128]{1,2,0:T(8,128)(2,1)S(1)} %get-tuple-element.52), channel_id=1, source_target_pairs={{0,4},{1,5},{2,6},{3,7},{4,0},{5,1},{6,2},{7,3},{8,12},{9,13},{10,... | collective-permute-start | bytes 3145736 | tf_op jit(solution)/shard_map/ppermute | solution.py:60
  96.0 1.3 copy-start.6
  97.3 1.7 copy-start.15
  97.3 2.3 copy-start.14
  97.3 2.9 copy-start.13
  97.3 57.2 %copy-start.1 = (bf16[2048,5,128]{0,2,1:T(8,128)(2,1)S(1)}, bf16[2048,5,128]{0,2,1:T(8,128)(2,1)}, u32[]{:S(2)}) copy-start(bf16[2048,5,128]{0,2,1:T(8,128)(2,1)} %copy-done) | copy-start | bytes 7864324
  98.9 130.4 %all-reduce.6.cloned.1.call-start = ((), (), s32[]{:S(2)}) async-start(), calls=%async_computation.1 | async-start | bytes 2621440 | tf_op jit(solution)/shard_map/psum | solution.py:115
  151.9 6.9 %collective-permute-start.6 = (f32[256,512]{0,1:T(8,128)}, f32[256,512]{0,1:T(8,128)}, u32[]{:S(2)}, u32[]{:S(2)}) collective-permute-start(f32[256,512]{0,1:T(8,128)} %all-reduce.4.cloned.1.call-done), channel_id=1, source_target_pairs={{0,4},{1,5},{2,6},{3,7},{4,0},{5,1},{6,2},{7,3},{8,12},{9,13},{10,... | collective-permute-start | bytes 1572872 | tf_op jit(solution)/shard_map/ppermute | solution.py:108
  154.5 4.3 %copy-start.7 = (f32[256,512]{0,1:T(8,128)S(1)}, f32[256,512]{0,1:T(8,128)}, u32[]{:S(2)}) copy-start(f32[256,512]{0,1:T(8,128)} %all-reduce.4.cloned.1.call-done) | copy-start | bytes 1572868
  158.8 1.4 copy-start.12
  160.9 34.5 %copy-start.3 = (f32[512,512]{1,0:T(8,128)}, f32[512,512]{1,0:T(8,128)S(1)}, u32[]{:S(2)}) copy-start(f32[512,512]{1,0:T(8,128)S(1)} %fusion.12) | copy-start | bytes 3145732
  230.3 14.9 %collective-permute-start.7 = (f32[128,512]{1,0:T(8,128)S(1)}, f32[128,512]{1,0:T(8,128)S(1)}, u32[]{:S(2)}, u32[]{:S(2)}) collective-permute-start(f32[128,512]{1,0:T(8,128)S(1)} %slice.160), channel_id=1, source_target_pairs={{16,144},{21,149},{26,154},{31,159},{32,160},{37,165},{42,170},{47... | collective-permute-start | bytes 786440 | tf_op jit(solution)/shard_map/ppermute | solution.py:41
  246.7 4.7 %collective-permute-start.8 = (f32[128,512]{1,0:T(8,128)S(1)}, f32[128,512]{1,0:T(8,128)S(1)}, u32[]{:S(2)}, u32[]{:S(2)}) collective-permute-start(f32[128,512]{1,0:T(8,128)S(1)} %broadcast_select_fusion.5), channel_id=1, source_target_pairs={{0,8},{5,13},{10,2},{15,7},{16,24},{21,29},{26,18},{31,23},{32,40}... | collective-permute-start | bytes 786440 | tf_op jit(solution)/shard_map/ppermute | solution.py:41
  252.1 5.1 %collective-permute-start.9 = (f32[128,512]{1,0:T(8,128)S(1)}, f32[128,512]{1,0:T(8,128)S(1)}, u32[]{:S(2)}, u32[]{:S(2)}) collective-permute-start(f32[128,512]{1,0:T(8,128)S(1)} %broadcast_select_fusion.6), channel_id=1, source_target_pairs={{0,4},{2,6},{5,1},{7,3},{8,12},{10,14},{13,9},{15,11},{16,20},{18,... | collective-permute-start | bytes 786440 | tf_op jit(solution)/shard_map/ppermute | solution.py:41
  258.0 64.5 %copy-start.2 = (f32[512,512]{0,1:T(8,128)S(1)}, f32[512,512]{0,1:T(8,128)}, u32[]{:S(2)}) copy-start(f32[512,512]{0,1:T(8,128)} %fusion.21) | copy-start | bytes 3145732
  258.0 69.9 %collective-permute-start.10 = (f32[128,512]{1,0:T(8,128)S(1)}, f32[128,512]{1,0:T(8,128)}, u32[]{:S(2)}, u32[]{:S(2)}) collective-permute-start(f32[128,512]{1,0:T(8,128)S(1)} %broadcast_select_fusion.7), channel_id=1, source_target_pairs={{0,16},{1,17},{2,18},{3,19},{4,20},{5,21},{6,22},{7,23},{8,24},{9,... | collective-permute-start | bytes 786440 | tf_op jit(solution)/shard_map/ppermute | solution.py:60
  262.4 70.2 %collective-permute-start.11 = (f32[128,512]{1,0:T(8,128)S(1)}, f32[128,512]{1,0:T(8,128)}, u32[]{:S(2)}, u32[]{:S(2)}) collective-permute-start(f32[128,512]{1,0:T(8,128)S(1)} %broadcast_select_fusion.7), channel_id=1, source_target_pairs={{0,32},{1,33},{2,34},{3,35},{4,36},{5,37},{6,38},{7,39},{8,40},{9,... | collective-permute-start | bytes 786440 | tf_op jit(solution)/shard_map/ppermute | solution.py:60
  266.1 68.7 %collective-permute-start.12 = (f32[128,512]{1,0:T(8,128)S(1)}, f32[128,512]{1,0:T(8,128)}, u32[]{:S(2)}, u32[]{:S(2)}) collective-permute-start(f32[128,512]{1,0:T(8,128)S(1)} %broadcast_select_fusion.7), channel_id=1, source_target_pairs={{0,48},{1,49},{2,50},{3,51},{4,52},{5,53},{6,54},{7,55},{8,56},{9,... | collective-permute-start | bytes 786440 | tf_op jit(solution)/shard_map/ppermute | solution.py:60
  266.1 69.7 %collective-permute-start.13 = (f32[128,512]{1,0:T(8,128)S(1)}, f32[128,512]{1,0:T(8,128)}, u32[]{:S(2)}, u32[]{:S(2)}) collective-permute-start(f32[128,512]{1,0:T(8,128)S(1)} %broadcast_select_fusion.7), channel_id=1, source_target_pairs={{0,64},{1,65},{2,66},{3,67},{4,68},{5,69},{6,70},{7,71},{8,72},{9,... | collective-permute-start | bytes 786440 | tf_op jit(solution)/shard_map/ppermute | solution.py:60
  266.4 70.3 %collective-permute-start.14 = (f32[128,512]{1,0:T(8,128)S(1)}, f32[128,512]{1,0:T(8,128)}, u32[]{:S(2)}, u32[]{:S(2)}) collective-permute-start(f32[128,512]{1,0:T(8,128)S(1)} %broadcast_select_fusion.7), channel_id=1, source_target_pairs={{0,80},{1,81},{2,82},{3,83},{4,84},{5,85},{6,86},{7,87},{8,88},{9,... | collective-permute-start | bytes 786440 | tf_op jit(solution)/shard_map/ppermute | solution.py:60
  321.3 4.1 %copy-start.8 = (f32[4,128,128]{1,2,0:T(8,128)S(1)}, f32[4,128,128]{1,2,0:T(8,128)}, u32[]{:S(2)}) copy-start(f32[4,128,128]{1,2,0:T(8,128)} %custom-call.33) | copy-start | bytes 786436
  327.9 13.0 %collective-permute-start.15 = (f32[128,512]{1,0:T(8,128)S(1)}, f32[128,512]{1,0:T(8,128)S(1)}, u32[]{:S(2)}, u32[]{:S(2)}) collective-permute-start(f32[128,512]{1,0:T(8,128)S(1)} %broadcast_select_fusion.7), channel_id=1, source_target_pairs={{0,96},{1,97},{2,98},{3,99},{4,100},{5,101},{6,102},{7,103},{8,104... | collective-permute-start | bytes 786440 | tf_op jit(solution)/shard_map/ppermute | solution.py:60
  332.6 23.7 %collective-permute-start.16 = (f32[128,512]{1,0:T(8,128)S(1)}, f32[128,512]{1,0:T(8,128)S(1)}, u32[]{:S(2)}, u32[]{:S(2)}) collective-permute-start(f32[128,512]{1,0:T(8,128)S(1)} %broadcast_select_fusion.7), channel_id=1, source_target_pairs={{0,112},{1,113},{2,114},{3,115},{4,116},{5,117},{6,118},{7,119},{8... | collective-permute-start | bytes 786440 | tf_op jit(solution)/shard_map/ppermute | solution.py:60
  356.8 3.5 copy-start.5
  363.0 1.7 copy-start.4
Sparse Core Ops, SparseCore 0:
  99.0 52.7 all-reduce.3
  160.4 52.5 all-reduce.5

commit v5 on v4

--- a/solution.py
+++ b/solution.py
@@ -99,7 +99,16 @@
     partial_value = lax.dot_general(
         flat_green, panel_cols, contract_rows, preferred_element_type=jnp.float32
     )
-    diag_half = lax.psum(diag_part, "col")
+    diag_half = diag_part
+    col_mask = 1
+    while col_mask < col_count:
+        col_pairs = [
+            (r * col_count + c, r * col_count + (c ^ col_mask))
+            for r in range(row_count)
+            for c in range(col_count)
+        ]
+        diag_half = diag_half + lax.ppermute(diag_half, ("row", "col"), col_pairs)
+        col_mask *= 2
     swap_pairs = [
         (r * col_count + c, (r ^ 1) * col_count + c)
         for r in range(row_count)

time: 391 us -> 372 us (0.951)
  waiting for transfers between devices: 111 us -> 81.1 us
  starting transfers between devices: 49.6 us -> 58.8 us
    psum x1 -> x0, waiting for transfers between devices: 49.1 us -> none  [local(): diag_half = lax.psum(diag_part, 'col')]
    ppermute x0 -> x2, waiting for transfers between devices: none -> 19.2 us  [local(): diag_half = diag_half + lax.ppermute(diag_half, ('row', 'col'), col_pairs)]
    ppermute x9, starting transfers between devices: 34.2 us -> 39.8 us  [gather_share(): recv.append(lax.ppermute(piece, ('row', 'col'), pairs))]
    ppermute x0 -> x2, starting transfers between devices: none -> 4.13 us  [local(): diag_half = diag_half + lax.ppermute(diag_half, ('row', 'col'), col_pairs)]
    unnamed x58 -> x56, local copies, waits for them, and re-layouts: 16.5 us -> 15.2 us
  transfers between devices with their start and end apart: 19 -> 20, of which waited for: 10 -> 11; matrix products, arithmetic and copies ran while one was open for 41% -> 43% of each run, Pallas kernels for 0% -> 0%
where the time goes in v5:
time: 372 us; the launch traced here: 365 us
  other arithmetic  134 us (36%)
  waiting for transfers between devices  81.1 us (22%)
  starting transfers between devices  58.8 us (16%)
  local copies, waits for them, and re-layouts  41.9 us (11%)
  matrix products  30.6 us (8%)
  between operations  18.1 us (5%)
    another operation x14, other arithmetic, local(): factor = jnp.linalg.cholesky(diag_block + jnp.diag(damping))  78.8 us
    another operation x4, other arithmetic, local(): lax.linalg.triangular_solve(factor, jnp.eye(PANEL, dtype=jnp.float32), le...  40.9 us
    ppermute x9, starting transfers between devices, gather_share(): recv.append(lax.ppermute(piece, ('row', 'col'), pairs))  39.8 us
    ppermute x7, waiting for transfers between devices, spread_share(): moved_list.append((lax.ppermute(piece, ('row', 'col'), pairs), gets))  34.4 us
    ppermute x9, waiting for transfers between devices, gather_share(): recv.append(lax.ppermute(piece, ('row', 'col'), pairs))  27.4 us
    ppermute x2, waiting for transfers between devices, local(): diag_half = diag_half + lax.ppermute(diag_half, ('row', 'col'), col_pairs)  19.2 us
    unnamed x56, local copies, waits for them, and re-layouts  15.2 us
    ppermute x7, starting transfers between devices, spread_share(): moved_list.append((lax.ppermute(piece, ('row', 'col'), pairs), gets))  12.5 us
  transfers between devices with their start and end apart: 20, of which 11 were waited for; matrix products, arithmetic and copies ran while one was open for 43% of the time, Pallas kernels for 0%

profile of v5, /device:TPU:1, one launch (start us, length us, event | category | flops | bytes accessed | tf_op | source)
XLA Modules:
  0.0 364.7 jit_solution(3165296320921264958)
XLA Ops:
  7.2 3.0 copy.63
  10.5 7.6 %gather_fusion = s32[2048,5]{1,0:T(8,128)} fusion(s32[1200,5]{1,0:T(8,128)S(1)} %bitcast.123, s32[2048]{0:T(1024)S(1)} %fusion.56), kind=kCustom, calls=%fused_computation | custom fusion | bytes 90112 | tf_op jit(solution)/shard_map/gather | solution.py:78
  18.2 1.5 copy.62
  20.0 1.5 copy-done
  21.5 5.7 %collective-permute-start = (bf16[2048,128]{0,1:T(8,128)(2,1)S(1)}, bf16[2048,128]{0,1:T(8,128)(2,1)S(1)}, u32[]{:S(2)}, u32[]{:S(2)}) collective-permute-start(bf16[2048,128]{0,1:T(8,128)(2,1)S(1)} %slice_bitcast_fusion), channel_id=1, source_target_pairs={{0,32},{1,33},{2,34},{3,35},{4,132},{5,133},{6,134},{7,135},{8,40}... | collective-permute-start | bytes 1572872 | tf_op jit(solution)/shard_map/ppermute | solution.py:41
  27.8 5.5 %collective-permute-done = bf16[2048,128]{0,1:T(8,128)(2,1)S(1)} collective-permute-done((bf16[2048,128]{0,1:T(8,128)(2,1)S(1)}, bf16[2048,128]{0,1:T(8,128)(2,1)S(1)}, u32[]{:S(2)}, u32[]{:S(2)}) %collective-permute-start) | collective-permute-done | bytes 524320 | tf_op jit(solution)/shard_map/ppermute | solution.py:41
  33.3 1.8 broadcast_select_fusion.1
  35.1 1.3 collective-permute-start.1
  37.0 7.1 %collective-permute-done.1 = bf16[2048,128]{0,1:T(8,128)(2,1)S(1)} collective-permute-done((bf16[2048,128]{0,1:T(8,128)(2,1)S(1)}, bf16[2048,128]{0,1:T(8,128)(2,1)S(1)}, u32[]{:S(2)}, u32[]{:S(2)}) %collective-permute-start.1) | collective-permute-done | bytes 524320 | tf_op jit(solution)/shard_map/ppermute | solution.py:41
  44.7 1.3 collective-permute-start.2
  46.7 8.6 %collective-permute-done.2 = bf16[2048,128]{0,1:T(8,128)(2,1)S(1)} collective-permute-done((bf16[2048,128]{0,1:T(8,128)(2,1)S(1)}, bf16[2048,128]{0,1:T(8,128)(2,1)S(1)}, u32[]{:S(2)}, u32[]{:S(2)}) %collective-permute-start.2) | collective-permute-done | bytes 524320 | tf_op jit(solution)/shard_map/ppermute | solution.py:41
  56.0 1.3 collective-permute-start.3
  57.9 9.2 %collective-permute-done.3 = bf16[2048,128]{0,1:T(8,128)(2,1)S(1)} collective-permute-done((bf16[2048,128]{0,1:T(8,128)(2,1)S(1)}, bf16[2048,128]{0,1:T(8,128)(2,1)S(1)}, u32[]{:S(2)}, u32[]{:S(2)}) %collective-permute-start.3) | collective-permute-done | bytes 524320 | tf_op jit(solution)/shard_map/ppermute | solution.py:41
  67.8 10.2 %collective-permute-start.4 = (bf16[2048,128]{0,1:T(8,128)(2,1)S(1)}, bf16[2048,128]{0,1:T(8,128)(2,1)S(1)}, u32[]{:S(2)}, u32[]{:S(2)}) collective-permute-start(bf16[2048,128]{0,1:T(8,128)(2,1)S(1)} %broadcast_select_fusion.4), channel_id=1, source_target_pairs={{0,8},{1,9},{2,10},{3,11},{4,12},{5,13},{6,14},{7,15},{8,0},{9,1},... | collective-permute-start | bytes 1572872 | tf_op jit(solution)/shard_map/ppermute | solution.py:60
  78.0 6.6 %collective-permute-done.4 = bf16[2048,128]{0,1:T(8,128)(2,1)S(1)} collective-permute-done((bf16[2048,128]{0,1:T(8,128)(2,1)S(1)}, bf16[2048,128]{0,1:T(8,128)(2,1)S(1)}, u32[]{:S(2)}, u32[]{:S(2)}) %collective-permute-start.4) | collective-permute-done | bytes 524320 | tf_op jit(solution)/shard_map/ppermute | solution.py:60
  85.1 7.6 %collective-permute-start.5 = (bf16[2,2048,128]{1,2,0:T(8,128)(2,1)S(1)}, bf16[2,2048,128]{1,2,0:T(8,128)(2,1)S(1)}, u32[]{:S(2)}, u32[]{:S(2)}) collective-permute-start(bf16[2,2048,128]{1,2,0:T(8,128)(2,1)S(1)} %get-tuple-element.52), channel_id=1, source_target_pairs={{0,4},{1,5},{2,6},{3,7},{4,0},{5,1},{6,2},{7,3},{8,12},{9,13},{10,... | collective-permute-start | bytes 3145736 | tf_op jit(solution)/shard_map/ppermute | solution.py:60
  92.8 2.3 collective-permute-done.5
  96.8 1.3 collective-permute-start.6
  98.1 11.9 %collective-permute-done.6 = f32[256,512]{0,1:T(8,128)S(1)} collective-permute-done((f32[256,512]{0,1:T(8,128)S(1)}, f32[256,512]{0,1:T(8,128)S(1)}, u32[]{:S(2)}, u32[]{:S(2)}) %collective-permute-start.6) | collective-permute-done | bytes 524320 | tf_op jit(solution)/shard_map/ppermute | solution.py:110
  110.1 2.8 collective-permute-start.7
  115.6 1.1 fusion.21
  116.7 7.3 %collective-permute-done.7 = f32[256,512]{0,1:T(8,128)} collective-permute-done((f32[256,512]{0,1:T(8,128)S(1)}, f32[256,512]{0,1:T(8,128)}, u32[]{:S(2)}, u32[]{:S(2)}) %collective-permute-start.7) | collective-permute-done | bytes 524320 | tf_op jit(solution)/shard_map/ppermute | solution.py:110
  124.0 1.9 add.164
  125.9 2.3 collective-permute-start.8
  128.3 4.2 %fusion.63 = f32[640,512]{1,0:T(8,128)} fusion(bf16[2048,640]{0,1:T(8,128)(2,1)S(1)} %bitcast.124, bf16[2048,512]{0,1:T(8,128)(2,1)} %bitcast.126), kind=kOutput, calls=%fused_computation.146 | convolution fusion | flops 1342177280 | bytes 6029312 | tf_op jit(solution)/shard_map/dot_general | solution.py:99
  132.5 1.4 maximum_select_fusion
  134.6 11.7 %cholesky.103 = f32[128,128]{1,0:T(8,128)S(1)} custom-call(f32[128,128]{1,0:T(8,128)S(1)} %cholesky.263), custom_call_target="Cholesky" | custom-call | tf_op jit(solution)/shard_map/jit(cholesky)/cholesky | solution.py:133
  146.4 9.8 %custom-call.30 = f32[1,128,128]{1,2,0:T(8,128)S(1)} custom-call(f32[1,128,128]{2,1,0:T(8,128)S(1)} %get-tuple-element.61), custom_call_target="InvertDiagBlocksLowerTriangular" | custom-call | tf_op jit(solution)/shard_map/jit(cholesky)/cholesky | solution.py:133
  157.1 12.1 %cholesky.215 = f32[128,128]{1,0:T(8,128)S(1)} custom-call(f32[128,128]{1,0:T(8,128)S(1)} %cholesky.267), custom_call_target="Cholesky" | custom-call | tf_op jit(solution)/shard_map/jit(cholesky)/cholesky | solution.py:133
  169.3 9.8 %custom-call.31 = f32[1,128,128]{1,2,0:T(8,128)S(1)} custom-call(f32[1,128,128]{2,1,0:T(8,128)S(1)} %get-tuple-element.59), custom_call_target="InvertDiagBlocksLowerTriangular" | custom-call | tf_op jit(solution)/shard_map/jit(cholesky)/cholesky | solution.py:133
  179.6 1.5 convolution_subtract_fusion.4
  181.2 11.7 %cholesky.236 = f32[128,128]{1,0:T(8,128)S(1)} custom-call(f32[128,128]{1,0:T(8,128)S(1)} %cholesky.272), custom_call_target="Cholesky" | custom-call | tf_op jit(solution)/shard_map/jit(cholesky)/cholesky | solution.py:133
  193.0 9.8 %custom-call.32 = f32[1,128,128]{1,2,0:T(8,128)S(1)} custom-call(f32[1,128,128]{2,1,0:T(8,128)S(1)} %get-tuple-element.57), custom_call_target="InvertDiagBlocksLowerTriangular" | custom-call | tf_op jit(solution)/shard_map/jit(cholesky)/cholesky | solution.py:133
  203.2 1.0 slice.160
  205.0 1.3 convolution_subtract_fusion.5
  206.3 11.7 %cholesky.253 = f32[128,128]{1,0:T(8,128)S(1)} custom-call(f32[128,128]{1,0:T(8,128)S(1)} %convolution_subtract_fusion.5), custom_call_target="Cholesky" | custom-call | tf_op jit(solution)/shard_map/jit(cholesky)/cholesky | solution.py:133
  218.8 1.7 broadcast_select_fusion.5
  225.9 1.3 collective-permute-start.11
  227.4 4.2 %collective-permute-done.11 = f32[128,512]{1,0:T(8,128)S(1)} collective-permute-done((f32[128,512]{1,0:T(8,128)S(1)}, f32[128,512]{1,0:T(8,128)S(1)}, u32[]{:S(2)}, u32[]{:S(2)}) %collective-permute-start.11) | collective-permute-done | bytes 262176 | tf_op jit(solution)/shard_map/ppermute | solution.py:41
  232.1 7.4 %collective-permute-start.12 = (f32[128,512]{1,0:T(8,128)S(1)}, f32[128,512]{1,0:T(8,128)}, u32[]{:S(2)}, u32[]{:S(2)}) collective-permute-start(f32[128,512]{1,0:T(8,128)S(1)} %broadcast_select_fusion.7), channel_id=1, source_target_pairs={{0,16},{1,17},{2,18},{3,19},{4,20},{5,21},{6,22},{7,23},{8,24},{9,... | collective-permute-start | bytes 786440 | tf_op jit(solution)/shard_map/ppermute | solution.py:60
  239.5 5.8 %collective-permute-start.13 = (f32[128,512]{1,0:T(8,128)S(1)}, f32[128,512]{1,0:T(8,128)}, u32[]{:S(2)}, u32[]{:S(2)}) collective-permute-start(f32[128,512]{1,0:T(8,128)S(1)} %broadcast_select_fusion.7), channel_id=1, source_target_pairs={{0,32},{1,33},{2,34},{3,35},{4,36},{5,37},{6,38},{7,39},{8,40},{9,... | collective-permute-start | bytes 786440 | tf_op jit(solution)/shard_map/ppermute | solution.py:60
  245.3 1.6 collective-permute-start.15
  247.2 11.0 %while.1 = (s32[]{:T(128)}, f32[512,512]{0,1:T(8,128)S(1)}, s32[4,2]{0,1:T(2,128)S(1)}, f32[4,128,128]{2,1,0:T(8,128)}, s32[]{:T(128)}) while((s32[]{:T(128)}, f32[512,512]{0,1:T(8,128)S(1)}, s32[4,2]{0,1:T(2,128)S(1)}, f32[4,128,128]{2,1,0:T(8,128)}, s32[]{:T(128)}) %tuple.42), condition=%wide.while_cond, body=%wide.while_body.sunk | while | flops 2 | bytes 393829 | solution.py:136
  247.9 1.4 dynamic-slice.7
  250.7 1.4 dynamic-slice.7
  253.4 1.4 dynamic-slice.7
  256.2 1.4 dynamic-slice.7
  258.2 40.8 %custom-call.33 = f32[4,128,128]{1,2,0:T(8,128)} custom-call(f32[4,128,128]{2,1,0:T(8,128)} %get-tuple-element.21), custom_call_target="InvertDiagBlocksLowerTriangular" | custom-call | tf_op jit(solution)/shard_map/triangular_solve | solution.py:136
  299.0 1.2 fusion.38
  300.8 1.3 fusion.50
  302.1 1.0 convolution_subtract_fusion
  303.6 1.5 convolution_subtract_fusion.2
  305.6 6.6 %collective-permute-start.17 = (f32[128,512]{1,0:T(8,128)S(1)}, f32[128,512]{1,0:T(8,128)S(1)}, u32[]{:S(2)}, u32[]{:S(2)}) collective-permute-start(f32[128,512]{1,0:T(8,128)S(1)} %broadcast_select_fusion.7), channel_id=1, source_target_pairs={{0,96},{1,97},{2,98},{3,99},{4,100},{5,101},{6,102},{7,103},{8,104... | collective-permute-start | bytes 786440 | tf_op jit(solution)/shard_map/ppermute | solution.py:60
  313.6 1.0 bitcast_dynamic-update-slice_fusion.6
  314.5 1.0 bitcast_dynamic-update-slice_fusion.5
  315.5 1.0 bitcast_dynamic-update-slice_fusion.4
  316.5 1.0 bitcast_dynamic-update-slice_fusion.3
  317.5 1.7 collective-permute-done.17
  319.2 16.8 %collective-permute-done.18 = f32[128,512]{1,0:T(8,128)S(1)} collective-permute-done((f32[128,512]{1,0:T(8,128)S(1)}, f32[128,512]{1,0:T(8,128)S(1)}, u32[]{:S(2)}, u32[]{:S(2)}) %collective-permute-start.18) | collective-permute-done | bytes 262176 | tf_op jit(solution)/shard_map/ppermute | solution.py:60
  336.5 3.5 fusion
  340.0 2.7 fusion.64
  343.1 1.4 copy-done.4
  344.5 9.0 %copy_subtract_fusion = f32[5,128,8,128]{3,1,2,0:T(8,128)S(1)} fusion(f32[5,128,8,128]{3,2,1,0:T(8,128)S(1)} %copy-done.4, f32[8,128,512]{2,1,0:T(8,128)S(1)} %fusion, f32[5,128,512]{1,2,0:T(8,128)S(1)} %fusion.28, pred[5]{0:T(512)(128)(4,1)S(1)} %add_compare_fusion), kind=kOutput, calls=%fused_computation.3 | convolution fusion | flops 4027842560 | bytes 8650757 | tf_op jit(solution)/shard_map/dot_general | solution.py:162
  353.5 3.0 copy.87
  (150 shorter events, 28.1 us)
Async XLA Ops:
  7.2 3.1 copy-start.8
  7.2 3.3 copy-start.9
  7.2 196.0 %all-reduce.3.cloned.1.call-start = ((), (), s32[]{:S(2)}) async-start(), calls=%async_computation | async-start | bytes 2621440 | tf_op jit(solution)/shard_map/psum | solution.py:124
  10.5 9.2 %copy-start.10 = (s32[2048]{0:T(1024)S(1)}, s32[2048]{0:T(1024)}, u32[]{:S(2)}) copy-start(s32[2048]{0:T(1024)} %param.16) | copy-start | bytes 24580
  19.8 7.5 %copy-start.18 = (pred[256]{0:T(512)(128)(4,1)S(1)}, pred[256]{0:T(512)(128)(4,1)}, u32[]{:S(2)}) copy-start(pred[256]{0:T(512)(128)(4,1)} %constant.244.clone) | copy-start | bytes 772
  20.0 1.5 copy-start
  21.5 14.9 %copy-start.17 = (pred[256]{0:T(512)(128)(4,1)S(1)}, pred[256]{0:T(512)(128)(4,1)}, u32[]{:S(2)}) copy-start(pred[256]{0:T(512)(128)(4,1)} %constant.245.clone) | copy-start | bytes 772
  21.5 24.6 %copy-start.16 = (pred[256]{0:T(512)(128)(4,1)S(1)}, pred[256]{0:T(512)(128)(4,1)}, u32[]{:S(2)}) copy-start(pred[256]{0:T(512)(128)(4,1)} %constant.246.clone) | copy-start | bytes 772
  21.5 11.8 %collective-permute-start = (bf16[2048,128]{0,1:T(8,128)(2,1)S(1)}, bf16[2048,128]{0,1:T(8,128)(2,1)S(1)}, u32[]{:S(2)}, u32[]{:S(2)}) collective-permute-start(bf16[2048,128]{0,1:T(8,128)(2,1)S(1)} %slice_bitcast_fusion), channel_id=1, source_target_pairs={{0,32},{1,33},{2,34},{3,35},{4,132},{5,133},{6,134},{7,135},{8,40}... | collective-permute-start | bytes 1572872 | tf_op jit(solution)/shard_map/ppermute | solution.py:41
  33.3 24.0 %copy-start.15 = (pred[256]{0:T(512)(128)(4,1)S(1)}, pred[256]{0:T(512)(128)(4,1)}, u32[]{:S(2)}) copy-start(pred[256]{0:T(512)(128)(4,1)} %constant.247.clone) | copy-start | bytes 772
  35.1 9.0 %collective-permute-start.1 = (bf16[2048,128]{0,1:T(8,128)(2,1)S(1)}, bf16[2048,128]{0,1:T(8,128)(2,1)S(1)}, u32[]{:S(2)}, u32[]{:S(2)}) collective-permute-start(bf16[2048,128]{0,1:T(8,128)(2,1)S(1)} %broadcast_select_fusion.1), channel_id=1, source_target_pairs={{0,128},{1,129},{2,130},{3,131},{4,36},{5,37},{6,38},{7,39},{8,136... | collective-permute-start | bytes 1572872 | tf_op jit(solution)/shard_map/ppermute | solution.py:41
  44.7 10.5 %collective-permute-start.2 = (bf16[2048,128]{0,1:T(8,128)(2,1)S(1)}, bf16[2048,128]{0,1:T(8,128)(2,1)S(1)}, u32[]{:S(2)}, u32[]{:S(2)}) collective-permute-start(bf16[2048,128]{0,1:T(8,128)(2,1)S(1)} %broadcast_select_fusion.2), channel_id=1, source_target_pairs={{0,16},{1,17},{2,18},{3,19},{4,68},{5,69},{6,70},{7,71},{8,24},{9,... | collective-permute-start | bytes 1572872 | tf_op jit(solution)/shard_map/ppermute | solution.py:41
  56.0 11.1 %collective-permute-start.3 = (bf16[2048,128]{0,1:T(8,128)(2,1)S(1)}, bf16[2048,128]{0,1:T(8,128)(2,1)S(1)}, u32[]{:S(2)}, u32[]{:S(2)}) collective-permute-start(bf16[2048,128]{0,1:T(8,128)(2,1)S(1)} %broadcast_select_fusion.3), channel_id=1, source_target_pairs={{0,64},{1,65},{2,66},{3,67},{4,20},{5,21},{6,22},{7,23},{8,72},{9,... | collective-permute-start | bytes 1572872 | tf_op jit(solution)/shard_map/ppermute | solution.py:41
  67.8 16.8 %collective-permute-start.4 = (bf16[2048,128]{0,1:T(8,128)(2,1)S(1)}, bf16[2048,128]{0,1:T(8,128)(2,1)S(1)}, u32[]{:S(2)}, u32[]{:S(2)}) collective-permute-start(bf16[2048,128]{0,1:T(8,128)(2,1)S(1)} %broadcast_select_fusion.4), channel_id=1, source_target_pairs={{0,8},{1,9},{2,10},{3,11},{4,12},{5,13},{6,14},{7,15},{8,0},{9,1},... | collective-permute-start | bytes 1572872 | tf_op jit(solution)/shard_map/ppermute | solution.py:60
  85.1 9.9 %collective-permute-start.5 = (bf16[2,2048,128]{1,2,0:T(8,128)(2,1)S(1)}, bf16[2,2048,128]{1,2,0:T(8,128)(2,1)S(1)}, u32[]{:S(2)}, u32[]{:S(2)}) collective-permute-start(bf16[2,2048,128]{1,2,0:T(8,128)(2,1)S(1)} %get-tuple-element.52), channel_id=1, source_target_pairs={{0,4},{1,5},{2,6},{3,7},{4,0},{5,1},{6,2},{7,3},{8,12},{9,13},{10,... | collective-permute-start | bytes 3145736 | tf_op jit(solution)/shard_map/ppermute | solution.py:60
  96.0 14.1 %copy-start.6 = (bf16[2,2,2048,128]{2,3,0,1:T(8,128)(2,1)}, bf16[2,2,2048,128]{2,3,0,1:T(8,128)(2,1)S(1)}, u32[]{:S(2)}) copy-start(bf16[2,2,2048,128]{2,3,0,1:T(8,128)(2,1)S(1)} %pad_maximum_fusion) | copy-start | bytes 6291460
  96.0 17.0 %copy-start.14 = (pred[256]{0:T(512)(128)(4,1)S(1)}, pred[256]{0:T(512)(128)(4,1)}, u32[]{:S(2)}) copy-start(pred[256]{0:T(512)(128)(4,1)} %constant.248.clone) | copy-start | bytes 772
  96.0 17.6 %copy-start.13 = (pred[256]{0:T(512)(128)(4,1)S(1)}, pred[256]{0:T(512)(128)(4,1)}, u32[]{:S(2)}) copy-start(pred[256]{0:T(512)(128)(4,1)} %constant.249.clone) | copy-start | bytes 772
  96.0 18.2 %copy-start.12 = (pred[256]{0:T(512)(128)(4,1)S(1)}, pred[256]{0:T(512)(128)(4,1)}, u32[]{:S(2)}) copy-start(pred[256]{0:T(512)(128)(4,1)} %constant.250.clone) | copy-start | bytes 772
  96.8 31.5 %copy-start.1 = (bf16[2048,5,128]{0,2,1:T(8,128)(2,1)S(1)}, bf16[2048,5,128]{0,2,1:T(8,128)(2,1)}, u32[]{:S(2)}) copy-start(bf16[2048,5,128]{0,2,1:T(8,128)(2,1)} %copy-done) | copy-start | bytes 7864324
  96.8 13.2 %collective-permute-start.6 = (f32[256,512]{0,1:T(8,128)S(1)}, f32[256,512]{0,1:T(8,128)S(1)}, u32[]{:S(2)}, u32[]{:S(2)}) collective-permute-start(f32[256,512]{0,1:T(8,128)S(1)} %fusion.13), channel_id=1, source_target_pairs={{0,1},{1,0},{2,3},{3,2},{4,5},{5,4},{6,7},{7,6},{8,9},{9,8},{10,11... | collective-permute-start | bytes 1572872 | tf_op jit(solution)/shard_map/ppermute | solution.py:110
  110.1 13.9 %collective-permute-start.7 = (f32[256,512]{0,1:T(8,128)S(1)}, f32[256,512]{0,1:T(8,128)}, u32[]{:S(2)}, u32[]{:S(2)}) collective-permute-start(f32[256,512]{0,1:T(8,128)S(1)} %add.163), channel_id=1, source_target_pairs={{0,2},{1,3},{2,0},{3,1},{4,6},{5,7},{6,4},{7,5},{8,10},{9,11},{10,... | collective-permute-start | bytes 1572872 | tf_op jit(solution)/shard_map/ppermute | solution.py:110
  125.9 6.5 %collective-permute-start.8 = (f32[256,512]{0,1:T(8,128)}, f32[256,512]{0,1:T(8,128)S(1)}, u32[]{:S(2)}, u32[]{:S(2)}) collective-permute-start(f32[256,512]{0,1:T(8,128)} %add.164), channel_id=1, source_target_pairs={{0,4},{1,5},{2,6},{3,7},{4,0},{5,1},{6,2},{7,3},{8,12},{9,13},{10,... | collective-permute-start | bytes 1572872 | tf_op jit(solution)/shard_map/ppermute | solution.py:117
  132.5 1.4 copy-start.11
  134.6 34.7 %copy-start.3 = (f32[512,512]{1,0:T(8,128)}, f32[512,512]{1,0:T(8,128)S(1)}, u32[]{:S(2)}) copy-start(f32[512,512]{1,0:T(8,128)S(1)} %fusion.12) | copy-start | bytes 3145732
  204.2 14.6 %collective-permute-start.9 = (f32[128,512]{1,0:T(8,128)S(1)}, f32[128,512]{1,0:T(8,128)S(1)}, u32[]{:S(2)}, u32[]{:S(2)}) collective-permute-start(f32[128,512]{1,0:T(8,128)S(1)} %slice.160), channel_id=1, source_target_pairs={{16,144},{21,149},{26,154},{31,159},{32,160},{37,165},{42,170},{47... | collective-permute-start | bytes 786440 | tf_op jit(solution)/shard_map/ppermute | solution.py:41
  220.4 4.8 %collective-permute-start.10 = (f32[128,512]{1,0:T(8,128)S(1)}, f32[128,512]{1,0:T(8,128)S(1)}, u32[]{:S(2)}, u32[]{:S(2)}) collective-permute-start(f32[128,512]{1,0:T(8,128)S(1)} %broadcast_select_fusion.5), channel_id=1, source_target_pairs={{0,8},{5,13},{10,2},{15,7},{16,24},{21,29},{26,18},{31,23},{32,40}... | collective-permute-start | bytes 786440 | tf_op jit(solution)/shard_map/ppermute | solution.py:41
  225.9 5.6 %collective-permute-start.11 = (f32[128,512]{1,0:T(8,128)S(1)}, f32[128,512]{1,0:T(8,128)S(1)}, u32[]{:S(2)}, u32[]{:S(2)}) collective-permute-start(f32[128,512]{1,0:T(8,128)S(1)} %broadcast_select_fusion.6), channel_id=1, source_target_pairs={{0,4},{2,6},{5,1},{7,3},{8,12},{10,14},{13,9},{15,11},{16,20},{18,... | collective-permute-start | bytes 786440 | tf_op jit(solution)/shard_map/ppermute | solution.py:41
  232.1 68.1 %copy-start.2 = (f32[512,512]{0,1:T(8,128)S(1)}, f32[512,512]{0,1:T(8,128)}, u32[]{:S(2)}) copy-start(f32[512,512]{0,1:T(8,128)} %fusion.21) | copy-start | bytes 3145732
  232.1 73.5 %collective-permute-start.12 = (f32[128,512]{1,0:T(8,128)S(1)}, f32[128,512]{1,0:T(8,128)}, u32[]{:S(2)}, u32[]{:S(2)}) collective-permute-start(f32[128,512]{1,0:T(8,128)S(1)} %broadcast_select_fusion.7), channel_id=1, source_target_pairs={{0,16},{1,17},{2,18},{3,19},{4,20},{5,21},{6,22},{7,23},{8,24},{9,... | collective-permute-start | bytes 786440 | tf_op jit(solution)/shard_map/ppermute | solution.py:60
  239.5 73.7 %collective-permute-start.13 = (f32[128,512]{1,0:T(8,128)S(1)}, f32[128,512]{1,0:T(8,128)}, u32[]{:S(2)}, u32[]{:S(2)}) collective-permute-start(f32[128,512]{1,0:T(8,128)S(1)} %broadcast_select_fusion.7), channel_id=1, source_target_pairs={{0,32},{1,33},{2,34},{3,35},{4,36},{5,37},{6,38},{7,39},{8,40},{9,... | collective-permute-start | bytes 786440 | tf_op jit(solution)/shard_map/ppermute | solution.py:60
  245.3 69.2 %collective-permute-start.14 = (f32[128,512]{1,0:T(8,128)S(1)}, f32[128,512]{1,0:T(8,128)}, u32[]{:S(2)}, u32[]{:S(2)}) collective-permute-start(f32[128,512]{1,0:T(8,128)S(1)} %broadcast_select_fusion.7), channel_id=1, source_target_pairs={{0,48},{1,49},{2,50},{3,51},{4,52},{5,53},{6,54},{7,55},{8,56},{9,... | collective-permute-start | bytes 786440 | tf_op jit(solution)/shard_map/ppermute | solution.py:60
  245.3 70.2 %collective-permute-start.15 = (f32[128,512]{1,0:T(8,128)S(1)}, f32[128,512]{1,0:T(8,128)}, u32[]{:S(2)}, u32[]{:S(2)}) collective-permute-start(f32[128,512]{1,0:T(8,128)S(1)} %broadcast_select_fusion.7), channel_id=1, source_target_pairs={{0,64},{1,65},{2,66},{3,67},{4,68},{5,69},{6,70},{7,71},{8,72},{9,... | collective-permute-start | bytes 786440 | tf_op jit(solution)/shard_map/ppermute | solution.py:60
  246.9 69.6 %collective-permute-start.16 = (f32[128,512]{1,0:T(8,128)S(1)}, f32[128,512]{1,0:T(8,128)}, u32[]{:S(2)}, u32[]{:S(2)}) collective-permute-start(f32[128,512]{1,0:T(8,128)S(1)} %broadcast_select_fusion.7), channel_id=1, source_target_pairs={{0,80},{1,81},{2,82},{3,83},{4,84},{5,85},{6,86},{7,87},{8,88},{9,... | collective-permute-start | bytes 786440 | tf_op jit(solution)/shard_map/ppermute | solution.py:60
  299.0 4.1 %copy-start.7 = (f32[4,128,128]{1,2,0:T(8,128)S(1)}, f32[4,128,128]{1,2,0:T(8,128)}, u32[]{:S(2)}) copy-start(f32[4,128,128]{1,2,0:T(8,128)} %custom-call.33) | copy-start | bytes 786436
  305.6 13.6 %collective-permute-start.17 = (f32[128,512]{1,0:T(8,128)S(1)}, f32[128,512]{1,0:T(8,128)S(1)}, u32[]{:S(2)}, u32[]{:S(2)}) collective-permute-start(f32[128,512]{1,0:T(8,128)S(1)} %broadcast_select_fusion.7), channel_id=1, source_target_pairs={{0,96},{1,97},{2,98},{3,99},{4,100},{5,101},{6,102},{7,103},{8,104... | collective-permute-start | bytes 786440 | tf_op jit(solution)/shard_map/ppermute | solution.py:60
  313.2 22.8 %collective-permute-start.18 = (f32[128,512]{1,0:T(8,128)S(1)}, f32[128,512]{1,0:T(8,128)S(1)}, u32[]{:S(2)}, u32[]{:S(2)}) collective-permute-start(f32[128,512]{1,0:T(8,128)S(1)} %broadcast_select_fusion.7), channel_id=1, source_target_pairs={{0,112},{1,113},{2,114},{3,115},{4,116},{5,117},{6,118},{7,119},{8... | collective-permute-start | bytes 786440 | tf_op jit(solution)/shard_map/ppermute | solution.py:60
  336.5 3.5 copy-start.5
  342.8 1.7 copy-start.4
Sparse Core Ops, SparseCore 0:
  134.0 58.2 all-reduce.2

commit v6 on v5

--- a/solution.py
+++ b/solution.py
@@ -67,6 +67,25 @@
     )
 
 
+def lower_inverse_from_blocks(factor, inv_diag, nb):
+    inv = jnp.stack(inv_diag)
+    size = nb
+    while inv.shape[0] > 1:
+        pair_count = inv.shape[0] // 2
+        first_inv = inv[0::2]
+        second_inv = inv[1::2]
+        below = jnp.stack([
+            factor[(2 * p + 1) * size:(2 * p + 2) * size, 2 * p * size:(2 * p + 1) * size]
+            for p in range(pair_count)
+        ])
+        low = -jnp.einsum("pij,pjk,pkl->pil", second_inv, below, first_inv, precision=lax.Precision.HIGHEST)
+        top = jnp.concatenate([first_inv, jnp.zeros_like(first_inv)], axis=2)
+        bottom = jnp.concatenate([low, second_inv], axis=2)
+        inv = jnp.concatenate([top, bottom], axis=1)
+        size *= 2
+    return inv[0]
+
+
 def local(green, arrival, row_gauge, row_time, damping, trail):
     row_count = lax.axis_size("row")
     col_count = lax.axis_size("col")
@@ -130,15 +149,38 @@
     far_piece = spread_share(
         normal_rows[:tile_width], far_holds, ((32,), (2,), (1,)), row_count, col_count
     )
-    factor = jnp.linalg.cholesky(diag_block + jnp.diag(damping))
-    factor, far_piece = lax.optimization_barrier((factor, far_piece))
+    by_inverse = (((1,), (1,)), ((), ()))
+    unit = jnp.eye(tile_width, dtype=jnp.float32)
+    trailing = diag_block + jnp.diag(damping)
+    factor_cols = []
+    inv_diag = []
+    for step in range(panel_tiles):
+        head = trailing[:tile_width, :tile_width]
+        head_factor = jnp.tril(jnp.linalg.cholesky(head))
+        head_inv = lax.linalg.triangular_solve(head_factor, unit, left_side=True, lower=True)
+        inv_diag.append(head_inv)
+        if step + 1 < panel_tiles:
+            panel = lax.dot_general(
+                trailing[tile_width:, :tile_width], head_inv, by_inverse,
+                precision=lax.Precision.HIGHEST, preferred_element_type=jnp.float32,
+            )
+            trailing = trailing[tile_width:, tile_width:] - lax.dot_general(
+                panel, panel, by_inverse,
+                precision=lax.Precision.HIGHEST, preferred_element_type=jnp.float32,
+            )
+            factor_cols.append(jnp.concatenate([head_factor, panel]))
+        else:
+            factor_cols.append(head_factor)
+        if step == 1:
+            trailing, far_piece = lax.optimization_barrier((trailing, far_piece))
+    factor = jnp.concatenate(
+        [jnp.pad(col, ((step * tile_width, 0), (0, 0))) for step, col in enumerate(factor_cols)],
+        axis=1,
+    )
     far_shared = gather_share(far_piece, (4, 8, 16), row_count, col_count)
-    factor_inv = lax.linalg.triangular_solve(
-        factor, jnp.eye(PANEL, dtype=jnp.float32), left_side=True, lower=True
-    )
+    factor_inv = lower_inverse_from_blocks(factor, inv_diag, tile_width)
     factor_inv, far_shared = lax.optimization_barrier((factor_inv, far_shared))
     far_normal = jnp.roll(far_shared, -1, axis=0).reshape(far_slots * tile_width, PANEL)
-    by_inverse = (((1,), (1,)), ((), ()))
     solved = lax.dot_general(
         normal_rows, factor_inv, by_inverse,
         precision=lax.Precision.HIGHEST, preferred_element_type=jnp.float32,

time: 372 us -> 341 us (0.917)
  other arithmetic: 134 us -> 105 us
  waiting for transfers between devices: 81.1 us -> 108 us
  local copies, waits for them, and re-layouts: 41.9 us -> 30.8 us
  matrix products: 30.6 us -> 21.9 us
  starting transfers between devices: 58.8 us -> 53 us
    another operation x18 -> x21, other arithmetic: 120 us -> 92.3 us  [the longest x12 49.9 us: local(): head_factor = jnp.tril(jnp.linalg.cholesky(head))]
    psum x1, waiting for transfers between devices: 0.02 us -> 20.8 us  [local(): normal_rows = lax.psum(partial_value, 'col')]
    another operation x34 -> x1, local copies, waits for them, and re-layouts: 11.6 us -> 0.64 us  [lower_inverse_from_blocks(): jnp.stack([factor[(2 * p + 1) * size:(2 * p + 2) * size, 2 * p * size:(2...]
    another operation x13 -> x4, matrix products: 10.5 us -> 1.14 us  [local(): lax.linalg.triangular_solve(head_factor, unit, left_side=True, lower=True)]
    ppermute x9, starting transfers between devices: 39.8 us -> 34.2 us  [gather_share(): recv.append(lax.ppermute(piece, ('row', 'col'), pairs))]
    dot_general x0 -> x10, matrix products: none -> 5.28 us  [the longest x4 2.84 us: lower_inverse_from_blocks(): jnp.einsum('pij,pjk,pkl->pil', second_inv, below, first_inv, precision=la...]
    ppermute x7, waiting for transfers between devices: 34.4 us -> 38.8 us  [spread_share(): moved_list.append((lax.ppermute(piece, ('row', 'col'), pairs), gets))]
    dot_general x1, matrix products: 8.99 us -> 4.75 us  [local(): lax.dot_general(lower_rows.reshape(tile_rows * tile_width, PANEL), far_ro...]
  transfers between devices with their start and end apart: 20 -> 20, of which waited for: 11 -> 12; matrix products, arithmetic and copies ran while one was open for 43% -> 34% of each run, Pallas kernels for 0% -> 0%
where the time goes in v6:
time: 341 us; the launch traced here: 334 us
  waiting for transfers between devices  108 us (32%)
  other arithmetic  105 us (31%)
  starting transfers between devices  53 us (16%)
  local copies, waits for them, and re-layouts  30.8 us (9%)
  matrix products  21.9 us (6%)
  between operations  15.3 us (4%)
    another operation x12, other arithmetic, local(): head_factor = jnp.tril(jnp.linalg.cholesky(head))  49.9 us
    another operation x8, other arithmetic, local(): lax.linalg.triangular_solve(head_factor, unit, left_side=True, lower=True)  42.4 us
    ppermute x7, waiting for transfers between devices, spread_share(): moved_list.append((lax.ppermute(piece, ('row', 'col'), pairs), gets))  38.8 us
    ppermute x9, starting transfers between devices, gather_share(): recv.append(lax.ppermute(piece, ('row', 'col'), pairs))  34.2 us
    ppermute x9, waiting for transfers between devices, gather_share(): recv.append(lax.ppermute(piece, ('row', 'col'), pairs))  27.6 us
    ppermute x2, waiting for transfers between devices, local(): diag_half = diag_half + lax.ppermute(diag_half, ('row', 'col'), col_pairs)  21.2 us
    psum x1, waiting for transfers between devices, local(): normal_rows = lax.psum(partial_value, 'col')  20.8 us
    unnamed x51, local copies, waits for them, and re-layouts  14.3 us
  transfers between devices with their start and end apart: 20, of which 12 were waited for; matrix products, arithmetic and copies ran while one was open for 34% of the time, Pallas kernels for 0%

profile of v6, /device:TPU:1, one launch (start us, length us, event | category | flops | bytes accessed | tf_op | source)
XLA Modules:
  0.0 334.2 jit_solution(13915979991550497865)
XLA Ops:
  7.2 3.0 copy.51
  10.5 7.6 %gather_fusion = s32[2048,5]{1,0:T(8,128)} fusion(s32[1200,5]{1,0:T(8,128)S(1)} %bitcast.142, s32[2048]{0:T(1024)S(1)} %fusion.57), kind=kCustom, calls=%fused_computation | custom fusion | bytes 90112 | tf_op jit(solution)/shard_map/gather | solution.py:97
  18.2 1.5 copy.50
  20.0 1.5 copy-done
  21.5 5.7 %collective-permute-start = (bf16[2048,128]{0,1:T(8,128)(2,1)S(1)}, bf16[2048,128]{0,1:T(8,128)(2,1)S(1)}, u32[]{:S(2)}, u32[]{:S(2)}) collective-permute-start(bf16[2048,128]{0,1:T(8,128)(2,1)S(1)} %slice_bitcast_fusion), channel_id=1, source_target_pairs={{0,32},{1,33},{2,34},{3,35},{4,132},{5,133},{6,134},{7,135},{8,40}... | collective-permute-start | bytes 1572872 | tf_op jit(solution)/shard_map/ppermute | solution.py:41
  27.8 5.5 %collective-permute-done = bf16[2048,128]{0,1:T(8,128)(2,1)S(1)} collective-permute-done((bf16[2048,128]{0,1:T(8,128)(2,1)S(1)}, bf16[2048,128]{0,1:T(8,128)(2,1)S(1)}, u32[]{:S(2)}, u32[]{:S(2)}) %collective-permute-start) | collective-permute-done | bytes 524320 | tf_op jit(solution)/shard_map/ppermute | solution.py:41
  33.3 1.8 broadcast_select_fusion.1
  35.1 1.3 collective-permute-start.1
  37.0 7.1 %collective-permute-done.1 = bf16[2048,128]{0,1:T(8,128)(2,1)S(1)} collective-permute-done((bf16[2048,128]{0,1:T(8,128)(2,1)S(1)}, bf16[2048,128]{0,1:T(8,128)(2,1)S(1)}, u32[]{:S(2)}, u32[]{:S(2)}) %collective-permute-start.1) | collective-permute-done | bytes 524320 | tf_op jit(solution)/shard_map/ppermute | solution.py:41
  44.0 0.7 broadcast_select_fusion.2
  44.7 1.3 collective-permute-start.2
  46.7 8.6 %collective-permute-done.2 = bf16[2048,128]{0,1:T(8,128)(2,1)S(1)} collective-permute-done((bf16[2048,128]{0,1:T(8,128)(2,1)S(1)}, bf16[2048,128]{0,1:T(8,128)(2,1)S(1)}, u32[]{:S(2)}, u32[]{:S(2)}) %collective-permute-start.2) | collective-permute-done | bytes 524320 | tf_op jit(solution)/shard_map/ppermute | solution.py:41
  55.3 0.7 broadcast_select_fusion.3
  56.0 1.3 collective-permute-start.3
  57.9 9.2 %collective-permute-done.3 = bf16[2048,128]{0,1:T(8,128)(2,1)S(1)} collective-permute-done((bf16[2048,128]{0,1:T(8,128)(2,1)S(1)}, bf16[2048,128]{0,1:T(8,128)(2,1)S(1)}, u32[]{:S(2)}, u32[]{:S(2)}) %collective-permute-start.3) | collective-permute-done | bytes 524320 | tf_op jit(solution)/shard_map/ppermute | solution.py:41
  67.1 0.7 broadcast_select_fusion.4
  67.8 10.2 %collective-permute-start.4 = (bf16[2048,128]{0,1:T(8,128)(2,1)S(1)}, bf16[2048,128]{0,1:T(8,128)(2,1)S(1)}, u32[]{:S(2)}, u32[]{:S(2)}) collective-permute-start(bf16[2048,128]{0,1:T(8,128)(2,1)S(1)} %broadcast_select_fusion.4), channel_id=1, source_target_pairs={{0,8},{1,9},{2,10},{3,11},{4,12},{5,13},{6,14},{7,15},{8,0},{9,1},... | collective-permute-start | bytes 1572872 | tf_op jit(solution)/shard_map/ppermute | solution.py:60
  78.0 6.6 %collective-permute-done.4 = bf16[2048,128]{0,1:T(8,128)(2,1)S(1)} collective-permute-done((bf16[2048,128]{0,1:T(8,128)(2,1)S(1)}, bf16[2048,128]{0,1:T(8,128)(2,1)S(1)}, u32[]{:S(2)}, u32[]{:S(2)}) %collective-permute-start.4) | collective-permute-done | bytes 524320 | tf_op jit(solution)/shard_map/ppermute | solution.py:60
  85.1 7.6 %collective-permute-start.5 = (bf16[2,2048,128]{1,2,0:T(8,128)(2,1)S(1)}, bf16[2,2048,128]{1,2,0:T(8,128)(2,1)S(1)}, u32[]{:S(2)}, u32[]{:S(2)}) collective-permute-start(bf16[2,2048,128]{1,2,0:T(8,128)(2,1)S(1)} %get-tuple-element.32), channel_id=1, source_target_pairs={{0,4},{1,5},{2,6},{3,7},{4,0},{5,1},{6,2},{7,3},{8,12},{9,13},{10,... | collective-permute-start | bytes 3145736 | tf_op jit(solution)/shard_map/ppermute | solution.py:60
  92.8 2.3 collective-permute-done.5
  95.1 0.7 fusion.11
  96.1 0.8 fusion.14
  96.8 1.3 collective-permute-start.6
  98.1 11.9 %collective-permute-done.6 = f32[256,512]{0,1:T(8,128)S(1)} collective-permute-done((f32[256,512]{0,1:T(8,128)S(1)}, f32[256,512]{0,1:T(8,128)S(1)}, u32[]{:S(2)}, u32[]{:S(2)}) %collective-permute-start.6) | collective-permute-done | bytes 524320 | tf_op jit(solution)/shard_map/ppermute | solution.py:129
  110.1 2.8 collective-permute-start.7
  114.8 9.2 %collective-permute-done.7 = f32[256,512]{0,1:T(8,128)} collective-permute-done((f32[256,512]{0,1:T(8,128)S(1)}, f32[256,512]{0,1:T(8,128)}, u32[]{:S(2)}, u32[]{:S(2)}) %collective-permute-start.7) | collective-permute-done | bytes 524320 | tf_op jit(solution)/shard_map/ppermute | solution.py:129
  124.0 1.9 add.142
  125.9 2.3 collective-permute-start.8
  128.3 4.2 %fusion.69 = f32[640,512]{1,0:T(8,128)} fusion(bf16[2048,640]{0,1:T(8,128)(2,1)S(1)} %bitcast.143, bf16[2048,512]{0,1:T(8,128)(2,1)} %bitcast.145), kind=kOutput, calls=%fused_computation.158 | convolution fusion | flops 1342177280 | bytes 6029312 | tf_op jit(solution)/shard_map/dot_general | solution.py:118
  132.5 1.4 maximum_select_fusion
  134.2 11.7 %cholesky.74 = f32[128,128]{1,0:T(8,128)S(1)} custom-call(f32[128,128]{1,0:T(8,128)S(1)} %fusion.54), custom_call_target="Cholesky" | custom-call | tf_op jit(solution)/shard_map/jit(cholesky)/cholesky | solution.py:159
  147.2 9.8 %custom-call.8 = f32[1,128,128]{1,2,0:T(8,128)S(1)} custom-call(f32[1,128,128]{2,1,0:T(8,128)S(1)} %get-tuple-element.28), custom_call_target="InvertDiagBlocksLowerTriangular" | custom-call | tf_op jit(solution)/shard_map/triangular_solve/custom-call.0 | solution.py:160
  158.6 12.1 %cholesky.85 = f32[128,128]{1,0:T(8,128)S(1)} custom-call(f32[128,128]{1,0:T(8,128)S(1)} %fusion.52), custom_call_target="Cholesky" | custom-call | tf_op jit(solution)/shard_map/jit(cholesky)/cholesky | solution.py:159
  171.3 20.8 %all-reduce.7.cloned.1.call-done = f32[640,512]{1,0:T(8,128)} async-done(((f32[640,512]{1,0:T(8,128)}), f32[640,512]{1,0:T(8,128)}) %all-reduce.7.cloned.1.call-update) | async-done | bytes 1310736 | tf_op jit(solution)/shard_map/psum | solution.py:143
  192.2 1.0 slice.124
  193.1 0.7 collective-permute-start.9
  194.5 9.8 %custom-call.9 = f32[1,128,128]{1,2,0:T(8,128)S(1)} custom-call(f32[1,128,128]{2,1,0:T(8,128)S(1)} %get-tuple-element.26), custom_call_target="InvertDiagBlocksLowerTriangular" | custom-call | tf_op jit(solution)/shard_map/triangular_solve/custom-call.0 | solution.py:160
  205.0 1.6 broadcast_select_fusion.5
  208.6 1.3 collective-permute-start.11
  210.3 8.5 %collective-permute-done.11 = f32[128,512]{1,0:T(8,128)S(1)} collective-permute-done((f32[128,512]{1,0:T(8,128)S(1)}, f32[128,512]{1,0:T(8,128)S(1)}, u32[]{:S(2)}, u32[]{:S(2)}) %collective-permute-start.11) | collective-permute-done | bytes 262176 | tf_op jit(solution)/shard_map/ppermute | solution.py:41
  219.5 4.4 %collective-permute-start.12 = (f32[128,512]{1,0:T(8,128)S(1)}, f32[128,512]{1,0:T(8,128)}, u32[]{:S(2)}, u32[]{:S(2)}) collective-permute-start(f32[128,512]{1,0:T(8,128)S(1)} %broadcast_select_fusion.7), channel_id=1, source_target_pairs={{0,16},{1,17},{2,18},{3,19},{4,20},{5,21},{6,22},{7,23},{8,24},{9,... | collective-permute-start | bytes 786440 | tf_op jit(solution)/shard_map/ppermute | solution.py:60
  223.9 3.7 %collective-permute-start.13 = (f32[128,512]{1,0:T(8,128)S(1)}, f32[128,512]{1,0:T(8,128)}, u32[]{:S(2)}, u32[]{:S(2)}) collective-permute-start(f32[128,512]{1,0:T(8,128)S(1)} %broadcast_select_fusion.7), channel_id=1, source_target_pairs={{0,32},{1,33},{2,34},{3,35},{4,36},{5,37},{6,38},{7,39},{8,40},{9,... | collective-permute-start | bytes 786440 | tf_op jit(solution)/shard_map/ppermute | solution.py:60
  227.9 3.0 collective-permute-start.16
  231.0 11.7 %cholesky.96 = f32[128,128]{1,0:T(8,128)S(1)} custom-call(f32[128,128]{1,0:T(8,128)S(1)} %fusion.50), custom_call_target="Cholesky" | custom-call | tf_op jit(solution)/shard_map/jit(cholesky)/cholesky | solution.py:159
  244.1 9.8 %custom-call.10 = f32[1,128,128]{1,2,0:T(8,128)S(1)} custom-call(f32[1,128,128]{2,1,0:T(8,128)S(1)} %get-tuple-element.24), custom_call_target="InvertDiagBlocksLowerTriangular" | custom-call | tf_op jit(solution)/shard_map/triangular_solve/custom-call.0 | solution.py:160
  254.9 11.7 %cholesky.107 = f32[128,128]{1,0:T(8,128)S(1)} custom-call(f32[128,128]{1,0:T(8,128)S(1)} %fusion.48), custom_call_target="Cholesky" | custom-call | tf_op jit(solution)/shard_map/jit(cholesky)/cholesky | solution.py:159
  267.2 1.2 select_bitcast_fusion
  268.4 9.8 %custom-call.11 = f32[1,128,128]{1,2,0:T(8,128)S(1)} custom-call(f32[1,128,128]{2,1,0:T(8,128)S(1)} %get-tuple-element.22), custom_call_target="InvertDiagBlocksLowerTriangular" | custom-call | tf_op jit(solution)/shard_map/triangular_solve/custom-call.0 | solution.py:160
  278.6 1.3 fusion.43
  281.8 3.8 %collective-permute-start.17 = (f32[128,512]{1,0:T(8,128)S(1)}, f32[128,512]{1,0:T(8,128)S(1)}, u32[]{:S(2)}, u32[]{:S(2)}) collective-permute-start(f32[128,512]{1,0:T(8,128)S(1)} %broadcast_select_fusion.7), channel_id=1, source_target_pairs={{0,96},{1,97},{2,98},{3,99},{4,100},{5,101},{6,102},{7,103},{8,104... | collective-permute-start | bytes 786440 | tf_op jit(solution)/shard_map/ppermute | solution.py:60
  285.6 1.0 bitcast_dynamic-update-slice_fusion.6
  286.6 1.1 collective-permute-start.18
  287.7 1.0 bitcast_dynamic-update-slice_fusion.5
  288.7 1.0 bitcast_dynamic-update-slice_fusion.4
  289.7 1.0 bitcast_dynamic-update-slice_fusion.3
  290.7 1.0 bitcast_dynamic-update-slice_fusion.2
  291.7 3.3 collective-permute-done.17
  294.9 15.5 %collective-permute-done.18 = f32[128,512]{1,0:T(8,128)S(1)} collective-permute-done((f32[128,512]{1,0:T(8,128)S(1)}, f32[128,512]{1,0:T(8,128)S(1)}, u32[]{:S(2)}, u32[]{:S(2)}) %collective-permute-start.18) | collective-permute-done | bytes 262176 | tf_op jit(solution)/shard_map/ppermute | solution.py:60
  310.9 3.5 %fusion = f32[8,128,512]{2,1,0:T(8,128)S(1)} fusion(f32[1,128,512]{2,1,0:T(8,128)S(1)} %slice.114, f32[7,128,512]{2,1,0:T(8,128)S(1)} %slice.113, f32[512,512]{1,0:T(8,128)S(1)} %fusion.12), kind=kOutput, calls=%fused_computation.8 | convolution fusion | flops 3221749760 | bytes 5242880 | tf_op jit(solution)/shard_map/dot_general | solution.py:188
  314.4 2.3 fusion.70
  317.0 1.5 copy-done.2
  318.4 4.7 %copy_subtract_fusion = f32[5,128,8,128]{3,1,2,0:T(8,128)S(1)} fusion(f32[5,128,8,128]{3,2,1,0:T(8,128)S(1)} %copy-done.2, f32[8,128,512]{2,1,0:T(8,128)S(1)} %fusion, f32[5,128,512]{2,1,0:T(8,128)S(1)} %fusion.19, pred[5]{0:T(512)(128)(4,1)S(1)} %add_compare_fusion), kind=kOutput, calls=%fused_computation.1 | convolution fusion | flops 4027842560 | bytes 8650757 | tf_op jit(solution)/shard_map/dot_general | solution.py:204
  323.2 3.0 copy.67
  326.2 0.8 constant_dynamic-slice_fusion
  (127 shorter events, 20.0 us)
Async XLA Ops:
  7.2 3.1 copy-start.6
  7.2 3.3 copy-start.7
  7.2 185.0 %all-reduce.7.cloned.1.call-start = ((), (), s32[]{:S(2)}) async-start(), calls=%async_computation | async-start | bytes 2621440 | tf_op jit(solution)/shard_map/psum | solution.py:143
  10.5 9.2 %copy-start.8 = (s32[2048]{0:T(1024)S(1)}, s32[2048]{0:T(1024)}, u32[]{:S(2)}) copy-start(s32[2048]{0:T(1024)} %param.19) | copy-start | bytes 24580
  19.8 7.5 %copy-start.16 = (pred[256]{0:T(512)(128)(4,1)S(1)}, pred[256]{0:T(512)(128)(4,1)}, u32[]{:S(2)}) copy-start(pred[256]{0:T(512)(128)(4,1)} %constant.142.clone) | copy-start | bytes 772
  20.0 1.5 copy-start
  21.5 14.9 %copy-start.15 = (pred[256]{0:T(512)(128)(4,1)S(1)}, pred[256]{0:T(512)(128)(4,1)}, u32[]{:S(2)}) copy-start(pred[256]{0:T(512)(128)(4,1)} %constant.143.clone) | copy-start | bytes 772
  21.5 24.6 %copy-start.14 = (pred[256]{0:T(512)(128)(4,1)S(1)}, pred[256]{0:T(512)(128)(4,1)}, u32[]{:S(2)}) copy-start(pred[256]{0:T(512)(128)(4,1)} %constant.144.clone) | copy-start | bytes 772
  21.5 11.8 %collective-permute-start = (bf16[2048,128]{0,1:T(8,128)(2,1)S(1)}, bf16[2048,128]{0,1:T(8,128)(2,1)S(1)}, u32[]{:S(2)}, u32[]{:S(2)}) collective-permute-start(bf16[2048,128]{0,1:T(8,128)(2,1)S(1)} %slice_bitcast_fusion), channel_id=1, source_target_pairs={{0,32},{1,33},{2,34},{3,35},{4,132},{5,133},{6,134},{7,135},{8,40}... | collective-permute-start | bytes 1572872 | tf_op jit(solution)/shard_map/ppermute | solution.py:41
  33.3 24.0 %copy-start.13 = (pred[256]{0:T(512)(128)(4,1)S(1)}, pred[256]{0:T(512)(128)(4,1)}, u32[]{:S(2)}) copy-start(pred[256]{0:T(512)(128)(4,1)} %constant.145.clone) | copy-start | bytes 772
  35.1 9.0 %collective-permute-start.1 = (bf16[2048,128]{0,1:T(8,128)(2,1)S(1)}, bf16[2048,128]{0,1:T(8,128)(2,1)S(1)}, u32[]{:S(2)}, u32[]{:S(2)}) collective-permute-start(bf16[2048,128]{0,1:T(8,128)(2,1)S(1)} %broadcast_select_fusion.1), channel_id=1, source_target_pairs={{0,128},{1,129},{2,130},{3,131},{4,36},{5,37},{6,38},{7,39},{8,136... | collective-permute-start | bytes 1572872 | tf_op jit(solution)/shard_map/ppermute | solution.py:41
  44.7 10.5 %collective-permute-start.2 = (bf16[2048,128]{0,1:T(8,128)(2,1)S(1)}, bf16[2048,128]{0,1:T(8,128)(2,1)S(1)}, u32[]{:S(2)}, u32[]{:S(2)}) collective-permute-start(bf16[2048,128]{0,1:T(8,128)(2,1)S(1)} %broadcast_select_fusion.2), channel_id=1, source_target_pairs={{0,16},{1,17},{2,18},{3,19},{4,68},{5,69},{6,70},{7,71},{8,24},{9,... | collective-permute-start | bytes 1572872 | tf_op jit(solution)/shard_map/ppermute | solution.py:41
  56.0 11.1 %collective-permute-start.3 = (bf16[2048,128]{0,1:T(8,128)(2,1)S(1)}, bf16[2048,128]{0,1:T(8,128)(2,1)S(1)}, u32[]{:S(2)}, u32[]{:S(2)}) collective-permute-start(bf16[2048,128]{0,1:T(8,128)(2,1)S(1)} %broadcast_select_fusion.3), channel_id=1, source_target_pairs={{0,64},{1,65},{2,66},{3,67},{4,20},{5,21},{6,22},{7,23},{8,72},{9,... | collective-permute-start | bytes 1572872 | tf_op jit(solution)/shard_map/ppermute | solution.py:41
  67.8 16.8 %collective-permute-start.4 = (bf16[2048,128]{0,1:T(8,128)(2,1)S(1)}, bf16[2048,128]{0,1:T(8,128)(2,1)S(1)}, u32[]{:S(2)}, u32[]{:S(2)}) collective-permute-start(bf16[2048,128]{0,1:T(8,128)(2,1)S(1)} %broadcast_select_fusion.4), channel_id=1, source_target_pairs={{0,8},{1,9},{2,10},{3,11},{4,12},{5,13},{6,14},{7,15},{8,0},{9,1},... | collective-permute-start | bytes 1572872 | tf_op jit(solution)/shard_map/ppermute | solution.py:60
  85.1 9.9 %collective-permute-start.5 = (bf16[2,2048,128]{1,2,0:T(8,128)(2,1)S(1)}, bf16[2,2048,128]{1,2,0:T(8,128)(2,1)S(1)}, u32[]{:S(2)}, u32[]{:S(2)}) collective-permute-start(bf16[2,2048,128]{1,2,0:T(8,128)(2,1)S(1)} %get-tuple-element.32), channel_id=1, source_target_pairs={{0,4},{1,5},{2,6},{3,7},{4,0},{5,1},{6,2},{7,3},{8,12},{9,13},{10,... | collective-permute-start | bytes 3145736 | tf_op jit(solution)/shard_map/ppermute | solution.py:60
  96.0 14.1 %copy-start.4 = (bf16[2,2,2048,128]{2,3,0,1:T(8,128)(2,1)}, bf16[2,2,2048,128]{2,3,0,1:T(8,128)(2,1)S(1)}, u32[]{:S(2)}) copy-start(bf16[2,2,2048,128]{2,3,0,1:T(8,128)(2,1)S(1)} %pad_maximum_fusion) | copy-start | bytes 6291460
  96.0 17.0 %copy-start.12 = (pred[256]{0:T(512)(128)(4,1)S(1)}, pred[256]{0:T(512)(128)(4,1)}, u32[]{:S(2)}) copy-start(pred[256]{0:T(512)(128)(4,1)} %constant.146.clone) | copy-start | bytes 772
  96.0 17.6 %copy-start.11 = (pred[256]{0:T(512)(128)(4,1)S(1)}, pred[256]{0:T(512)(128)(4,1)}, u32[]{:S(2)}) copy-start(pred[256]{0:T(512)(128)(4,1)} %constant.147.clone) | copy-start | bytes 772
  96.0 18.2 %copy-start.10 = (pred[256]{0:T(512)(128)(4,1)S(1)}, pred[256]{0:T(512)(128)(4,1)}, u32[]{:S(2)}) copy-start(pred[256]{0:T(512)(128)(4,1)} %constant.148.clone) | copy-start | bytes 772
  96.8 31.5 %copy-start.1 = (bf16[2048,5,128]{0,2,1:T(8,128)(2,1)S(1)}, bf16[2048,5,128]{0,2,1:T(8,128)(2,1)}, u32[]{:S(2)}) copy-start(bf16[2048,5,128]{0,2,1:T(8,128)(2,1)} %copy-done) | copy-start | bytes 7864324
  96.8 13.2 %collective-permute-start.6 = (f32[256,512]{0,1:T(8,128)S(1)}, f32[256,512]{0,1:T(8,128)S(1)}, u32[]{:S(2)}, u32[]{:S(2)}) collective-permute-start(f32[256,512]{0,1:T(8,128)S(1)} %fusion.14), channel_id=1, source_target_pairs={{0,1},{1,0},{2,3},{3,2},{4,5},{5,4},{6,7},{7,6},{8,9},{9,8},{10,11... | collective-permute-start | bytes 1572872 | tf_op jit(solution)/shard_map/ppermute | solution.py:129
  110.1 13.9 %collective-permute-start.7 = (f32[256,512]{0,1:T(8,128)S(1)}, f32[256,512]{0,1:T(8,128)}, u32[]{:S(2)}, u32[]{:S(2)}) collective-permute-start(f32[256,512]{0,1:T(8,128)S(1)} %add.141), channel_id=1, source_target_pairs={{0,2},{1,3},{2,0},{3,1},{4,6},{5,7},{6,4},{7,5},{8,10},{9,11},{10,... | collective-permute-start | bytes 1572872 | tf_op jit(solution)/shard_map/ppermute | solution.py:129
  125.9 6.5 %collective-permute-start.8 = (f32[256,512]{0,1:T(8,128)}, f32[256,512]{0,1:T(8,128)S(1)}, u32[]{:S(2)}, u32[]{:S(2)}) collective-permute-start(f32[256,512]{0,1:T(8,128)} %add.142), channel_id=1, source_target_pairs={{0,4},{1,5},{2,6},{3,7},{4,0},{5,1},{6,2},{7,3},{8,12},{9,13},{10,... | collective-permute-start | bytes 1572872 | tf_op jit(solution)/shard_map/ppermute | solution.py:136
  132.5 1.4 copy-start.9
  193.1 11.8 %collective-permute-start.9 = (f32[128,512]{1,0:T(8,128)S(1)}, f32[128,512]{1,0:T(8,128)S(1)}, u32[]{:S(2)}, u32[]{:S(2)}) collective-permute-start(f32[128,512]{1,0:T(8,128)S(1)} %slice.124), channel_id=1, source_target_pairs={{16,144},{21,149},{26,154},{31,159},{32,160},{37,165},{42,170},{47... | collective-permute-start | bytes 786440 | tf_op jit(solution)/shard_map/ppermute | solution.py:41
  206.6 1.4 collective-permute-start.10
  208.6 10.2 %collective-permute-start.11 = (f32[128,512]{1,0:T(8,128)S(1)}, f32[128,512]{1,0:T(8,128)S(1)}, u32[]{:S(2)}, u32[]{:S(2)}) collective-permute-start(f32[128,512]{1,0:T(8,128)S(1)} %broadcast_select_fusion.6), channel_id=1, source_target_pairs={{0,4},{2,6},{5,1},{7,3},{8,12},{10,14},{13,9},{15,11},{16,20},{18,... | collective-permute-start | bytes 786440 | tf_op jit(solution)/shard_map/ppermute | solution.py:41
  219.5 62.3 %collective-permute-start.12 = (f32[128,512]{1,0:T(8,128)S(1)}, f32[128,512]{1,0:T(8,128)}, u32[]{:S(2)}, u32[]{:S(2)}) collective-permute-start(f32[128,512]{1,0:T(8,128)S(1)} %broadcast_select_fusion.7), channel_id=1, source_target_pairs={{0,16},{1,17},{2,18},{3,19},{4,20},{5,21},{6,22},{7,23},{8,24},{9,... | collective-permute-start | bytes 786440 | tf_op jit(solution)/shard_map/ppermute | solution.py:60
  223.9 62.7 %collective-permute-start.13 = (f32[128,512]{1,0:T(8,128)S(1)}, f32[128,512]{1,0:T(8,128)}, u32[]{:S(2)}, u32[]{:S(2)}) collective-permute-start(f32[128,512]{1,0:T(8,128)S(1)} %broadcast_select_fusion.7), channel_id=1, source_target_pairs={{0,32},{1,33},{2,34},{3,35},{4,36},{5,37},{6,38},{7,39},{8,40},{9,... | collective-permute-start | bytes 786440 | tf_op jit(solution)/shard_map/ppermute | solution.py:60
  227.6 61.1 %collective-permute-start.14 = (f32[128,512]{1,0:T(8,128)S(1)}, f32[128,512]{1,0:T(8,128)}, u32[]{:S(2)}, u32[]{:S(2)}) collective-permute-start(f32[128,512]{1,0:T(8,128)S(1)} %broadcast_select_fusion.7), channel_id=1, source_target_pairs={{0,48},{1,49},{2,50},{3,51},{4,52},{5,53},{6,54},{7,55},{8,56},{9,... | collective-permute-start | bytes 786440 | tf_op jit(solution)/shard_map/ppermute | solution.py:60
  227.6 62.1 %collective-permute-start.15 = (f32[128,512]{1,0:T(8,128)S(1)}, f32[128,512]{1,0:T(8,128)}, u32[]{:S(2)}, u32[]{:S(2)}) collective-permute-start(f32[128,512]{1,0:T(8,128)S(1)} %broadcast_select_fusion.7), channel_id=1, source_target_pairs={{0,64},{1,65},{2,66},{3,67},{4,68},{5,69},{6,70},{7,71},{8,72},{9,... | collective-permute-start | bytes 786440 | tf_op jit(solution)/shard_map/ppermute | solution.py:60
  227.9 62.8 %collective-permute-start.16 = (f32[128,512]{1,0:T(8,128)S(1)}, f32[128,512]{1,0:T(8,128)}, u32[]{:S(2)}, u32[]{:S(2)}) collective-permute-start(f32[128,512]{1,0:T(8,128)S(1)} %broadcast_select_fusion.7), channel_id=1, source_target_pairs={{0,80},{1,81},{2,82},{3,83},{4,84},{5,85},{6,86},{7,87},{8,88},{9,... | collective-permute-start | bytes 786440 | tf_op jit(solution)/shard_map/ppermute | solution.py:60
  278.6 2.4 copy-start.5
  281.8 13.1 %collective-permute-start.17 = (f32[128,512]{1,0:T(8,128)S(1)}, f32[128,512]{1,0:T(8,128)S(1)}, u32[]{:S(2)}, u32[]{:S(2)}) collective-permute-start(f32[128,512]{1,0:T(8,128)S(1)} %broadcast_select_fusion.7), channel_id=1, source_target_pairs={{0,96},{1,97},{2,98},{3,99},{4,100},{5,101},{6,102},{7,103},{8,104... | collective-permute-start | bytes 786440 | tf_op jit(solution)/shard_map/ppermute | solution.py:60
  286.6 23.8 %collective-permute-start.18 = (f32[128,512]{1,0:T(8,128)S(1)}, f32[128,512]{1,0:T(8,128)S(1)}, u32[]{:S(2)}, u32[]{:S(2)}) collective-permute-start(f32[128,512]{1,0:T(8,128)S(1)} %broadcast_select_fusion.7), channel_id=1, source_target_pairs={{0,112},{1,113},{2,114},{3,115},{4,116},{5,117},{6,118},{7,119},{8... | collective-permute-start | bytes 786440 | tf_op jit(solution)/shard_map/ppermute | solution.py:60
  310.9 3.5 %copy-start.3 = (f32[640,512]{1,0:T(8,128)S(1)}, f32[640,512]{1,0:T(8,128)}, u32[]{:S(2)}) copy-start(f32[640,512]{1,0:T(8,128)} %all-reduce.7.cloned.1.call-done) | copy-start | bytes 3932164
  316.7 1.7 copy-start.2
Sparse Core Ops, SparseCore 0:
  134.0 58.1 all-reduce.6
